TPU v7x, 32 devices: a whole 2x2x4 slice. The times are simulated.
32 devices in a mesh: fsdp: 8 (over y, x, core), tensor: 4 (over z).
Axes of the slice: x: 2, y: 2, z: 4, core: 2. Of those that a mesh axis runs over, the one named last changes fastest.
Arguments:
- tokens: bfloat16 [16384, 768], P(('fsdp', 'tensor')), may hold values from -6 to 6
- segments: int32 [8, 2048], P('fsdp'), may hold values from 0 to 8, as said below
- query_weight: bfloat16 [768, 768], P('fsdp', 'tensor'), may hold values from -0.21875 to 0.21875
- query_bias: float32 [768], replicated, may hold values from -3 to 3
- key_weight: bfloat16 [768, 768], P('fsdp', 'tensor'), may hold values from -0.21875 to 0.21875
- value_weight: bfloat16 [768, 768], P('fsdp', 'tensor'), may hold values from -0.21875 to 0.21875
- value_bias: float32 [768], replicated, may hold values from -3 to 3
- mix_weight: bfloat16 [768, 768], P('tensor', 'fsdp'), may hold values from -1.75 to 1.75
- mix_bias: float32 [768], replicated, may hold values from -3 to 3
- norm_gain: float32 [768], replicated, may hold values from 0.25 to 1.75
- norm_shift: float32 [768], replicated, may hold values from -3 to 3
- up_weight: bfloat16 [768, 3072], P('fsdp', 'tensor'), may hold values from -0.21875 to 0.21875
- up_bias: float32 [3072], replicated, may hold values from -3 to 3
- down_weight: bfloat16 [3072, 768], P('tensor', 'fsdp'), may hold values from -0.109375 to 0.109375
- down_bias: float32 [768], replicated, may hold values from -3 to 3
- final_gain: float32 [768], replicated, may hold values from 0.25 to 1.75
- final_shift: float32 [768], replicated, may hold values from -3 to 3
- out_grad: bfloat16 [16384, 768], P(('fsdp', 'tensor')), may hold values from -6 to 6
Outputs:
- layer_out: bfloat16 [16384, 768], P(('fsdp', 'tensor'))
- tokens_grad: float32 [16384, 768], P(('fsdp', 'tensor'))
- query_weight_grad: float32 [768, 768], P('fsdp', 'tensor')
- query_bias_grad: float32 [768], replicated
- key_weight_grad: float32 [768, 768], P('fsdp', 'tensor')
- value_weight_grad: float32 [768, 768], P('fsdp', 'tensor')
- value_bias_grad: float32 [768], replicated
- mix_weight_grad: float32 [768, 768], P('tensor', 'fsdp')
- mix_bias_grad: float32 [768], replicated
- norm_gain_grad: float32 [768], replicated
- norm_shift_grad: float32 [768], replicated
- up_weight_grad: float32 [768, 3072], P('fsdp', 'tensor')
- up_bias_grad: float32 [3072], replicated
- down_weight_grad: float32 [3072, 768], P('tensor', 'fsdp')
- down_bias_grad: float32 [768], replicated
- final_gain_grad: float32 [768], replicated
- final_shift_grad: float32 [768], replicated
Inputs may be any that keep to these rules, and one draw needn't show every extreme that they name: `segments`: each row is one sequence: its live part begins at the first position and its ids never decrease along it, running from 1 to 8, with 8 reached in every row and some ids possibly skipped; after it come 1 to 256 padding positions with id 0.
All inputs are finite; a program needn't handle non-finite values.
Results may differ from a plain program's by a relative error of at most 0.013.
The roundings to bfloat16 on the way count: a program that leaves them out, or rounds other values in their place, can miss the bound.
Values may be sent and summed in bfloat16 or wider, within the bound.
No kernel may reach another device: no remote copies, remote signals or barrier semaphores. Data moves between devices by JAX's collectives and lax.ppermute only.
A program may use at most 128 MiB of HBM per device.

v0:
```python
from functools import partial

import jax
import jax.numpy as jnp
from jax import lax
from jax.experimental import pallas as pl
from jax.experimental.pallas import tpu as pltpu
from jax.sharding import PartitionSpec as P

HD = 64
GROUP = 256
BLOCK = 256
EPSILON = 1e-05
MASKED = -1e30
LOG2E = 1.4426950408889634
SCORE = HD**-0.5 * LOG2E
EXTRA = 16
FEW = 1000
BF = jnp.bfloat16
F32 = jnp.float32


def after(value, *others):
    return lax.optimization_barrier((value,) + others)[0] if others else value


def nt(a, b):
    return lax.dot_general(a, b, (((1,), (1,)), ((), ())), preferred_element_type=F32)


def nn(a, b):
    return lax.dot_general(a, b, (((1,), (0,)), ((), ())), preferred_element_type=F32)


def line_first(own):
    below = lax.ppermute(own, "tensor", [(0, 1), (1, 2), (2, 3)])
    above = lax.ppermute(own, "tensor", [(1, 0), (2, 1), (3, 2)])
    return jnp.where(lax.axis_index("tensor") < 3, above, below), below, above


def line_second(below, above, *gate):
    below2 = lax.ppermute(below, "tensor", [(1, 2), (2, 3)])
    above2 = lax.ppermute(above, "tensor", [(2, 1), (1, 0)])
    below2, above2 = after((below2, above2), *gate)
    return jnp.where(lax.axis_index("tensor") < 2, above2, below2)


def line_third(slot_c, below, *gate):
    far = after(lax.ppermute(slot_c, "tensor", [(1, 0), (2, 3)]), *gate)
    t = lax.axis_index("tensor")
    return jnp.where((t == 0) | (t == 3), far, below)


def slot_owner(t):
    return jnp.stack([t, jnp.where(t < 3, t + 1, 2), lax.rem(t + 2, 4), jnp.where(t == 3, 0, lax.rem(t + 3, 4))])


def owner_slot(t):
    owner = slot_owner(t)
    places = jnp.arange(4)
    return [jnp.sum(jnp.where(owner == j, places, 0)) for j in range(4)]


def in_line_order(slots, t):
    return jnp.concatenate([lax.dynamic_slice_in_dim(slots, s, 1, axis=0) for s in owner_slot(t)])


def spread(slots, t):
    owner = slot_owner(t)
    arrived = []
    for shift in (1, 3, 2):
        goal = lax.rem(t + shift, 4)
        slot = sum(jnp.where(owner[j] == goal, j, 0) for j in range(4))
        block = lax.dynamic_index_in_dim(slots, slot, 0, keepdims=False)
        arrived.append(lax.ppermute(block, "tensor", [(i, (i + shift) % 4) for i in range(4)]))
    return arrived


def total(own, arrived):
    return own.astype(F32) + sum(a.astype(F32) for a in arrived)


def partner(bit):
    n = lax.axis_size("fsdp")
    return [(i, i ^ bit) for i in range(n)]


def outer_bits():
    n = lax.axis_size("fsdp")
    return [1 << k for k in range(1, n.bit_length() - 1)]


def assembled(pieces):
    n = len(pieces)
    f = lax.axis_index("fsdp")
    stacked = jnp.stack(pieces).reshape(2, n // 2, *pieces[0].shape)
    blocks = []
    for a in range(n):
        rel = f ^ a
        block = lax.dynamic_slice_in_dim(stacked, rel & 1, 1, axis=0)
        blocks.append(lax.dynamic_slice_in_dim(block, rel >> 1, 1, axis=1)[0, 0])
    return jnp.concatenate(blocks)


def outer_axes(block):
    n = lax.axis_size("fsdp")
    bits = outer_bits()
    return block.reshape((2,) * len(bits) + (block.shape[0] // (n // 2), block.shape[1])), sorted(bits, reverse=True)


def start_halving(blocks, lefts, pair):
    kept, arrived, rest = [], [], []
    for block, left, bit in zip(blocks, lefts, pair):
        axis = left.index(bit)
        kept.append(lax.index_in_dim(block, 0, axis, keepdims=False))
        arrived.append(lax.ppermute(lax.index_in_dim(block, 1, axis, keepdims=False), "fsdp", partner(bit)))
        rest.append([b for b in left if b != bit])
    return kept, arrived, rest


def add_low(kept, arrived):
    return [(a.astype(F32) + b.astype(F32)).astype(BF) for a, b in zip(kept, arrived)]


def stack_heads(x):
    lane = lax.broadcasted_iota(jnp.int32, (BLOCK, x.shape[1]), 1)
    zero = jnp.zeros((BLOCK, x.shape[1]), x.dtype)
    heads = x.shape[1] // HD
    return jnp.concatenate(
        [
            jnp.where((lane >= h * HD) & (lane < (h + 1) * HD), x[j * BLOCK : (j + 1) * BLOCK], zero)
            for j in range(x.shape[0] // BLOCK)
            for h in range(heads)
        ],
        axis=0,
    )


def block_kind(seg, q_at, k_at):
    q_lo, q_hi = seg[q_at], seg[q_at + BLOCK - 1]
    k_lo, k_hi = seg[k_at], seg[k_at + BLOCK - 1]
    meet = (q_lo <= k_hi) & (k_lo <= q_hi)
    one = (q_lo == q_hi) & (k_lo == q_lo) & (k_hi == q_lo)
    return jnp.where(one, 2, jnp.where(meet, 1, 0))


def ids_down(ids_refs, col_s):
    rows = ids_refs[0].shape[1]

    @pl.when(pl.program_id(0) == 0)
    def _():
        for j, ids in enumerate(ids_refs):
            wide = jnp.broadcast_to(ids[...].astype(F32), (col_s.shape[1], rows))
            col_s[j * rows : (j + 1) * rows, :] = wide.T


def each_block(seg, where, slots, rows, visit):
    per = rows // BLOCK
    for j, slot in enumerate(slots):

        def step(i, _, j=j, slot=slot):
            kb, qb = i // per, lax.rem(i, per)
            at = pl.ds(pl.multiple_of(kb * BLOCK, BLOCK), BLOCK)
            kind = block_kind(seg, where[0] * rows + qb * BLOCK, where[1 + slot] * rows + kb * BLOCK)
            visit(j, at, kb, qb, kind)
            return 0

        lax.fori_loop(0, per * per, step, 0)


def piece_copy(pieces, j, f, column, width, target, sem):
    r = pieces[0].shape[0]
    place = 0
    if len(pieces) > 1:
        core, outer = j // (len(pieces) // 2), j % (len(pieces) // 2)
        place = f ^ (2 * outer + core)
    rows = pl.ds(pl.multiple_of(place * r, r), r)
    return pltpu.make_async_copy(
        pieces[j].at[:, column * width : (column + 1) * width], target.at[rows, :], sem
    )


def lanes(index, size):
    return pl.ds(pl.multiple_of(index * size, size), size)


def forward_kernel(seg, where, *refs, slots, count):
    refs = list(refs)

    def take(count):
        taken, refs[:] = refs[:count], refs[count:]
        return taken

    x_refs = take(len(slots))
    ids_refs = take(len(slots))
    pieces = (take(count), take(count))
    bq_ref, bv_ref, sq_ref = take(3)
    q_ref, k_ref, v_ref, o_ref, lse_ref, w_ref, q_s, col_s, m_s, l_s, acc_s, ids_s, w_s, sems = refs

    @pl.when(pl.program_id(0) == 0)
    def _():
        copies = [
            piece_copy(pieces[m // 2], j, where[6], m % 2, w_s.shape[2], w_s.at[m], sems.at[m, j])
            for m in range(3)
            for j in range(count)
        ]
        for copy in copies:
            copy.start()
        for copy in copies:
            copy.wait()

    w_ref[...] = w_s[:, :, lanes(pl.program_id(0), q_ref.shape[1])]
    wq_ref, wk_ref, wv_ref = (w_ref.at[m] for m in range(3))
    rows, width = q_ref.shape
    heads = width // HD
    wide = heads * BLOCK
    q_ref[...] = (nn(x_refs[0][...], wq_ref[...]) + bq_ref[...]).astype(BF)
    m_s[...] = jnp.full(m_s.shape, MASKED, F32)
    l_s[...] = jnp.zeros(l_s.shape, F32)
    acc_s[...] = jnp.zeros(acc_s.shape, F32)
    for j, x_ref in enumerate(x_refs):
        at = slice(j * rows, (j + 1) * rows)
        k_ref[at, :] = nn(x_ref[...], wk_ref[...]).astype(BF)
        v_ref[at, :] = (nn(x_ref[...], wv_ref[...]) + bv_ref[...]).astype(BF)
    q_s[...] = stack_heads(q_ref[...])
    ids_down(ids_refs, col_s)
    ids_s[...] = sq_ref[...].astype(F32)

    def block(at, qb, masked):
        stacked, part = lanes(qb, wide), lanes(qb, BLOCK)
        s = nt(k_ref[at, :], q_s[stacked, :])
        if masked:
            same = col_s[at, 0:1] == ids_s[:, part]
            s = jnp.where(jnp.concatenate([same] * heads, axis=1), s, MASKED)
        m_old = m_s[:, stacked]
        m_new = jnp.maximum(m_old, jnp.max(s, axis=0, keepdims=True))
        alpha = jnp.exp2((m_old - m_new) * SCORE)
        p = jnp.exp2((s - m_new) * SCORE)
        p_low = p.astype(BF)
        l_s[:, stacked] = alpha * l_s[:, stacked] + jnp.sum(p, axis=0, keepdims=True)
        m_s[:, stacked] = m_new
        v_t = v_ref[at, :].T
        for h in range(heads):
            hs, qs = slice(h * HD, (h + 1) * HD), slice(h * BLOCK, (h + 1) * BLOCK)
            acc_s[hs, part] = acc_s[hs, part] * alpha[:, qs] + nn(v_t[hs], p_low[:, qs])

    def visit(j, _, kb, qb, kind):
        at = pl.ds(pl.multiple_of(j * rows + kb * BLOCK, BLOCK), BLOCK)
        pl.when(kind == 1)(lambda: block(at, qb, True))
        pl.when(kind == 2)(lambda: block(at, qb, False))

    each_block(seg, where, slots, rows, visit)
    for j in range(rows // BLOCK):
        inverse = 1.0 / l_s[:, j * wide : (j + 1) * wide]
        spread_out = jnp.concatenate(
            [jnp.broadcast_to(inverse[:, h * BLOCK : (h + 1) * BLOCK], (HD, BLOCK)) for h in range(heads)], axis=0
        )
        at = slice(j * BLOCK, (j + 1) * BLOCK)
        o_ref[at, :] = (acc_s[:, at] * spread_out).T.astype(BF)
    lse_ref[0] = m_s[...] * SCORE + jnp.log2(l_s[...])


def attend_forward(xs, pieces, biases, seg, where):
    rows, width = xs[0].shape
    slots = tuple(range(len(xs)))
    keys = rows * len(xs)
    count = len(pieces[0])
    groups, wide = width // GROUP, GROUP // HD * rows
    block_spec = pl.BlockSpec((rows, GROUP), lambda i, s, w: (0, i))
    keys_spec = pl.BlockSpec((keys, GROUP), lambda i, s, w: (0, i))
    b_spec = pl.BlockSpec((1, GROUP), lambda i, s, w: (0, i))
    row_spec = pl.BlockSpec((1, 1, wide), lambda i, s, w: (i, 0, 0))
    block_shape = jax.ShapeDtypeStruct((rows, width), BF)
    keys_shape = jax.ShapeDtypeStruct((keys, width), BF)

    def ids_spec(entry):
        return pl.BlockSpec((1, rows), lambda i, s, w: (0, w[entry]))

    in_specs = [pl.BlockSpec((rows, width), lambda i, s, w: (0, 0))] * len(xs)
    in_specs += [ids_spec(1 + s) for s in slots] + [pl.BlockSpec(memory_space=pl.ANY)] * (2 * count) + [b_spec] * 2 + [ids_spec(0)]
    return pl.pallas_call(
        partial(forward_kernel, slots=slots, count=count),
        out_shape=(
            block_shape,
            keys_shape,
            keys_shape,
            block_shape,
            jax.ShapeDtypeStruct((groups, 1, wide), F32),
            jax.ShapeDtypeStruct((3, width, width), BF),
        ),
        grid_spec=pltpu.PrefetchScalarGridSpec(
            num_scalar_prefetch=2,
            grid=(groups,),
            in_specs=in_specs,
            out_specs=[
                block_spec, keys_spec, keys_spec, block_spec, row_spec,
                pl.BlockSpec((3, width, GROUP), lambda i, s, w: (0, 0, i)),
            ],
            scratch_shapes=[
                pltpu.VMEM((wide, GROUP), BF),
                pltpu.VMEM((keys, 128), F32),
                pltpu.VMEM((1, wide), F32),
                pltpu.VMEM((1, wide), F32),
                pltpu.VMEM((GROUP, rows), F32),
                pltpu.VMEM((1, rows), F32),
                pltpu.VMEM((3, width, width), BF),
                pltpu.SemaphoreType.DMA((3, count)),
            ],
        ),
        cost_estimate=pl.CostEstimate(flops=FEW, bytes_accessed=FEW, transcendentals=0),
        name="attend_forward",
    )(seg[0], where, *xs, *([seg] * len(slots)), *pieces[0], *pieces[1], *(b[None, :] for b in biases), seg)


def backward_kernel(seg, where, *refs, slots, first, last):
    refs = list(refs)

    def take(count):
        taken, refs[:] = refs[:count], refs[count:]
        return taken

    q_ref, do_ref, o_ref, lse_ref, wk_ref, wv_ref, sq_ref = take(7)
    k_refs, v_refs, ids_refs = take(len(slots)), take(len(slots)), take(len(slots))
    if not first:
        (dq_in,) = take(1)
    if last:
        wq_ref, base_ref = take(2)
        dk_s, dv_s, dq_ref, dx_ref, q_s, do_s, delta_s, col_s, ids_s, dx_s, dq_s = refs
    else:
        dk_s, dv_s, dq_s, dx_ref, q_s, do_s, delta_s, col_s, ids_s, dx_s = refs
    g = pl.program_id(0)
    ids_down(ids_refs, col_s)
    ids_s[...] = sq_ref[...].astype(F32)
    rows, width = q_ref.shape
    heads = width // HD
    wide = heads * BLOCK
    q_s[...] = stack_heads(q_ref[...])
    do_s[...] = stack_heads(do_ref[...])
    prod = (do_ref[...].astype(F32) * o_ref[...].astype(F32)).T
    for j in range(rows // BLOCK):
        for h in range(heads):
            piece = prod[h * HD : (h + 1) * HD, j * BLOCK : (j + 1) * BLOCK]
            delta_s[:, j * wide + h * BLOCK : j * wide + (h + 1) * BLOCK] = jnp.sum(piece, axis=0, keepdims=True)
    dq_s[...] = jnp.zeros_like(dq_s) if first else dq_in[...]

    def block(j, at, out_at, qb, masked):
        stacked, part = lanes(qb, wide), lanes(qb, BLOCK)
        k = k_refs[j][at, :]
        k_t = k.T
        s = nt(k, q_s[stacked, :]) * SCORE - lse_ref[0, :, stacked]
        if masked:
            same = col_s[out_at, 0:1] == ids_s[:, part]
            s = jnp.where(jnp.concatenate([same] * heads, axis=1), s, MASKED)
        p = jnp.exp2(s)
        dp = nt(v_refs[j][at, :], do_s[stacked, :])
        ds = (p * (dp - delta_s[:, stacked])).astype(BF)
        dv = nn(p.astype(BF), do_s[stacked, :])
        dk = nn(ds, q_s[stacked, :])
        for h in range(heads):
            hs = slice(h * HD, (h + 1) * HD)
            dq_s[hs, part] += nn(k_t[hs], ds[:, h * BLOCK : (h + 1) * BLOCK])
        return dk, dv

    def visit(j, at, kb, qb, kind):
        out_at = pl.ds(pl.multiple_of(j * rows + kb * BLOCK, BLOCK), BLOCK)

        @pl.when(qb == 0)
        def _():
            acc_k[...] = jnp.zeros(acc_k.shape, F32)
            acc_v[...] = jnp.zeros(acc_v.shape, F32)

        def add(masked):
            dk, dv = block(j, at, out_at, qb, masked)
            acc_k[...] += dk
            acc_v[...] += dv

        pl.when(kind == 1)(lambda: add(True))
        pl.when(kind == 2)(lambda: add(False))

        @pl.when(qb == rows // BLOCK - 1)
        def _():
            dk_s[out_at, :] = (acc_k[...] * HD**-0.5).astype(BF)
            dv_s[out_at, :] = acc_v[...].astype(BF)

    def scoped(acc_k_ref, acc_v_ref):
        nonlocal acc_k, acc_v
        acc_k, acc_v = acc_k_ref, acc_v_ref
        each_block(seg, where, slots, rows, visit)

    acc_k = acc_v = None
    pl.run_scoped(scoped, pltpu.VMEM((BLOCK, width), F32), pltpu.VMEM((BLOCK, width), F32))

    if last:
        dq_ref[...] = (dq_s[...] * HD**-0.5).T.astype(BF)
    for j in range(len(slots)):
        at = slice(j * rows, (j + 1) * rows)
        dx = nt(dk_s[at, :], wk_ref[...]) + nt(dv_s[at, :], wv_ref[...])
        if last and j == 0:
            dx = dx + nt(dq_ref[...], wq_ref[...])

        @pl.when(g == 0)
        def _(at=at, dx=dx, j=j):
            dx_s[at, :] = dx + base_ref[...] if last and j == 0 else dx

        @pl.when(g > 0)
        def _(at=at, dx=dx):
            dx_s[at, :] += dx

    @pl.when(g == pl.num_programs(0) - 1)
    def _():
        dx_ref[...] = dx_s[...].astype(dx_ref.dtype)


def attend_backward(q, k, v, do, o, lse, slots, weights, seg, where, dq=None, base=None):
    rows, width = q.shape
    keys = rows * len(slots)
    first, last = dq is None, base is not None
    groups, wide = width // GROUP, GROUP // HD * rows
    q_spec = pl.BlockSpec((rows, GROUP), lambda i, s, w: (0, i))
    wq_spec, wk_spec, wv_spec = (
        pl.BlockSpec((None, width, GROUP), lambda i, s, w, m=m: (m, 0, i)) for _, m in weights
    )
    row_spec = pl.BlockSpec((1, 1, wide), lambda i, s, w: (i, 0, 0))
    acc_spec = pl.BlockSpec((GROUP, rows), lambda i, s, w: (i, 0))
    keys_spec = pl.BlockSpec((keys, GROUP), lambda i, s, w: (0, i))

    def ids_spec(entry):
        return pl.BlockSpec((1, rows), lambda i, s, w: (0, w[entry]))

    def slot_spec(slot):
        return pl.BlockSpec((rows, GROUP), lambda i, s, w: (slot, i))

    wq, wk, wv = (a for a, _ in weights)
    count = len(slots)
    ins = [q, do, o, lse, wk, wv, seg] + [k] * count + [v] * count + [seg] * count
    in_specs = [q_spec, q_spec, q_spec, row_spec, wk_spec, wv_spec, ids_spec(0)]
    in_specs += [slot_spec(s) for s in slots] * 2 + [ids_spec(1 + s) for s in slots]
    if not first:
        ins.append(dq)
        in_specs.append(acc_spec)
    scratch = [pltpu.VMEM((wide, GROUP), BF), pltpu.VMEM((wide, GROUP), BF), pltpu.VMEM((1, wide), F32)]
    scratch += [pltpu.VMEM((keys, 128), F32), pltpu.VMEM((1, rows), F32), pltpu.VMEM((keys, width), F32)]
    if last:
        ins += [wq, base]
        in_specs += [wq_spec, pl.BlockSpec((rows, width), lambda i, s, w: (0, 0))]
        scratch.append(pltpu.VMEM((GROUP, rows), F32))
    keys_shape = jax.ShapeDtypeStruct((keys, width), BF)
    results = [
        (keys_spec, keys_shape),
        (keys_spec, keys_shape),
        (q_spec, jax.ShapeDtypeStruct((rows, width), BF))
        if last
        else (acc_spec, jax.ShapeDtypeStruct((width, rows), F32)),
        (
            pl.BlockSpec((keys, width), lambda i, s, w: (0, 0)),
            jax.ShapeDtypeStruct((keys, width), F32 if last else BF),
        ),
    ]
    return pl.pallas_call(
        partial(backward_kernel, slots=slots, first=first, last=last),
        out_shape=tuple(r[1] for r in results),
        grid_spec=pltpu.PrefetchScalarGridSpec(
            num_scalar_prefetch=2,
            grid=(groups,),
            in_specs=in_specs,
            out_specs=[r[0] for r in results],
            scratch_shapes=scratch,
        ),
        cost_estimate=pl.CostEstimate(flops=FEW, bytes_accessed=FEW, transcendentals=0),
        name="attend_backward",
    )(seg[0], where, *ins)


def attn_grad_kernel(core_ref, *refs, calls, slots, block_rows):
    x_refs, dq_ref, extra_ref, refs = refs[:slots], refs[slots], refs[slots + 1], refs[slots + 2 :]
    dk_refs, dv_refs, refs = refs[:calls], refs[calls : 2 * calls], refs[2 * calls :]
    first_ref, second_ref, x_s, w_s = refs
    rows = dq_ref.shape[0]

    @pl.when(pl.program_id(0) == 0)
    def _():
        for j, x_ref in enumerate(x_refs):
            x_s[:, j * rows : (j + 1) * rows] = x_ref[...].T

    sums = [
        jnp.sum(dq_ref[...].astype(F32), axis=0, keepdims=True),
        sum(jnp.sum(d[...].astype(F32), axis=0, keepdims=True) for d in dv_refs),
        extra_ref[...],
        jnp.zeros((EXTRA - 2 - extra_ref.shape[0], w_s.shape[1]), F32),
    ]
    sums = jnp.concatenate(sums, axis=0)

    def over_keys(parts):
        total, start = 0.0, 0
        for d in parts:
            total = total + nn(x_s[:, start : start + d.shape[0]], d[...])
            start += d.shape[0]
        return total

    for m, parts in enumerate(((dq_ref,), dk_refs, dv_refs)):
        if not block_rows:
            first_ref[m] = over_keys(parts)
            continue
        w_s[...] = over_keys(parts)
        core = core_ref[0]
        at = slice(m * block_rows, (m + 1) * block_rows)
        for b in range(first_ref.shape[0]):
            far = pl.multiple_of((2 * b + 1 - core) * block_rows, block_rows)
            near = pl.multiple_of((2 * b + core) * block_rows, block_rows)
            first_ref[b, at] = w_s[pl.ds(far, block_rows), :].astype(BF)
            second_ref[b, at] = w_s[pl.ds(near, block_rows), :]
    if block_rows:
        for b in range(first_ref.shape[0]):
            first_ref[b, 3 * block_rows :] = sums.astype(BF)
            second_ref[b, 3 * block_rows :] = sums
    else:
        second_ref[...] = sums


def attn_grads(core, xs, dq, extra, dks, dvs, n):
    rows, width = dq.shape
    block_rows = width // n if (width // n) % 16 == 0 else 0
    x_spec = pl.BlockSpec((rows, width), lambda i, c: (0, 0))

    def d_spec(d):
        return pl.BlockSpec((d.shape[0], GROUP), lambda i, c: (0, i))

    if block_rows:
        shape = (n // 2, 3 * block_rows + EXTRA)
        spec = pl.BlockSpec((*shape, GROUP), lambda i, c: (0, 0, i))
        results = [(spec, jax.ShapeDtypeStruct((*shape, width), t)) for t in (BF, F32)]
    else:
        spec = pl.BlockSpec((3, width, GROUP), lambda i, c: (0, 0, i))
        results = [(spec, jax.ShapeDtypeStruct((3, width, width), F32))]
        spec = pl.BlockSpec((EXTRA, GROUP), lambda i, c: (0, i))
        results.append((spec, jax.ShapeDtypeStruct((EXTRA, width), F32)))
    return pl.pallas_call(
        partial(attn_grad_kernel, calls=len(dks), slots=len(xs), block_rows=block_rows),
        out_shape=tuple(r[1] for r in results),
        grid_spec=pltpu.PrefetchScalarGridSpec(
            num_scalar_prefetch=1,
            grid=(width // GROUP,),
            in_specs=[x_spec] * len(xs) + [d_spec(d) for d in (dq, extra, *dks, *dvs)],
            out_specs=[r[0] for r in results],
            scratch_shapes=[pltpu.VMEM((width, rows * len(xs)), BF), pltpu.VMEM((width, GROUP), F32)],
        ),
        cost_estimate=pl.CostEstimate(flops=FEW, bytes_accessed=FEW, transcendentals=0),
        name="attn_grads",
    )(core, *xs, dq, extra, *dks, *dvs)


def norm_parts(rows_in):
    mean = jnp.mean(rows_in, axis=-1, keepdims=True)
    centred = rows_in - mean
    spread = jnp.mean(centred * centred, axis=-1, keepdims=True)
    r = lax.rsqrt(spread + EPSILON)
    return centred * r, r


def norm_back(g_y, n, r, gain):
    e = g_y * gain
    return r * (e - jnp.mean(e, axis=-1, keepdims=True) - n * jnp.mean(e * n, axis=-1, keepdims=True))


def gelu_parts(u):
    c = 0.7978845608028654
    square = u * u
    th = jnp.tanh(c * u * (1.0 + 0.044715 * square))
    half = 0.5 * (1.0 + th)
    slope = half + 0.5 * u * (1.0 - th * th) * (c + 3 * 0.044715 * c * square)
    return u * half, slope


def down_rows(x):
    return jnp.sum(x, axis=0, keepdims=True)


def middle_kernel(known, *refs, count):
    w_refs, refs = (refs[:count], refs[count : 2 * count]), refs[2 * count :]
    ctx_ref, x_ref, grad_ref, vec_ref, bias_ref = refs[:5]
    out_ref, first_ref, gctx_ref, lefts_ref, rights_ref, sums_ref, bias_grad_ref = refs[5:12]
    w_s, mix_ref, slope_s, n1_s, r1_s, acc_s, sems, mix_sems = refs[12:]
    parts, units = bias_ref.shape
    rows, width = x_ref.shape

    def copy(which, t, j):
        return piece_copy(
            w_refs[which], j, known[1], 2 * width // units + t, units, w_s.at[which, t], sems.at[which, t, j]
        )

    mix_copies = [
        piece_copy(w_refs[1], j, known[1], 1, width, mix_ref, mix_sems.at[j]) for j in range(count)
    ]
    for mix_copy in mix_copies:
        mix_copy.start()
    for which in range(2):
        for t in range(parts):
            for j in range(count):
                copy(which, t, j).start()
    for mix_copy in mix_copies:
        mix_copy.wait()

    def cols(t):
        return pl.ds(pl.multiple_of(t * units, units), units)

    first_sum = x_ref[...].astype(F32) + nt(ctx_ref[...], mix_ref[...]) + vec_ref[0:1, :]
    n1, r1 = norm_parts(first_sum)
    n1_s[...] = n1
    r1_s[...] = jnp.broadcast_to(r1, r1_s.shape)
    acc_s[...] = n1 * vec_ref[1:2, :] + vec_ref[2:3, :]
    lefts_ref[1] = acc_s[...].astype(BF)

    for which in range(2):
        for t in range(parts):
            for j in range(count):
                copy(which, t, j).wait()

    def up(t, _):
        pre = nn(lefts_ref[1], w_s[0, t]) + bias_ref[pl.ds(t, 1), :]
        act, slope = gelu_parts(pre)
        slope_s[t] = slope
        low = act.astype(BF)
        rights_ref[:, cols(t)] = low
        acc_s[...] += nt(low, w_s[1, t])
        return 0

    lax.fori_loop(0, parts, up, 0)
    n2, r2 = norm_parts(acc_s[...] + vec_ref[3:4, :])
    out_ref[...] = (n2 * vec_ref[4:5, :] + vec_ref[5:6, :]).astype(BF)
    row = lax.broadcasted_iota(jnp.int32, (rows, width), 0)
    g_out = jnp.where(row < known[0], grad_ref[...].astype(F32), 0.0)
    g_second = norm_back(g_out, n2, r2, vec_ref[4:5, :])
    sums_ref[3:4, :] = down_rows(g_second)
    sums_ref[4:5, :] = down_rows(g_out * n2)
    sums_ref[5:6, :] = down_rows(g_out)
    lefts_ref[0] = g_second.astype(BF)
    acc_s[...] = g_second

    def back(t, _):
        g_pre = (nn(lefts_ref[0], w_s[1, t]) * slope_s[t]).astype(BF)
        rights_ref[:, cols(parts + t)] = g_pre
        bias_grad_ref[pl.ds(t, 1), :] = down_rows(g_pre.astype(F32))
        acc_s[...] += nt(g_pre, w_s[0, t])
        return 0

    lax.fori_loop(0, parts, back, 0)
    g_normed = acc_s[...]
    n1 = n1_s[...]
    g_first = norm_back(g_normed, n1, r1_s[:, 0:1], vec_ref[1:2, :])
    sums_ref[0:1, :] = down_rows(g_first)
    sums_ref[1:2, :] = down_rows(g_normed * n1)
    sums_ref[2:3, :] = down_rows(g_normed)
    sums_ref[6:8, :] = jnp.zeros((2, width), F32)
    first_ref[...] = g_first
    low = g_first.astype(BF)
    lefts_ref[2] = low
    gctx_ref[...] = nn(low, mix_ref[...]).astype(BF)
    rights_ref[:, 2 * parts * units :] = ctx_ref[...]


def middle(known, pieces, ctx, x, grad, vectors, bias):
    rows, width = x.shape
    parts, units = bias.shape
    count = len(pieces[0])
    vmem = pl.BlockSpec(memory_space=pltpu.VMEM)
    shapes = [
        ((rows, width), BF),
        ((rows, width), F32),
        ((rows, width), BF),
        ((3, rows, width), BF),
        ((rows, 2 * parts * units + width), BF),
        ((8, width), F32),
        ((parts, units), F32),
    ]
    return pl.pallas_call(
        partial(middle_kernel, count=count),
        out_shape=tuple(jax.ShapeDtypeStruct(*s) for s in shapes),
        in_specs=[pl.BlockSpec(memory_space=pltpu.SMEM)] + [pl.BlockSpec(memory_space=pl.ANY)] * (2 * count) + [vmem] * 5,
        out_specs=[vmem] * len(shapes),
        scratch_shapes=[
            pltpu.VMEM((2, parts, width, units), BF),
            pltpu.VMEM((width, width), BF),
            pltpu.VMEM((parts, rows, units), F32),
            pltpu.VMEM((rows, width), F32),
            pltpu.VMEM((rows, 128), F32),
            pltpu.VMEM((rows, width), F32),
            pltpu.SemaphoreType.DMA((2, parts, count)),
            pltpu.SemaphoreType.DMA((count,)),
        ],
        compiler_params=pltpu.CompilerParams(vmem_limit_bytes=63 << 20),
        cost_estimate=pl.CostEstimate(flops=FEW, bytes_accessed=FEW, transcendentals=0),
        name="middle",
    )(known, *pieces[0], *pieces[1], ctx, x, grad, vectors, bias)


def ffn_grad_kernel(place, left_ref, right_ref, *refs, core):
    out_ref, left_s, chosen_s = refs[-3:]

    @pl.when(pl.program_id(0) % 4 == 0)
    def _():
        left_s[...] = left_ref[0].T
        if core is not None:
            size = left_s.shape[0] // core[1]
            for q in range(core[1] // 2):
                block = place[0] ^ (2 * q + core[0])
                chosen_s[q * size : (q + 1) * size, :] = left_s[pl.ds(pl.multiple_of(block * size, size), size), :]

    total = nn((left_s if core is None else chosen_s)[...], right_ref[...])
    if len(refs) == 4:
        total = total + refs[0][...].astype(F32)
    out_ref[...] = total.astype(BF)


def ffn_grads(place, lefts, rights, core=None, got=None):
    _, rows, width = lefts.shape
    units = rights.shape[1] // 9
    out_rows = width if core is None else width // 2
    out_spec = pl.BlockSpec((out_rows, units), lambda i, p: (0, i))
    return pl.pallas_call(
        partial(ffn_grad_kernel, core=core),
        out_shape=jax.ShapeDtypeStruct((out_rows, rights.shape[1]), BF),
        grid_spec=pltpu.PrefetchScalarGridSpec(
            num_scalar_prefetch=1,
            grid=(9,),
            in_specs=[
                pl.BlockSpec((1, rows, width), lambda i, p: (i // 4, 0, 0)),
                pl.BlockSpec((rows, units), lambda i, p: (0, i)),
            ]
            + ([] if got is None else [out_spec]),
            out_specs=out_spec,
            scratch_shapes=[pltpu.VMEM((width, rows), BF), pltpu.VMEM((width // 2, rows), BF)],
        ),
        cost_estimate=pl.CostEstimate(flops=FEW, bytes_accessed=FEW, transcendentals=0),
        name="ffn_grads",
    )(place, lefts, rights, *(() if got is None else (got,)))


def on_device(
    tokens,
    segments,
    query_weight,
    query_bias,
    key_weight,
    value_weight,
    value_bias,
    mix_weight,
    mix_bias,
    norm_gain,
    norm_shift,
    up_weight,
    up_bias,
    down_weight,
    down_bias,
    final_gain,
    final_shift,
    out_grad,
):
    t = lax.axis_index("tensor")
    f = lax.axis_index("fsdp")
    n = lax.axis_size("fsdp")
    rows, width = tokens.shape
    r, units = up_weight.shape
    cols = query_weight.shape[1]
    owner = slot_owner(t)

    shard = jnp.stack(
        [
            jnp.concatenate([query_weight, key_weight, value_weight, mix_weight.T], axis=1),
            up_weight,
            down_weight.T,
        ]
    )
    w_a, w_below, w_above = line_first(shard)
    w_c = line_second(w_below, w_above)
    x_a, x_below, x_above = line_first(after(tokens, w_c))
    w_slots = (shard, w_a, w_c, line_third(w_c, w_below))

    def half(first, last):
        line = [w[0][:, m * cols : (m + 1) * cols] for m in (first, first + 1) for w in w_slots]
        return jnp.concatenate(line + [w[last] for w in w_slots], axis=1)

    own = (half(0, 1), half(2, 2))
    bits = outer_bits()
    orders = (bits, bits[::-1])
    held = [{0: own[0]}, {0: own[1]}]
    passed = []

    def pass_on(step):
        arrived = []
        for i in range(2):
            bit = orders[i][step]
            for place in sorted(held[i]):
                got = lax.ppermute(held[i][place], "fsdp", partner(bit))
                arrived.append((i, place | (bit >> 1), got))
        return arrived

    def keep(arrived, *gate):
        values = after(tuple(a[2] for a in arrived), *gate)
        for (i, place, _), value in zip(arrived, values):
            held[i][place] = value
        passed.append(values)

    def to_partner(values, *gate):
        return after(tuple(lax.ppermute(v, "fsdp", partner(1)) for v in values), *gate)

    first = pass_on(0)
    direct = []
    if len(bits) == 2:
        direct = [
            (i, orders[i][1] >> 1, lax.ppermute(own[i], "fsdp", partner(orders[i][1]))) for i in range(2)
        ]
    far_own = to_partner(own)
    keep(first, x_a)
    x_c = line_second(*after((x_below, x_above), *passed[0]))
    if direct:
        forwarded = [
            (i, 3, lax.ppermute(held[i][orders[i][0] >> 1], "fsdp", partner(orders[i][1]))) for i in range(2)
        ]
        far_first = to_partner(passed[0])
        keep(direct, x_c, *far_own)
        x_b = line_third(after(x_c, *passed[1]), x_below, *far_first)
        far_direct = to_partner(passed[1])
        keep(forwarded)
        far_last = to_partner(passed[2])
        far = [{0: far_own[i], orders[i][0] >> 1: far_first[i]} for i in range(2)]
        for i in range(2):
            far[i][orders[i][1] >> 1], far[i][3] = far_direct[i], far_last[i]
    else:
        x_b = line_third(x_c, x_below)
        for step in range(1, len(bits)):
            keep(pass_on(step))
        far = [dict(zip(sorted(h), to_partner([h[p] for p in sorted(h)]))) for h in held]
    pieces = [[h[p] for h in (near, away) for p in sorted(near)] for near, away in zip(held, far)]
    if r % 16:
        pieces = [[assembled(p)] for p in pieces]

    def by_slot(vector):
        parts = vector.reshape(4, -1)
        return jnp.concatenate([lax.dynamic_slice_in_dim(parts, owner[i], 1, axis=0)[0] for i in range(4)])

    seg = jnp.where(segments == 0, 9, segments)
    where = jnp.concatenate([t[None], owner, (f & 1)[None], f[None]]).astype(jnp.int32)
    xs = (tokens, x_a, x_c, x_b)
    q, k, v, ctx, lse, w_all = attend_forward(xs, pieces, (by_slot(query_bias), by_slot(value_bias)), seg, where)
    weights = tuple((w_all, m) for m in range(3))

    own_ids = lax.dynamic_slice_in_dim(seg[0], t * rows, rows)
    known = jnp.stack([jnp.sum((own_ids < 9).astype(jnp.int32)), f.astype(jnp.int32)])
    vectors = jnp.stack([mix_bias, norm_gain, norm_shift, down_bias, final_gain, final_shift])
    layer_out, g_first, g_ctx, lefts, rights, sums, up_sums = middle(
        known, pieces, ctx, tokens, out_grad, vectors, by_slot(up_bias).reshape(4, units)
    )
    place = f.astype(jnp.int32)[None]
    if r % 16:
        full = ffn_grads(place, lefts, rights).reshape(n, r, -1)
        kept, sent = (
            jnp.concatenate([lax.dynamic_slice_in_dim(full, f ^ (2 * q + c), 1)[0] for q in range(n // 2)])
            for c in range(2)
        )
    else:
        sent = ffn_grads(place, lefts, rights, (1, n))
    got = lax.ppermute(sent, "fsdp", partner(1))
    g_ctx = after(g_ctx, sent)

    args = (q, k, v, g_ctx, ctx, lse)
    dk_b, dv_b, dq, dx_b = attend_backward(*args, (3,), weights, seg, where)
    r1 = lax.ppermute(dx_b, "tensor", [(0, 1), (3, 2)])
    lefts = after(lefts, dx_b)
    if r % 16:
        near = (kept.astype(F32) + got.astype(F32)).astype(BF)
    else:
        near = ffn_grads(place, lefts, rights, (0, n), got)
    steps = list(zip(outer_bits(), outer_bits()[::-1]))
    blocks, lefts = zip(*(outer_axes(b) for b in (near[:, : 4 * units], near[:, 4 * units :])))
    halves = start_halving(blocks, lefts, steps[0])
    dk_n, dv_n, dq, dx_n = attend_backward(*args, (2, 1), weights, seg, where, after(dq, near))
    dx_c, dx_a = dx_n[:rows], dx_n[rows:]
    blocks = add_low(halves[0], after(halves[1], dx_n))
    halves = start_halving(blocks, halves[2], steps[1])
    middle_x = (dx_c.astype(F32) + r1.astype(F32)).astype(BF)
    rx = lax.ppermute(middle_x, "tensor", [(0, 1), (3, 2)])
    ry = lax.ppermute(middle_x, "tensor", [(1, 2), (2, 1)])
    dk_o, dv_o, dq, dx_own = attend_backward(
        *args, (0,), weights, seg, where, after(dq, middle_x, *blocks), g_first
    )
    rx, ry = (a.astype(F32) for a in after((rx, ry), dx_own))
    up_x = (dx_a.astype(F32) + jnp.where(t == 1, rx, ry)).astype(BF)
    down_x = jnp.where(t == 3, dx_a.astype(F32), dx_b.astype(F32) + jnp.where(t == 1, ry, rx)).astype(BF)
    from_below = lax.ppermute(up_x, "tensor", [(0, 1), (1, 2), (2, 3)])
    from_above = lax.ppermute(down_x, "tensor", [(1, 0), (2, 1), (3, 2)])

    d_one, d_two = add_low(halves[0], after(halves[1], dx_own))
    for pair in steps[2:]:
        halves = start_halving([d_one, d_two], halves[2], pair)
        d_one, d_two = add_low(halves[0], halves[1])
    early = jnp.stack(
        [
            jnp.concatenate(
                [
                    d_one[:, i * units : (i + 1) * units],
                    d_two[:, i * units : (i + 1) * units],
                    d_two[:, 4 * units + i * cols : 4 * units + (i + 1) * cols],
                ],
                axis=1,
            )
            for i in range(4)
        ]
    )

    xs = (xs[0], xs[2], xs[1], xs[3])
    extra = jnp.concatenate([sums[:6], in_line_order(up_sums, t)])
    dq = after(dq, up_x, down_x, early)
    sent, kept = attn_grads(where[5:6], xs, dq, extra, (dk_o, dk_n, dk_b), (dv_o, dv_n, dv_b), n)
    if r % 16:
        split = sent.reshape(3, n // 2, 2, r, width)
        sums = jnp.broadcast_to(kept, (n // 2, EXTRA, width))
        sent, kept = (
            jnp.concatenate(
                [
                    lax.dynamic_index_in_dim(split, c, 2, keepdims=False)
                    .transpose(1, 0, 2, 3)
                    .reshape(n // 2, 3 * r, width),
                    sums,
                ],
                axis=1,
            )
            for c in (1 - (f & 1), f & 1)
        )
        sent = sent.astype(BF)
    sent = after(sent, from_below, from_above)
    early_own, early = early[0], spread(early, t)
    got = lax.ppermute(sent, "fsdp", partner(1))
    near = (kept + after(got, early[0]).astype(F32)).astype(BF)
    same_core = [list(range(c, n, 2)) for c in range(2)]
    arrived = lax.all_to_all(near, "fsdp", split_axis=0, concat_axis=0, axis_index_groups=same_core, tiled=True)
    arrived = after(arrived, *early)
    late = jnp.sum(arrived.astype(F32), axis=0).astype(BF)
    count = 12
    by_head = jnp.stack([late[3 * r : 3 * r + 2, i * cols : (i + 1) * cols] for i in range(4)])
    by_head = in_line_order(by_head, t).reshape(8, cols)
    whole = [late[3 * r + 2 : 3 * r + count, i * cols : (i + 1) * cols] for i in range(4)]
    below = jnp.concatenate([by_head, *whole])
    late = jnp.stack(
        [jnp.concatenate([late[: 3 * r, i * cols : (i + 1) * cols], below]) for i in range(4)]
    )
    late = total(late[0], spread(late, t))
    early = total(early_own, early)
    tokens_grad = dx_own + from_below.astype(F32) + from_above.astype(F32)
    qv = late[3 * r : 3 * r + 8].reshape(4, 2, cols).transpose(1, 0, 2).reshape(2, width)
    sums = late[3 * r + 8 :].reshape(4, count - 2, cols).transpose(1, 0, 2).reshape(count - 2, width)
    up_sums = sums[6:].reshape(-1)
    late = late[: 3 * r].reshape(3, r, cols)

    return (
        layer_out,
        tokens_grad,
        late[0],
        qv[0],
        late[1],
        late[2],
        qv[1],
        early[:, 2 * units :].T,
        sums[0],
        sums[1],
        sums[2],
        early[:, units : 2 * units],
        up_sums,
        early[:, :units].T,
        sums[3],
        sums[4],
        sums[5],
    )


def solution(mesh):
    both, rows_f, square, flipped = (
        P(("fsdp", "tensor"), None),
        P("fsdp", None),
        P("fsdp", "tensor"),
        P("tensor", "fsdp"),
    )
    return jax.shard_map(
        on_device,
        mesh=mesh,
        in_specs=(
            both, rows_f, square, P(), square, square, P(), flipped, P(), P(), P(),
            square, P(), flipped, P(), P(), P(), both,
        ),
        out_specs=(
            both, both, square, P(), square, square, P(), flipped, P(), P(), P(),
            square, P(), flipped, P(), P(), P(),
        ),
        check_vma=False,
    )
```

profile of v0, /device:TPU:0, one launch (start us, length us, event | category | flops | bytes accessed | tf_op | source)
XLA Modules:
  0.0 432.5 jit_solution(441074342007713142)
XLA Ops:
  4.9 5.6 %collective-permute-start.1 = (bf16[3,96,768]{2,1,0:T(8,128)(2,1)S(1)}, bf16[3,96,768]{2,1,0:T(8,128)(2,1)S(1)}, u32[]{:S(2)}, u32[]{:S(2)}) collective-permute-start(bf16[3,96,768]{2,1,0:T(8,128)(2,1)S(1)} %pad_maximum_fusion.2), channel_id=1, source_target_pairs={{0,1},{1,2},{2,3},{4,5},{5,6},{6,7},{8,9},{9,10},{10,11},{12,13},{... | collective-permute-start | bytes 1327112 | tf_op jit(solution)/shard_map/ppermute | solution.py:36
  10.5 8.2 %collective-permute-done = bf16[3,96,768]{2,1,0:T(8,128)(2,1)S(1)} collective-permute-done((bf16[3,96,768]{2,1,0:T(8,128)(2,1)S(1)}, bf16[3,96,768]{2,1,0:T(8,128)(2,1)S(1)}, u32[]{:S(2)}, u32[]{:S(2)}) %collective-permute-start) | collective-permute-done | bytes 442400 | tf_op jit(solution)/shard_map/ppermute | solution.py:37
  20.7 11.2 %collective-permute-done.2 = bf16[3,96,768]{2,1,0:T(8,128)(2,1)S(1)} collective-permute-done((bf16[3,96,768]{2,1,0:T(8,128)(2,1)S(1)}, bf16[3,96,768]{2,1,0:T(8,128)(2,1)S(1)}, u32[]{:S(2)}, u32[]{:S(2)}) %collective-permute-start.2) | collective-permute-done | bytes 442400 | tf_op jit(solution)/shard_map/ppermute | solution.py:43
  33.3 5.5 %collective-permute-start.8 = (bf16[512,768]{1,0:T(8,128)(2,1)S(1)}, bf16[512,768]{1,0:T(8,128)(2,1)}, u32[]{:S(2)}, u32[]{:S(2)}) collective-permute-start(bf16[512,768]{1,0:T(8,128)(2,1)S(1)} %copy-done.2), channel_id=1, source_target_pairs={{0,1},{1,2},{2,3},{4,5},{5,6},{6,7},{8,9},{9,10},{10,11},{12,13},{... | collective-permute-start | bytes 2359304 | tf_op jit(solution)/shard_map/ppermute | solution.py:36
  40.9 5.6 %collective-permute-done.4 = bf16[3,96,768]{2,1,0:T(8,128)(2,1)S(1)} collective-permute-done((bf16[3,96,768]{2,1,0:T(8,128)(2,1)S(1)}, bf16[3,96,768]{2,1,0:T(8,128)(2,1)S(1)}, u32[]{:S(2)}, u32[]{:S(2)}) %collective-permute-start.4) | collective-permute-done | bytes 442400 | tf_op jit(solution)/shard_map/ppermute | solution.py:49
  51.5 1.6 collective-permute-start.5
  53.6 7.7 %collective-permute-done.7 = bf16[512,768]{1,0:T(8,128)(2,1)} collective-permute-done((bf16[512,768]{1,0:T(8,128)(2,1)S(1)}, bf16[512,768]{1,0:T(8,128)(2,1)}, u32[]{:S(2)}, u32[]{:S(2)}) %collective-permute-start.7) | collective-permute-done | bytes 786464 | tf_op jit(solution)/shard_map/ppermute | solution.py:37
  61.3 2.1 broadcast_select_fusion.2.refs_1_.refs_2_
  63.5 2.6 collective-permute-done.6.refs_18_.refs_10_
  66.1 8.2 %collective-permute-done.5.refs_9_.refs_1_ = bf16[96,4608]{1,0:T(8,128)(2,1)} collective-permute-done((bf16[96,4608]{1,0:T(8,128)(2,1)S(1)}, bf16[96,4608]{1,0:T(8,128)(2,1)}, u32[]{:S(2)}, u32[]{:S(2)}) %collective-permute-start.5) | collective-permute-done | bytes 884768 | tf_op jit(solution)/shard_map/ppermute | solution.py:793
  76.3 10.9 %collective-permute-done.10.refs_17_.refs_9_ = bf16[96,4608]{1,0:T(8,128)(2,1)S(1)} collective-permute-done((bf16[96,4608]{1,0:T(8,128)(2,1)S(1)}, bf16[96,4608]{1,0:T(8,128)(2,1)S(1)}, u32[]{:S(2)}, u32[]{:S(2)}) %collective-permute-start.10) | collective-permute-done | bytes 884768 | tf_op jit(solution)/shard_map/ppermute | solution.py:810
  93.6 16.2 %collective-permute-done.9.refs_10_.refs_2_ = bf16[96,4608]{1,0:T(8,128)(2,1)} collective-permute-done((bf16[96,4608]{1,0:T(8,128)(2,1)S(1)}, bf16[96,4608]{1,0:T(8,128)(2,1)}, u32[]{:S(2)}, u32[]{:S(2)}) %collective-permute-start.9) | collective-permute-done | bytes 884768 | tf_op jit(solution)/shard_map/ppermute | solution.py:810
  109.8 1.8 collective-permute-start.23
  112.2 9.6 %collective-permute-done.15.refs_11_.refs_3_ = bf16[96,4608]{1,0:T(8,128)(2,1)} collective-permute-done((bf16[96,4608]{1,0:T(8,128)(2,1)}, bf16[96,4608]{1,0:T(8,128)(2,1)}, u32[]{:S(2)}, u32[]{:S(2)}) %collective-permute-start.15) | collective-permute-done | bytes 884768 | tf_op jit(solution)/shard_map/ppermute | solution.py:817
  127.5 2.1 broadcast_select_fusion.refs_3_
  130.5 26.2 %attend_forward.1 = (bf16[512,768]{1,0:T(8,128)(2,1)}, bf16[2048,768]{1,0:T(8,128)(2,1)}, bf16[2048,768]{1,0:T(8,128)(2,1)}, bf16[512,768]{1,0:T(8,128)(2,1)}, f...) custom-call(s32[2048]{0:T(1024)} %bitcast.112, s32[7]{0:T(128)} %concatenate.59.where, bf16[512,768]{1,0:T(8,128)(2,1)} %refs_0_.3, ...), custom_call_target="tpu_custom_call" | custom-call | flops 1000 | bytes 1000 | tf_op jit(solution)/shard_map/attend_forward/pallas_call | solution.py:281
  156.8 29.1 %middle.1 = (bf16[512,768]{1,0:T(8,128)(2,1)}, f32[512,768]{1,0:T(8,128)}, bf16[512,768]{1,0:T(8,128)(2,1)}, bf16[3,512,768]{2,1,0:T(8,128)(2,1)}, bf16[512,6912...) custom-call(s32[2]{0:T(128)} %pad_add_fusion.known, bf16[96,4608]{1,0:T(8,128)(2,1)} %copy-done.1, ...), custom_call_target="tpu_custom_call" | custom-call | flops 1000 | bytes 1000 | tf_op jit(solution)/shard_map/middle/pallas_call | solution.py:675
  185.9 11.5 %ffn_grads.2 = bf16[384,6912]{1,0:T(8,128)(2,1)} custom-call(s32[1]{0:T(128)} %bitcast.1.place, bf16[3,512,768]{2,1,0:T(8,128)(2,1)} %get-tuple-element.89.left_ref, bf16[512,6912]{1,0:T(8,128)(2,1)} %get-tuple-element.81.right_ref), custom_call_target="tpu_custom_call" | custom-call | flops 1000 | bytes 1000 | tf_op jit(solution)/shard_map/ffn_grads/pallas_call | solution.py:719
  197.4 2.2 collective-permute-start.24
  199.6 8.4 %attend_backward.3 = (bf16[512,768]{1,0:T(8,128)(2,1)}, bf16[512,768]{1,0:T(8,128)(2,1)}, f32[768,512]{1,0:T(8,128)}, bf16[512,768]{1,0:T(8,128)(2,1)}) custom-call(s32[2048]{0:T(1024)} %bitcast.113, s32[7]{0:T(128)} %concatenate.59.where, bf16[512,768]{1,0:T(8,128)(2,1)} %get-tuple-element.78.refs_0_, bf16[512,768]{1,0:T(8,128)(2,1)} %get-tuple-element.82.refs_1_, ...), custom_call_target="tpu_custom_call" | custom-call | flops 1000 | bytes 1000 | tf_op jit(solution)/shard_map/attend_backward/pallas_call | solution.py:459
  208.3 13.1 %ffn_grads.3 = bf16[384,6912]{1,0:T(8,128)(2,1)} custom-call(s32[1]{0:T(128)} %bitcast.1.place, bf16[3,512,768]{2,1,0:T(8,128)(2,1)} %get-tuple-element.89.left_ref, bf16[512,6912]{1,0:T(8,128)(2,1)} %get-tuple-element.81.right_ref, bf16[384,6912]{1,0:T(8,128)(2,1)} %collective-permute-done.24.refs_0_), custom_call_target="tpu_custom_call" | custom-call | flops 1000 | bytes 1000 | tf_op jit(solution)/shard_map/ffn_grads/pallas_call | solution.py:719
  221.4 1.8 slice.347
  223.2 3.6 fusion.17
  226.9 1.5 collective-permute-start.27
  230.4 21.4 %collective-permute-start.25 = (bf16[512,768]{1,0:T(8,128)(2,1)}, bf16[512,768]{1,0:T(8,128)(2,1)}, u32[]{:S(2)}, u32[]{:S(2)}) collective-permute-start(bf16[512,768]{1,0:T(8,128)(2,1)} %get-tuple-element.88), channel_id=1, source_target_pairs={{0,1},{3,2},{4,5},{7,6},{8,9},{11,10},{12,13},{15,14},{16,17},{19,... | collective-permute-start | bytes 2359304 | tf_op jit(solution)/shard_map/ppermute | solution.py:867
  251.7 15.6 %attend_backward.4 = (bf16[1024,768]{1,0:T(8,128)(2,1)}, bf16[1024,768]{1,0:T(8,128)(2,1)}, f32[768,512]{1,0:T(8,128)}, bf16[1024,768]{1,0:T(8,128)(2,1)}) custom-call(s32[2048]{0:T(1024)} %bitcast.114, s32[7]{0:T(128)} %concatenate.59.where, bf16[512,768]{1,0:T(8,128)(2,1)} %get-tuple-element.78.refs_0_, bf16[512,768]{1,0:T(8,128)(2,1)} %get-tuple-element.82.refs_1_, ...), custom_call_target="tpu_custom_call" | custom-call | flops 1000 | bytes 1000 | tf_op jit(solution)/shard_map/attend_backward/pallas_call | solution.py:459
  268.3 2.4 add_convert_fusion.1
  270.7 8.1 %collective-permute-start.28 = (bf16[512,768]{1,0:T(8,128)(2,1)}, bf16[512,768]{1,0:T(8,128)(2,1)}, u32[]{:S(2)}, u32[]{:S(2)}) collective-permute-start(bf16[512,768]{1,0:T(8,128)(2,1)} %add_convert_fusion.1), channel_id=1, source_target_pairs={{0,1},{3,2},{4,5},{7,6},{8,9},{11,10},{12,13},{15,14},{16,17},{19,... | collective-permute-start | bytes 2359304 | tf_op jit(solution)/shard_map/ppermute | solution.py:881
  278.9 1.6 collective-permute-start.29
  281.5 1.7 fusion.1
  283.2 1.7 fusion
  285.8 9.9 %collective-permute-start.33 = (bf16[96,3840]{1,0:T(8,128)(2,1)}, bf16[96,3840]{1,0:T(8,128)(2,1)S(1)}, u32[]{:S(2)}, u32[]{:S(2)}) collective-permute-start(bf16[96,3840]{1,0:T(8,128)(2,1)} %slice_bitcast_fusion.3), channel_id=1, source_target_pairs={{0,8},{4,12},{8,0},{12,4},{16,24},{20,28},{24,16},{28,20},{1,9},{5... | collective-permute-start | bytes 2211848 | tf_op jit(solution)/shard_map/ppermute | solution.py:116
  306.5 20.3 %attend_backward.5 = (bf16[512,768]{1,0:T(8,128)(2,1)}, bf16[512,768]{1,0:T(8,128)(2,1)}, bf16[512,768]{1,0:T(8,128)(2,1)}, f32[512,768]{1,0:T(8,128)}) custom-call(s32[2048]{0:T(1024)} %bitcast.115, s32[7]{0:T(128)} %concatenate.59.where, bf16[512,768]{1,0:T(8,128)(2,1)} %get-tuple-element.78.refs_0_, bf16[512,768]{1,0:T(8,128)(2,1)} %get-tuple-element.82.refs_1_, ...), custom_call_target="tpu_custom_call" | custom-call | flops 1000 | bytes 1000 | tf_op jit(solution)/shard_map/attend_backward/pallas_call | solution.py:459
  326.8 3.5 fusion.2
  330.3 2.2 collective-permute-start.30
  335.7 12.0 %attn_grads.1 = (bf16[4,304,768]{2,1,0:T(8,128)(2,1)}, f32[4,304,768]{2,1,0:T(8,128)}) custom-call(s32[1]{0:T(128)} %bitcast.21.core_ref, bf16[512,768]{1,0:T(8,128)(2,1)} %refs_0_.3, bf16[512,768]{1,0:T(8,128)(2,1)} %copy-done.3, bf16[512,768]{1,0:T(8,128)(2,1)} %broadcast_select_fusion.2.refs_1_.refs_2_, bf16[512,768]{1,0:T(8,128)(2,1)} %broadcast_select_fusion.refs_3_, ...), custom_call_target="tpu_custom_call" | custom-call | flops 1000 | bytes 1000 | tf_op jit(solution)/shard_map/attn_grads/pallas_call | solution.py:537
  349.1 5.0 %collective-permute-done.31 = bf16[512,768]{1,0:T(8,128)(2,1)} collective-permute-done((bf16[512,768]{1,0:T(8,128)(2,1)}, bf16[512,768]{1,0:T(8,128)(2,1)}, u32[]{:S(2)}, u32[]{:S(2)}) %collective-permute-start.31) | collective-permute-done | bytes 786464 | tf_op jit(solution)/shard_map/ppermute | solution.py:890
  355.0 4.4 %collective-permute-start.35 = (bf16[96,1728]{1,0:T(8,128)(2,1)S(1)}, bf16[96,1728]{1,0:T(8,128)(2,1)S(1)}, u32[]{:S(2)}, u32[]{:S(2)}) collective-permute-start(bf16[96,1728]{1,0:T(8,128)(2,1)S(1)} %get-tuple-element.173), channel_id=1, source_target_pairs={{0,1},{1,2},{2,3},{3,0},{4,5},{5,6},{6,7},{7,4},{8,9},{9,10},{10,1... | collective-permute-start | bytes 995336 | tf_op jit(solution)/shard_map/ppermute | solution.py:75
  359.4 8.9 %collective-permute-done.35 = bf16[96,1728]{1,0:T(8,128)(2,1)S(1)} collective-permute-done((bf16[96,1728]{1,0:T(8,128)(2,1)S(1)}, bf16[96,1728]{1,0:T(8,128)(2,1)S(1)}, u32[]{:S(2)}, u32[]{:S(2)}) %collective-permute-start.35) | collective-permute-done | bytes 331808 | tf_op jit(solution)/shard_map/ppermute | solution.py:75
  369.0 3.7 add_convert_fusion
  372.7 3.7 all-to-all-start
  376.5 2.5 collective-permute-start.36
  379.6 3.2 convert_add_fusion.3
  382.8 4.7 %collective-permute-done.36 = bf16[96,1728]{1,0:T(8,128)(2,1)S(1)} collective-permute-done((bf16[96,1728]{1,0:T(8,128)(2,1)S(1)}, bf16[96,1728]{1,0:T(8,128)(2,1)S(1)}, u32[]{:S(2)}, u32[]{:S(2)}) %collective-permute-start.36) | collective-permute-done | bytes 331808 | tf_op jit(solution)/shard_map/ppermute | solution.py:75
  387.5 14.5 %collective-permute-done.37 = bf16[96,1728]{1,0:T(8,128)(2,1)S(1)} collective-permute-done((bf16[96,1728]{1,0:T(8,128)(2,1)S(1)}, bf16[96,1728]{1,0:T(8,128)(2,1)S(1)}, u32[]{:S(2)}, u32[]{:S(2)}) %collective-permute-start.37) | collective-permute-done | bytes 331808 | tf_op jit(solution)/shard_map/ppermute | solution.py:75
  406.7 3.2 collective-permute-start.39
  411.0 4.2 collective-permute-done.38
  416.4 8.7 %collective-permute-done.40 = bf16[336,192]{1,0:T(8,128)(2,1)S(1)} collective-permute-done((bf16[336,192]{1,0:T(8,128)(2,1)S(1)}, bf16[336,192]{1,0:T(8,128)(2,1)S(1)}, u32[]{:S(2)}, u32[]{:S(2)}) %collective-permute-start.40) | collective-permute-done | bytes 129056 | tf_op jit(solution)/shard_map/ppermute | solution.py:75
  (213 shorter events, 59.4 us)
Async XLA Ops:
  3.6 15.1 %collective-permute-start = (bf16[3,96,768]{2,1,0:T(8,128)(2,1)S(1)}, bf16[3,96,768]{2,1,0:T(8,128)(2,1)S(1)}, u32[]{:S(2)}, u32[]{:S(2)}) collective-permute-start(bf16[3,96,768]{2,1,0:T(8,128)(2,1)S(1)} %pad_maximum_fusion.2), channel_id=1, source_target_pairs={{1,0},{2,1},{3,2},{5,4},{6,5},{7,6},{9,8},{10,9},{11,10},{13,12},{... | collective-permute-start | bytes 1327112 | tf_op jit(solution)/shard_map/ppermute | solution.py:37
  4.9 15.1 %collective-permute-start.1 = (bf16[3,96,768]{2,1,0:T(8,128)(2,1)S(1)}, bf16[3,96,768]{2,1,0:T(8,128)(2,1)S(1)}, u32[]{:S(2)}, u32[]{:S(2)}) collective-permute-start(bf16[3,96,768]{2,1,0:T(8,128)(2,1)S(1)} %pad_maximum_fusion.2), channel_id=1, source_target_pairs={{0,1},{1,2},{2,3},{4,5},{5,6},{6,7},{8,9},{9,10},{10,11},{12,13},{... | collective-permute-start | bytes 1327112 | tf_op jit(solution)/shard_map/ppermute | solution.py:36
  18.7 13.2 %collective-permute-start.2 = (bf16[3,96,768]{2,1,0:T(8,128)(2,1)S(1)}, bf16[3,96,768]{2,1,0:T(8,128)(2,1)S(1)}, u32[]{:S(2)}, u32[]{:S(2)}) collective-permute-start(bf16[3,96,768]{2,1,0:T(8,128)(2,1)S(1)} %collective-permute-done), channel_id=1, source_target_pairs={{2,1},{1,0},{6,5},{5,4},{10,9},{9,8},{14,13},{13,12},{18,17},{17,1... | collective-permute-start | bytes 1327112 | tf_op jit(solution)/shard_map/ppermute | solution.py:43
  20.0 11.9 %collective-permute-start.3 = (bf16[3,96,768]{2,1,0:T(8,128)(2,1)S(1)}, bf16[3,96,768]{2,1,0:T(8,128)(2,1)S(1)}, u32[]{:S(2)}, u32[]{:S(2)}) collective-permute-start(bf16[3,96,768]{2,1,0:T(8,128)(2,1)S(1)} %collective-permute-done.1), channel_id=1, source_target_pairs={{1,2},{2,3},{5,6},{6,7},{9,10},{10,11},{13,14},{14,15},{17,18},{18... | collective-permute-start | bytes 1327112 | tf_op jit(solution)/shard_map/ppermute | solution.py:42
  32.0 14.4 %collective-permute-start.4 = (bf16[3,96,768]{2,1,0:T(8,128)(2,1)S(1)}, bf16[3,96,768]{2,1,0:T(8,128)(2,1)S(1)}, u32[]{:S(2)}, u32[]{:S(2)}) collective-permute-start(bf16[3,96,768]{2,1,0:T(8,128)(2,1)S(1)} %broadcast_select_fusion.4), channel_id=1, source_target_pairs={{1,0},{2,3},{5,4},{6,7},{9,8},{10,11},{13,12},{14,15},{17,16},{18,... | collective-permute-start | bytes 1327112 | tf_op jit(solution)/shard_map/ppermute | solution.py:49
  33.3 20.3 %collective-permute-start.8 = (bf16[512,768]{1,0:T(8,128)(2,1)S(1)}, bf16[512,768]{1,0:T(8,128)(2,1)}, u32[]{:S(2)}, u32[]{:S(2)}) collective-permute-start(bf16[512,768]{1,0:T(8,128)(2,1)S(1)} %copy-done.2), channel_id=1, source_target_pairs={{0,1},{1,2},{2,3},{4,5},{5,6},{6,7},{8,9},{9,10},{10,11},{12,13},{... | collective-permute-start | bytes 2359304 | tf_op jit(solution)/shard_map/ppermute | solution.py:36
  38.8 22.5 %collective-permute-start.7 = (bf16[512,768]{1,0:T(8,128)(2,1)S(1)}, bf16[512,768]{1,0:T(8,128)(2,1)}, u32[]{:S(2)}, u32[]{:S(2)}) collective-permute-start(bf16[512,768]{1,0:T(8,128)(2,1)S(1)} %copy-done.2), channel_id=1, source_target_pairs={{1,0},{2,1},{3,2},{5,4},{6,5},{7,6},{9,8},{10,9},{11,10},{13,12},{... | collective-permute-start | bytes 2359304 | tf_op jit(solution)/shard_map/ppermute | solution.py:37
  49.1 16.9 %collective-permute-start.6 = (bf16[96,4608]{1,0:T(8,128)(2,1)S(1)}, bf16[96,4608]{1,0:T(8,128)(2,1)S(1)}, u32[]{:S(2)}, u32[]{:S(2)}) collective-permute-start(bf16[96,4608]{1,0:T(8,128)(2,1)S(1)} %concatenate.58.refs_16_.refs_8_), channel_id=1, source_target_pairs={{0,16},{4,20},{8,24},{12,28},{16,0},{20,4},{24,8},{28,12},{1,17},{... | collective-permute-start | bytes 2654216 | tf_op jit(solution)/shard_map/ppermute | solution.py:793
  51.5 22.8 %collective-permute-start.5 = (bf16[96,4608]{1,0:T(8,128)(2,1)S(1)}, bf16[96,4608]{1,0:T(8,128)(2,1)}, u32[]{:S(2)}, u32[]{:S(2)}) collective-permute-start(bf16[96,4608]{1,0:T(8,128)(2,1)S(1)} %concatenate.57.refs_8_.refs_0_), channel_id=1, source_target_pairs={{0,8},{4,12},{8,0},{12,4},{16,24},{20,28},{24,16},{28,20},{1,9},{5... | collective-permute-start | bytes 2654216 | tf_op jit(solution)/shard_map/ppermute | solution.py:793
  53.0 34.1 %collective-permute-start.10 = (bf16[96,4608]{1,0:T(8,128)(2,1)S(1)}, bf16[96,4608]{1,0:T(8,128)(2,1)S(1)}, u32[]{:S(2)}, u32[]{:S(2)}) collective-permute-start(bf16[96,4608]{1,0:T(8,128)(2,1)S(1)} %concatenate.58.refs_16_.refs_8_), channel_id=1, source_target_pairs={{0,8},{4,12},{8,0},{12,4},{16,24},{20,28},{24,16},{28,20},{1,9},{5... | collective-permute-start | bytes 2654216 | tf_op jit(solution)/shard_map/ppermute | solution.py:810
  53.6 34.7 %collective-permute-start.14 = (bf16[96,4608]{1,0:T(8,128)(2,1)S(1)}, bf16[96,4608]{1,0:T(8,128)(2,1)S(1)}, u32[]{:S(2)}, u32[]{:S(2)}) collective-permute-start(bf16[96,4608]{1,0:T(8,128)(2,1)S(1)} %concatenate.58.refs_16_.refs_8_), channel_id=1, source_target_pairs={{0,4},{4,0},{8,12},{12,8},{16,20},{20,16},{24,28},{28,24},{1,5},{5... | collective-permute-start | bytes 2654216 | tf_op jit(solution)/shard_map/ppermute | solution.py:804
  61.3 27.0 %collective-permute-start.13 = (bf16[96,4608]{1,0:T(8,128)(2,1)S(1)}, bf16[96,4608]{1,0:T(8,128)(2,1)S(1)}, u32[]{:S(2)}, u32[]{:S(2)}) collective-permute-start(bf16[96,4608]{1,0:T(8,128)(2,1)S(1)} %concatenate.57.refs_8_.refs_0_), channel_id=1, source_target_pairs={{0,4},{4,0},{8,12},{12,8},{16,20},{20,16},{24,28},{28,24},{1,5},{5... | collective-permute-start | bytes 2654216 | tf_op jit(solution)/shard_map/ppermute | solution.py:804
  63.4 60.8 %copy-start.29 = (f32[768]{0:T(1024)S(1)}, f32[768]{0:T(1024)}, u32[]{:S(2)}) copy-start(f32[768]{0:T(1024)} %param.28) | copy-start | bytes 9220
  63.4 60.8 %copy-start.30 = (f32[768]{0:T(1024)S(1)}, f32[768]{0:T(1024)}, u32[]{:S(2)}) copy-start(f32[768]{0:T(1024)} %param.32) | copy-start | bytes 9220
  63.5 60.9 %copy-start.31 = (f32[768]{0:T(1024)S(1)}, f32[768]{0:T(1024)}, u32[]{:S(2)}) copy-start(f32[768]{0:T(1024)} %param.33) | copy-start | bytes 9220
  63.5 60.9 %copy-start.32 = (f32[768]{0:T(1024)S(1)}, f32[768]{0:T(1024)}, u32[]{:S(2)}) copy-start(f32[768]{0:T(1024)} %param.34) | copy-start | bytes 9220
  63.5 62.1 %copy-start.26 = (s32[1,2048]{1,0:T(1,128)S(1)}, s32[1,2048]{1,0:T(1,128)}, u32[]{:S(2)}) copy-start(s32[1,2048]{1,0:T(1,128)} %param.19) | copy-start | bytes 24580
  66.1 63.5 %copy-start.5 = (bf16[96,4608]{1,0:T(8,128)(2,1)}, bf16[96,4608]{1,0:T(8,128)(2,1)S(1)}, u32[]{:S(2)}) copy-start(bf16[96,4608]{1,0:T(8,128)(2,1)S(1)} %collective-permute-done.6.refs_18_.refs_10_) | copy-start | bytes 2654212
  74.2 14.6 %collective-permute-start.11 = (bf16[512,768]{1,0:T(8,128)(2,1)}, bf16[512,768]{1,0:T(8,128)(2,1)S(1)}, u32[]{:S(2)}, u32[]{:S(2)}) collective-permute-start(bf16[512,768]{1,0:T(8,128)(2,1)} %collective-permute-done.7), channel_id=1, source_target_pairs={{2,1},{1,0},{6,5},{5,4},{10,9},{9,8},{14,13},{13,12},{18,17},{17,1... | collective-permute-start | bytes 2359304 | tf_op jit(solution)/shard_map/ppermute | solution.py:43
  75.5 14.2 %collective-permute-start.12 = (bf16[512,768]{1,0:T(8,128)(2,1)}, bf16[512,768]{1,0:T(8,128)(2,1)S(1)}, u32[]{:S(2)}, u32[]{:S(2)}) collective-permute-start(bf16[512,768]{1,0:T(8,128)(2,1)} %collective-permute-done.8), channel_id=1, source_target_pairs={{1,2},{2,3},{5,6},{6,7},{9,10},{10,11},{13,14},{14,15},{17,18},{18... | collective-permute-start | bytes 2359304 | tf_op jit(solution)/shard_map/ppermute | solution.py:42
  87.1 22.7 %collective-permute-start.9 = (bf16[96,4608]{1,0:T(8,128)(2,1)S(1)}, bf16[96,4608]{1,0:T(8,128)(2,1)}, u32[]{:S(2)}, u32[]{:S(2)}) collective-permute-start(bf16[96,4608]{1,0:T(8,128)(2,1)S(1)} %concatenate.57.refs_8_.refs_0_), channel_id=1, source_target_pairs={{0,16},{4,20},{8,24},{12,28},{16,0},{20,4},{24,8},{28,12},{1,17},{... | collective-permute-start | bytes 2654216 | tf_op jit(solution)/shard_map/ppermute | solution.py:810
  88.3 23.4 %collective-permute-start.16 = (bf16[96,4608]{1,0:T(8,128)(2,1)}, bf16[96,4608]{1,0:T(8,128)(2,1)}, u32[]{:S(2)}, u32[]{:S(2)}) collective-permute-start(bf16[96,4608]{1,0:T(8,128)(2,1)} %collective-permute-done.5.refs_9_.refs_1_), channel_id=1, source_target_pairs={{0,4},{4,0},{8,12},{12,8},{16,20},{20,16},{24,28},{28,24},{1,5},{5... | collective-permute-start | bytes 2654216 | tf_op jit(solution)/shard_map/ppermute | solution.py:804
  88.3 23.4 %collective-permute-start.21 = (bf16[96,4608]{1,0:T(8,128)(2,1)S(1)}, bf16[96,4608]{1,0:T(8,128)(2,1)}, u32[]{:S(2)}, u32[]{:S(2)}) collective-permute-start(bf16[96,4608]{1,0:T(8,128)(2,1)S(1)} %collective-permute-done.6.refs_18_.refs_10_), channel_id=1, source_target_pairs={{0,4},{4,0},{8,12},{12,8},{16,20},{20,16},{24,28},{28,24},{1,5},{5... | collective-permute-start | bytes 2654216 | tf_op jit(solution)/shard_map/ppermute | solution.py:804
  88.8 33.1 %collective-permute-start.15 = (bf16[96,4608]{1,0:T(8,128)(2,1)}, bf16[96,4608]{1,0:T(8,128)(2,1)}, u32[]{:S(2)}, u32[]{:S(2)}) collective-permute-start(bf16[96,4608]{1,0:T(8,128)(2,1)} %collective-permute-done.5.refs_9_.refs_1_), channel_id=1, source_target_pairs={{0,16},{4,20},{8,24},{12,28},{16,0},{20,4},{24,8},{28,12},{1,17},{... | collective-permute-start | bytes 2654216 | tf_op jit(solution)/shard_map/ppermute | solution.py:817
  90.6 31.2 %collective-permute-start.19 = (bf16[96,4608]{1,0:T(8,128)(2,1)S(1)}, bf16[96,4608]{1,0:T(8,128)(2,1)}, u32[]{:S(2)}, u32[]{:S(2)}) collective-permute-start(bf16[96,4608]{1,0:T(8,128)(2,1)S(1)} %collective-permute-done.6.refs_18_.refs_10_), channel_id=1, source_target_pairs={{0,8},{4,12},{8,0},{12,4},{16,24},{20,28},{24,16},{28,20},{1,9},{5... | collective-permute-start | bytes 2654216 | tf_op jit(solution)/shard_map/ppermute | solution.py:817
  109.8 17.7 %collective-permute-start.23 = (bf16[512,768]{1,0:T(8,128)(2,1)S(1)}, bf16[512,768]{1,0:T(8,128)(2,1)}, u32[]{:S(2)}, u32[]{:S(2)}) collective-permute-start(bf16[512,768]{1,0:T(8,128)(2,1)S(1)} %broadcast_select_fusion.1.refs_2_.refs_1_), channel_id=1, source_target_pairs={{1,0},{2,3},{5,4},{6,7},{9,8},{10,11},{13,12},{14,15},{17,16},{18,... | collective-permute-start | bytes 2359304 | tf_op jit(solution)/shard_map/ppermute | solution.py:49
  111.7 17.9 %collective-permute-start.17 = (bf16[96,4608]{1,0:T(8,128)(2,1)}, bf16[96,4608]{1,0:T(8,128)(2,1)S(1)}, u32[]{:S(2)}, u32[]{:S(2)}) collective-permute-start(bf16[96,4608]{1,0:T(8,128)(2,1)} %collective-permute-done.9.refs_10_.refs_2_), channel_id=1, source_target_pairs={{0,4},{4,0},{8,12},{12,8},{16,20},{20,16},{24,28},{28,24},{1,5},{5... | collective-permute-start | bytes 2654216 | tf_op jit(solution)/shard_map/ppermute | solution.py:804
  111.8 17.8 %collective-permute-start.20 = (bf16[96,4608]{1,0:T(8,128)(2,1)S(1)}, bf16[96,4608]{1,0:T(8,128)(2,1)}, u32[]{:S(2)}, u32[]{:S(2)}) collective-permute-start(bf16[96,4608]{1,0:T(8,128)(2,1)S(1)} %copy-done.7), channel_id=1, source_target_pairs={{0,4},{4,0},{8,12},{12,8},{16,20},{20,16},{24,28},{28,24},{1,5},{5... | collective-permute-start | bytes 2654216 | tf_op jit(solution)/shard_map/ppermute | solution.py:804
  121.9 7.7 %collective-permute-start.18 = (bf16[96,4608]{1,0:T(8,128)(2,1)}, bf16[96,4608]{1,0:T(8,128)(2,1)}, u32[]{:S(2)}, u32[]{:S(2)}) collective-permute-start(bf16[96,4608]{1,0:T(8,128)(2,1)} %collective-permute-done.15.refs_11_.refs_3_), channel_id=1, source_target_pairs={{0,4},{4,0},{8,12},{12,8},{16,20},{20,16},{24,28},{28,24},{1,5},{5... | collective-permute-start | bytes 2654216 | tf_op jit(solution)/shard_map/ppermute | solution.py:804
  121.9 7.7 %collective-permute-start.22 = (bf16[96,4608]{1,0:T(8,128)(2,1)}, bf16[96,4608]{1,0:T(8,128)(2,1)}, u32[]{:S(2)}, u32[]{:S(2)}) collective-permute-start(bf16[96,4608]{1,0:T(8,128)(2,1)} %collective-permute-done.19.refs_19_.refs_11_), channel_id=1, source_target_pairs={{0,4},{4,0},{8,12},{12,8},{16,20},{20,16},{24,28},{28,24},{1,5},{5... | collective-permute-start | bytes 2654216 | tf_op jit(solution)/shard_map/ppermute | solution.py:804
  197.4 10.9 %collective-permute-start.24 = (bf16[384,6912]{1,0:T(8,128)(2,1)}, bf16[384,6912]{1,0:T(8,128)(2,1)}, u32[]{:S(2)}, u32[]{:S(2)}) collective-permute-start(bf16[384,6912]{1,0:T(8,128)(2,1)} %ffn_grads.2), channel_id=1, source_target_pairs={{0,4},{4,0},{8,12},{12,8},{16,20},{20,16},{24,28},{28,24},{1,5},{5... | collective-permute-start | bytes 15925256 | tf_op jit(solution)/shard_map/ppermute | solution.py:862
  226.9 54.6 %collective-permute-start.27 = (bf16[2,96,3840]{2,1,0:T(8,128)(2,1)}, bf16[2,96,3840]{2,1,0:T(8,128)(2,1)}, u32[]{:S(2)}, u32[]{:S(2)}) collective-permute-start(bf16[2,96,3840]{2,1,0:T(8,128)(2,1)} %bitcast.33), channel_id=1, source_target_pairs={{0,16},{4,20},{8,24},{12,28},{16,0},{20,4},{24,8},{28,12},{1,17},{... | collective-permute-start | bytes 4423688 | tf_op jit(solution)/shard_map/ppermute | solution.py:116
  229.4 51.0 %collective-permute-start.26 = (bf16[2,96,3072]{2,1,0:T(8,128)(2,1)}, bf16[2,96,3072]{2,1,0:T(8,128)(2,1)S(1)}, u32[]{:S(2)}, u32[]{:S(2)}) collective-permute-start(bf16[2,96,3072]{2,1,0:T(8,128)(2,1)} %slice_bitcast_fusion), channel_id=1, source_target_pairs={{0,8},{4,12},{8,0},{12,4},{16,24},{20,28},{24,16},{28,20},{1,9},{5... | collective-permute-start | bytes 3538952 | tf_op jit(solution)/shard_map/ppermute | solution.py:116
  230.4 37.9 %collective-permute-start.25 = (bf16[512,768]{1,0:T(8,128)(2,1)}, bf16[512,768]{1,0:T(8,128)(2,1)}, u32[]{:S(2)}, u32[]{:S(2)}) collective-permute-start(bf16[512,768]{1,0:T(8,128)(2,1)} %get-tuple-element.88), channel_id=1, source_target_pairs={{0,1},{3,2},{4,5},{7,6},{8,9},{11,10},{12,13},{15,14},{16,17},{19,... | collective-permute-start | bytes 2359304 | tf_op jit(solution)/shard_map/ppermute | solution.py:867
  270.7 56.0 %collective-permute-start.28 = (bf16[512,768]{1,0:T(8,128)(2,1)}, bf16[512,768]{1,0:T(8,128)(2,1)}, u32[]{:S(2)}, u32[]{:S(2)}) collective-permute-start(bf16[512,768]{1,0:T(8,128)(2,1)} %add_convert_fusion.1), channel_id=1, source_target_pairs={{0,1},{3,2},{4,5},{7,6},{8,9},{11,10},{12,13},{15,14},{16,17},{19,... | collective-permute-start | bytes 2359304 | tf_op jit(solution)/shard_map/ppermute | solution.py:881
  278.9 47.9 %collective-permute-start.29 = (bf16[512,768]{1,0:T(8,128)(2,1)}, bf16[512,768]{1,0:T(8,128)(2,1)}, u32[]{:S(2)}, u32[]{:S(2)}) collective-permute-start(bf16[512,768]{1,0:T(8,128)(2,1)} %add_convert_fusion.1), channel_id=1, source_target_pairs={{1,2},{2,1},{5,6},{6,5},{9,10},{10,9},{13,14},{14,13},{17,18},{18,... | collective-permute-start | bytes 2359304 | tf_op jit(solution)/shard_map/ppermute | solution.py:882
  285.8 47.9 %collective-permute-start.33 = (bf16[96,3840]{1,0:T(8,128)(2,1)}, bf16[96,3840]{1,0:T(8,128)(2,1)S(1)}, u32[]{:S(2)}, u32[]{:S(2)}) collective-permute-start(bf16[96,3840]{1,0:T(8,128)(2,1)} %slice_bitcast_fusion.3), channel_id=1, source_target_pairs={{0,8},{4,12},{8,0},{12,4},{16,24},{20,28},{24,16},{28,20},{1,9},{5... | collective-permute-start | bytes 2211848 | tf_op jit(solution)/shard_map/ppermute | solution.py:116
  296.6 37.1 %collective-permute-start.32 = (bf16[96,3072]{1,0:T(8,128)(2,1)}, bf16[96,3072]{1,0:T(8,128)(2,1)}, u32[]{:S(2)}, u32[]{:S(2)}) collective-permute-start(bf16[96,3072]{1,0:T(8,128)(2,1)} %slice_bitcast_fusion.4), channel_id=1, source_target_pairs={{0,16},{4,20},{8,24},{12,28},{16,0},{20,4},{24,8},{28,12},{1,17},{... | collective-permute-start | bytes 1769480 | tf_op jit(solution)/shard_map/ppermute | solution.py:116
  330.3 18.8 %collective-permute-start.30 = (bf16[512,768]{1,0:T(8,128)(2,1)}, bf16[512,768]{1,0:T(8,128)(2,1)}, u32[]{:S(2)}, u32[]{:S(2)}) collective-permute-start(bf16[512,768]{1,0:T(8,128)(2,1)} %get-tuple-element.169), channel_id=1, source_target_pairs={{0,1},{1,2},{2,3},{4,5},{5,6},{6,7},{8,9},{9,10},{10,11},{12,13},{... | collective-permute-start | bytes 2359304 | tf_op jit(solution)/shard_map/ppermute | solution.py:889
  332.5 21.6 %collective-permute-start.31 = (bf16[512,768]{1,0:T(8,128)(2,1)}, bf16[512,768]{1,0:T(8,128)(2,1)}, u32[]{:S(2)}, u32[]{:S(2)}) collective-permute-start(bf16[512,768]{1,0:T(8,128)(2,1)} %get-tuple-element.170), channel_id=1, source_target_pairs={{1,0},{2,1},{3,2},{5,4},{6,5},{7,6},{9,8},{10,9},{11,10},{13,12},{... | collective-permute-start | bytes 2359304 | tf_op jit(solution)/shard_map/ppermute | solution.py:890
  354.1 14.2 %collective-permute-start.34 = (bf16[4,304,768]{2,1,0:T(8,128)(2,1)}, bf16[4,304,768]{2,1,0:T(8,128)(2,1)S(1)}, u32[]{:S(2)}, u32[]{:S(2)}) collective-permute-start(bf16[4,304,768]{2,1,0:T(8,128)(2,1)} %get-tuple-element.114), channel_id=1, source_target_pairs={{0,4},{4,0},{8,12},{12,8},{16,20},{20,16},{24,28},{28,24},{1,5},{5... | collective-permute-start | bytes 5603336 | tf_op jit(solution)/shard_map/ppermute | solution.py:932
  355.0 13.3 %collective-permute-start.35 = (bf16[96,1728]{1,0:T(8,128)(2,1)S(1)}, bf16[96,1728]{1,0:T(8,128)(2,1)S(1)}, u32[]{:S(2)}, u32[]{:S(2)}) collective-permute-start(bf16[96,1728]{1,0:T(8,128)(2,1)S(1)} %get-tuple-element.173), channel_id=1, source_target_pairs={{0,1},{1,2},{2,3},{3,0},{4,5},{5,6},{6,7},{7,4},{8,9},{9,10},{10,1... | collective-permute-start | bytes 995336 | tf_op jit(solution)/shard_map/ppermute | solution.py:75
  372.7 30.2 %all-to-all-start = ((bf16[4,304,768]{2,1,0:T(8,128)(2,1)}), bf16[4,304,768]{2,1,0:T(8,128)(2,1)S(1)}, u32[]{:S(2)}, u32[]{:S(2)}) async-start(bf16[4,304,768]{2,1,0:T(8,128)(2,1)} %add_convert_fusion), calls=%async_computation | async-start | bytes 3735552 | tf_op jit(solution)/shard_map/all_to_all | solution.py:935
  376.5 11.0 %collective-permute-start.36 = (bf16[96,1728]{1,0:T(8,128)(2,1)S(1)}, bf16[96,1728]{1,0:T(8,128)(2,1)S(1)}, u32[]{:S(2)}, u32[]{:S(2)}) collective-permute-start(bf16[96,1728]{1,0:T(8,128)(2,1)S(1)} %copy-done.21), channel_id=1, source_target_pairs={{0,3},{1,0},{2,1},{3,2},{4,7},{5,4},{6,5},{7,6},{8,11},{9,8},{10,9... | collective-permute-start | bytes 995336 | tf_op jit(solution)/shard_map/ppermute | solution.py:75
  379.0 23.0 %collective-permute-start.37 = (bf16[96,1728]{1,0:T(8,128)(2,1)S(1)}, bf16[96,1728]{1,0:T(8,128)(2,1)S(1)}, u32[]{:S(2)}, u32[]{:S(2)}) collective-permute-start(bf16[96,1728]{1,0:T(8,128)(2,1)S(1)} %copy-done.20), channel_id=1, source_target_pairs={{0,2},{1,3},{2,0},{3,1},{4,6},{5,7},{6,4},{7,5},{8,10},{9,11},{10,... | collective-permute-start | bytes 995336 | tf_op jit(solution)/shard_map/ppermute | solution.py:75
  406.1 9.2 %collective-permute-start.38 = (bf16[336,192]{1,0:T(8,128)(2,1)S(1)}, bf16[336,192]{1,0:T(8,128)(2,1)S(1)}, u32[]{:S(2)}, u32[]{:S(2)}) collective-permute-start(bf16[336,192]{1,0:T(8,128)(2,1)S(1)} %get-tuple-element.184), channel_id=1, source_target_pairs={{0,1},{1,2},{2,3},{3,0},{4,5},{5,6},{6,7},{7,4},{8,9},{9,10},{10,1... | collective-permute-start | bytes 387080 | tf_op jit(solution)/shard_map/ppermute | solution.py:75
  406.7 9.7 %collective-permute-start.39 = (bf16[336,192]{1,0:T(8,128)(2,1)S(1)}, bf16[336,192]{1,0:T(8,128)(2,1)S(1)}, u32[]{:S(2)}, u32[]{:S(2)}) collective-permute-start(bf16[336,192]{1,0:T(8,128)(2,1)S(1)} %get-tuple-element.186), channel_id=1, source_target_pairs={{0,3},{1,0},{2,1},{3,2},{4,7},{5,4},{6,5},{7,6},{8,11},{9,8},{10,9... | collective-permute-start | bytes 387080 | tf_op jit(solution)/shard_map/ppermute | solution.py:75
  409.9 15.2 %collective-permute-start.40 = (bf16[336,192]{1,0:T(8,128)(2,1)S(1)}, bf16[336,192]{1,0:T(8,128)(2,1)S(1)}, u32[]{:S(2)}, u32[]{:S(2)}) collective-permute-start(bf16[336,192]{1,0:T(8,128)(2,1)S(1)} %get-tuple-element.185), channel_id=1, source_target_pairs={{0,2},{1,3},{2,0},{3,1},{4,6},{5,7},{6,4},{7,5},{8,10},{9,11},{10,... | collective-permute-start | bytes 387080 | tf_op jit(solution)/shard_map/ppermute | solution.py:75
  (29 other events, 518.8 us)
where the time goes:
time: 433 us; the launch traced here: 432 us
  Pallas kernels  136 us (31%)
  waiting for transfers between devices  130 us (30%)
  starting transfers between devices  93 us (21%)
  local copies, waits for them, and re-layouts  34.2 us (8%)
  other arithmetic  29.3 us (7%)
  between operations  9.6 us (2%)
    pallas_call x3, Pallas kernels, attend_backward(): pl.pallas_call(partial(backward_kernel, slots=slots, first=first, last=la...  44.3 us
    ppermute x6, waiting for transfers between devices, spread(): lax.ppermute(block, 'tensor', [(i, (i + shift) % 4) for i in range(4)])  42.3 us
    pallas_call x1, Pallas kernels, middle(): pl.pallas_call(partial(middle_kernel, count=count), out_shape=tuple((jax....  29.1 us
    ppermute x2, waiting for transfers between devices, on_device(): lax.ppermute(own[i], 'fsdp', partner(orders[i][1]))  27.1 us
    pallas_call x1, Pallas kernels, attend_forward(): pl.pallas_call(partial(forward_kernel, slots=slots, count=count), out_sha...  26.2 us
    pallas_call x2, Pallas kernels, ffn_grads(): pl.pallas_call(partial(ffn_grad_kernel, core=core), out_shape=jax.ShapeDt...  24.6 us
    ppermute x1, starting transfers between devices, on_device(): r1 = lax.ppermute(dx_b, 'tensor', [(0, 1), (3, 2)])  21.4 us
    ppermute x2, waiting for transfers between devices, line_first(): above = lax.ppermute(own, 'tensor', [(1, 0), (2, 1), (3, 2)])  15.9 us
  transfers between devices with their start and end apart: 42, of which 19 were waited for; matrix products, arithmetic and copies ran while one was open for 9% of the time, Pallas kernels for 13%

commit v1 on v0

--- a/solution.py
+++ b/solution.py
@@ -15,6 +15,7 @@
 LOG2E = 1.4426950408889634
 SCORE = HD**-0.5 * LOG2E
 EXTRA = 16
+SHIFTS = (1, 3, 2)
 FEW = 1000
 BF = jnp.bfloat16
 F32 = jnp.float32
@@ -57,20 +58,16 @@
 
 def owner_slot(t):
     owner = slot_owner(t)
-    places = jnp.arange(4)
-    return [jnp.sum(jnp.where(owner == j, places, 0)) for j in range(4)]
-
-
-def in_line_order(slots, t):
-    return jnp.concatenate([lax.dynamic_slice_in_dim(slots, s, 1, axis=0) for s in owner_slot(t)])
-
-
-def spread(slots, t):
-    owner = slot_owner(t)
+    return [sum(jnp.where(owner[k] == j, k, 0) for k in range(4)) for j in range(4)]
+
+
+def in_line_order(slots, slot_of):
+    return jnp.concatenate([lax.dynamic_slice_in_dim(slots, s, 1, axis=0) for s in slot_of])
+
+
+def spread(slots, goals):
     arrived = []
-    for shift in (1, 3, 2):
-        goal = lax.rem(t + shift, 4)
-        slot = sum(jnp.where(owner[j] == goal, j, 0) for j in range(4))
+    for shift, slot in zip(SHIFTS, goals):
         block = lax.dynamic_index_in_dim(slots, slot, 0, keepdims=False)
         arrived.append(lax.ppermute(block, "tensor", [(i, (i + shift) % 4) for i in range(4)]))
     return arrived
@@ -109,13 +106,14 @@
 
 
 def start_halving(blocks, lefts, pair):
-    kept, arrived, rest = [], [], []
+    kept, arrived, rest, sent = [], [], [], []
     for block, left, bit in zip(blocks, lefts, pair):
         axis = left.index(bit)
         kept.append(lax.index_in_dim(block, 0, axis, keepdims=False))
-        arrived.append(lax.ppermute(lax.index_in_dim(block, 1, axis, keepdims=False), "fsdp", partner(bit)))
+        sent.append(lax.index_in_dim(block, 1, axis, keepdims=False))
+        arrived.append(lax.ppermute(sent[-1], "fsdp", partner(bit)))
         rest.append([b for b in left if b != bit])
-    return kept, arrived, rest
+    return (kept, arrived, rest), sent
 
 
 def add_low(kept, arrived):
@@ -578,8 +576,8 @@
 def middle_kernel(known, *refs, count):
     w_refs, refs = (refs[:count], refs[count : 2 * count]), refs[2 * count :]
     ctx_ref, x_ref, grad_ref, vec_ref, bias_ref = refs[:5]
-    out_ref, first_ref, gctx_ref, lefts_ref, rights_ref, sums_ref, bias_grad_ref = refs[5:12]
-    w_s, mix_ref, slope_s, n1_s, r1_s, acc_s, sems, mix_sems = refs[12:]
+    out_ref, first_ref, gctx_ref, lefts_ref, rights_ref, sums_ref = refs[5:11]
+    w_s, mix_ref, slope_s, n1_s, r1_s, acc_s, sems, mix_sems = refs[11:]
     parts, units = bias_ref.shape
     rows, width = x_ref.shape
 
@@ -616,7 +614,7 @@
                 copy(which, t, j).wait()
 
     def up(t, _):
-        pre = nn(lefts_ref[1], w_s[0, t]) + bias_ref[pl.ds(t, 1), :]
+        pre = nn(lefts_ref[1], w_s[0, t]) + bias_ref[pl.ds(known[2 + t], 1), :]
         act, slope = gelu_parts(pre)
         slope_s[t] = slope
         low = act.astype(BF)
@@ -639,7 +637,7 @@
     def back(t, _):
         g_pre = (nn(lefts_ref[0], w_s[1, t]) * slope_s[t]).astype(BF)
         rights_ref[:, cols(parts + t)] = g_pre
-        bias_grad_ref[pl.ds(t, 1), :] = down_rows(g_pre.astype(F32))
+        sums_ref[pl.ds(6 + known[2 + t], 1), :] = down_rows(g_pre.astype(F32))
         acc_s[...] += nt(g_pre, w_s[0, t])
         return 0
 
@@ -650,7 +648,6 @@
     sums_ref[0:1, :] = down_rows(g_first)
     sums_ref[1:2, :] = down_rows(g_normed * n1)
     sums_ref[2:3, :] = down_rows(g_normed)
-    sums_ref[6:8, :] = jnp.zeros((2, width), F32)
     first_ref[...] = g_first
     low = g_first.astype(BF)
     lefts_ref[2] = low
@@ -669,8 +666,7 @@
         ((rows, width), BF),
         ((3, rows, width), BF),
         ((rows, 2 * parts * units + width), BF),
-        ((8, width), F32),
-        ((parts, units), F32),
+        ((6 + parts, width), F32),
     ]
     return pl.pallas_call(
         partial(middle_kernel, count=count),
@@ -693,46 +689,47 @@
     )(known, *pieces[0], *pieces[1], ctx, x, grad, vectors, bias)
 
 
-def ffn_grad_kernel(place, left_ref, right_ref, *refs, core):
-    out_ref, left_s, chosen_s = refs[-3:]
+def ffn_grad_kernel(place, left_ref, right_ref, kept_ref, sent_ref, left_s, chosen_s, *, n):
+    half = kept_ref.shape[0]
 
     @pl.when(pl.program_id(0) % 4 == 0)
     def _():
         left_s[...] = left_ref[0].T
-        if core is not None:
-            size = left_s.shape[0] // core[1]
-            for q in range(core[1] // 2):
-                block = place[0] ^ (2 * q + core[0])
-                chosen_s[q * size : (q + 1) * size, :] = left_s[pl.ds(pl.multiple_of(block * size, size), size), :]
-
-    total = nn((left_s if core is None else chosen_s)[...], right_ref[...])
-    if len(refs) == 4:
-        total = total + refs[0][...].astype(F32)
-    out_ref[...] = total.astype(BF)
-
-
-def ffn_grads(place, lefts, rights, core=None, got=None):
+        size = left_s.shape[0] // n
+        if size % 16:
+            chosen_s[...] = left_s[...]
+        else:
+            for j in range(n):
+                core, outer = j // (n // 2), j % (n // 2)
+                block = place[0] ^ (2 * outer + core)
+                chosen_s[j * size : (j + 1) * size, :] = left_s[pl.ds(pl.multiple_of(block * size, size), size), :]
+
+    total = nn(chosen_s[...], right_ref[...])
+    kept_ref[...] = total[:half].astype(BF)
+    sent_ref[...] = total[half:].astype(BF)
+
+
+def ffn_grads(place, lefts, rights, n):
     _, rows, width = lefts.shape
     units = rights.shape[1] // 9
-    out_rows = width if core is None else width // 2
-    out_spec = pl.BlockSpec((out_rows, units), lambda i, p: (0, i))
+    out_spec = pl.BlockSpec((width // 2, units), lambda i, p: (0, i))
+    out_shape = jax.ShapeDtypeStruct((width // 2, rights.shape[1]), BF)
     return pl.pallas_call(
-        partial(ffn_grad_kernel, core=core),
-        out_shape=jax.ShapeDtypeStruct((out_rows, rights.shape[1]), BF),
+        partial(ffn_grad_kernel, n=n),
+        out_shape=(out_shape, out_shape),
         grid_spec=pltpu.PrefetchScalarGridSpec(
             num_scalar_prefetch=1,
             grid=(9,),
             in_specs=[
                 pl.BlockSpec((1, rows, width), lambda i, p: (i // 4, 0, 0)),
                 pl.BlockSpec((rows, units), lambda i, p: (0, i)),
-            ]
-            + ([] if got is None else [out_spec]),
-            out_specs=out_spec,
-            scratch_shapes=[pltpu.VMEM((width, rows), BF), pltpu.VMEM((width // 2, rows), BF)],
+            ],
+            out_specs=[out_spec, out_spec],
+            scratch_shapes=[pltpu.VMEM((width, rows), BF), pltpu.VMEM((width, rows), BF)],
         ),
         cost_estimate=pl.CostEstimate(flops=FEW, bytes_accessed=FEW, transcendentals=0),
         name="ffn_grads",
-    )(place, lefts, rights, *(() if got is None else (got,)))
+    )(place, lefts, rights)
 
 
 def on_device(
@@ -763,6 +760,23 @@
     cols = query_weight.shape[1]
     owner = slot_owner(t)
 
+    def by_slot(vector):
+        parts = vector.reshape(4, -1)
+        return jnp.concatenate([lax.dynamic_slice_in_dim(parts, owner[i], 1, axis=0)[0] for i in range(4)])
+
+    seg = jnp.where(segments == 0, 9, segments)
+    where = jnp.concatenate([t[None], owner, (f & 1)[None], f[None]]).astype(jnp.int32)
+    own_ids = lax.dynamic_slice_in_dim(seg[0], t * rows, rows)
+    known = jnp.concatenate([jnp.stack([jnp.sum((own_ids < 9).astype(jnp.int32)), f]), owner]).astype(jnp.int32)
+    vectors = jnp.stack([mix_bias, norm_gain, norm_shift, down_bias, final_gain, final_shift])
+    shifts = (by_slot(query_bias), by_slot(value_bias))
+    slot_of = owner_slot(t)
+    goals = [sum(jnp.where(owner[k] == lax.rem(t + shift, 4), k, 0) for k in range(4)) for shift in SHIFTS]
+    seg, where, known, vectors, shifts, slot_of, goals = lax.optimization_barrier(
+        (seg, where, known, vectors, shifts, slot_of, goals)
+    )
+    small_operands = (seg, where, known, vectors, *shifts, *slot_of, *goals)
+
     shard = jnp.stack(
         [
             jnp.concatenate([query_weight, key_weight, value_weight, mix_weight.T], axis=1),
@@ -771,9 +785,10 @@
         ]
     )
     w_a, w_below, w_above = line_first(shard)
-    w_c = line_second(w_below, w_above)
+    w_c = after(line_second(w_below, w_above), *small_operands)
+    w_b = line_third(w_c, w_below)
+    w_slots = (shard, w_a, w_c, w_b)
     x_a, x_below, x_above = line_first(after(tokens, w_c))
-    w_slots = (shard, w_a, w_c, line_third(w_c, w_below))
 
     def half(first, last):
         line = [w[0][:, m * cols : (m + 1) * cols] for m in (first, first + 1) for w in w_slots]
@@ -811,14 +826,14 @@
         ]
     far_own = to_partner(own)
     keep(first, x_a)
-    x_c = line_second(*after((x_below, x_above), *passed[0]))
+    x_c = line_second(*after((x_below, x_above), *far_own))
     if direct:
         forwarded = [
             (i, 3, lax.ppermute(held[i][orders[i][0] >> 1], "fsdp", partner(orders[i][1]))) for i in range(2)
         ]
         far_first = to_partner(passed[0])
         keep(direct, x_c, *far_own)
-        x_b = line_third(after(x_c, *passed[1]), x_below, *far_first)
+        x_b = line_third(x_c, x_below, *far_first)
         far_direct = to_partner(passed[1])
         keep(forwarded)
         far_last = to_partner(passed[2])
@@ -834,83 +849,59 @@
     if r % 16:
         pieces = [[assembled(p)] for p in pieces]
 
-    def by_slot(vector):
-        parts = vector.reshape(4, -1)
-        return jnp.concatenate([lax.dynamic_slice_in_dim(parts, owner[i], 1, axis=0)[0] for i in range(4)])
-
-    seg = jnp.where(segments == 0, 9, segments)
-    where = jnp.concatenate([t[None], owner, (f & 1)[None], f[None]]).astype(jnp.int32)
     xs = (tokens, x_a, x_c, x_b)
-    q, k, v, ctx, lse, w_all = attend_forward(xs, pieces, (by_slot(query_bias), by_slot(value_bias)), seg, where)
+    q, k, v, ctx, lse, w_all = attend_forward(xs, pieces, shifts, seg, where)
     weights = tuple((w_all, m) for m in range(3))
 
-    own_ids = lax.dynamic_slice_in_dim(seg[0], t * rows, rows)
-    known = jnp.stack([jnp.sum((own_ids < 9).astype(jnp.int32)), f.astype(jnp.int32)])
-    vectors = jnp.stack([mix_bias, norm_gain, norm_shift, down_bias, final_gain, final_shift])
-    layer_out, g_first, g_ctx, lefts, rights, sums, up_sums = middle(
-        known, pieces, ctx, tokens, out_grad, vectors, by_slot(up_bias).reshape(4, units)
+    layer_out, g_first, g_ctx, lefts, rights, extra = middle(
+        known, pieces, ctx, tokens, out_grad, vectors, up_bias.reshape(4, units)
     )
     place = f.astype(jnp.int32)[None]
+    kept, sent = ffn_grads(place, lefts, rights, n)
     if r % 16:
-        full = ffn_grads(place, lefts, rights).reshape(n, r, -1)
+        full = jnp.concatenate([kept, sent]).reshape(n, r, -1)
         kept, sent = (
             jnp.concatenate([lax.dynamic_slice_in_dim(full, f ^ (2 * q + c), 1)[0] for q in range(n // 2)])
             for c in range(2)
         )
-    else:
-        sent = ffn_grads(place, lefts, rights, (1, n))
     got = lax.ppermute(sent, "fsdp", partner(1))
     g_ctx = after(g_ctx, sent)
 
     args = (q, k, v, g_ctx, ctx, lse)
-    dk_b, dv_b, dq, dx_b = attend_backward(*args, (3,), weights, seg, where)
+    dk_n, dv_n, dq, dx_n = attend_backward(*args, (3, 2, 1), weights, seg, where)
+    dx_b, dx_c, dx_a = (dx_n[i * rows : (i + 1) * rows] for i in range(3))
     r1 = lax.ppermute(dx_b, "tensor", [(0, 1), (3, 2)])
-    lefts = after(lefts, dx_b)
-    if r % 16:
-        near = (kept.astype(F32) + got.astype(F32)).astype(BF)
-    else:
-        near = ffn_grads(place, lefts, rights, (0, n), got)
     steps = list(zip(outer_bits(), outer_bits()[::-1]))
-    blocks, lefts = zip(*(outer_axes(b) for b in (near[:, : 4 * units], near[:, 4 * units :])))
-    halves = start_halving(blocks, lefts, steps[0])
-    dk_n, dv_n, dq, dx_n = attend_backward(*args, (2, 1), weights, seg, where, after(dq, near))
-    dx_c, dx_a = dx_n[:rows], dx_n[rows:]
-    blocks = add_low(halves[0], after(halves[1], dx_n))
-    halves = start_halving(blocks, halves[2], steps[1])
-    middle_x = (dx_c.astype(F32) + r1.astype(F32)).astype(BF)
+    got = after(got, dx_n)
+    held = [outer_axes(kept[:, : 4 * units]), outer_axes(kept[:, 4 * units :])]
+    come = [outer_axes(got[:, : 4 * units])[0], outer_axes(got[:, 4 * units :])[0]]
+    lefts = [h[1] for h in held]
+    held = [h[0] for h in held]
+    axes = [left.index(bit) for left, bit in zip(lefts, steps[0])]
+
+    def at(blocks, index):
+        return [lax.index_in_dim(b, index, axis, keepdims=False) for b, axis in zip(blocks, axes)]
+
+    out_halves = add_low(at(held, 1), at(come, 1))
+    arrived = [lax.ppermute(o, "fsdp", partner(bit)) for o, bit in zip(out_halves, steps[0])]
+    dk_o, dv_o, dq, dx_own = attend_backward(
+        *args, (0,), weights, seg, where, after(dq, dx_b, *out_halves), g_first
+    )
+    middle_x = (dx_c.astype(F32) + after(r1, dx_own).astype(F32)).astype(BF)
     rx = lax.ppermute(middle_x, "tensor", [(0, 1), (3, 2)])
     ry = lax.ppermute(middle_x, "tensor", [(1, 2), (2, 1)])
-    dk_o, dv_o, dq, dx_own = attend_backward(
-        *args, (0,), weights, seg, where, after(dq, middle_x, *blocks), g_first
-    )
-    rx, ry = (a.astype(F32) for a in after((rx, ry), dx_own))
-    up_x = (dx_a.astype(F32) + jnp.where(t == 1, rx, ry)).astype(BF)
-    down_x = jnp.where(t == 3, dx_a.astype(F32), dx_b.astype(F32) + jnp.where(t == 1, ry, rx)).astype(BF)
-    from_below = lax.ppermute(up_x, "tensor", [(0, 1), (1, 2), (2, 3)])
-    from_above = lax.ppermute(down_x, "tensor", [(1, 0), (2, 1), (3, 2)])
-
-    d_one, d_two = add_low(halves[0], after(halves[1], dx_own))
-    for pair in steps[2:]:
-        halves = start_halving([d_one, d_two], halves[2], pair)
-        d_one, d_two = add_low(halves[0], halves[1])
-    early = jnp.stack(
-        [
-            jnp.concatenate(
-                [
-                    d_one[:, i * units : (i + 1) * units],
-                    d_two[:, i * units : (i + 1) * units],
-                    d_two[:, 4 * units + i * cols : 4 * units + (i + 1) * cols],
-                ],
-                axis=1,
-            )
-            for i in range(4)
-        ]
-    )
-
-    xs = (xs[0], xs[2], xs[1], xs[3])
-    extra = jnp.concatenate([sums[:6], in_line_order(up_sums, t)])
-    dq = after(dq, up_x, down_x, early)
-    sent, kept = attn_grads(where[5:6], xs, dq, extra, (dk_o, dk_n, dk_b), (dv_o, dv_n, dv_b), n)
+
+    arrived = after(arrived, dx_own)
+    blocks = [
+        (a.astype(F32) + b.astype(F32) + c.astype(F32)).astype(BF)
+        for a, b, c in zip(at(held, 0), at(come, 0), arrived)
+    ]
+    lefts = [[b for b in left if b != bit] for left, bit in zip(lefts, steps[0])]
+    halves, out_halves = start_halving(blocks, lefts, steps[1])
+
+    xs = (xs[0], xs[3], xs[2], xs[1])
+    dq = after(dq, middle_x, *out_halves)
+    sent, kept = attn_grads(where[5:6], xs, dq, extra, (dk_o, dk_n), (dv_o, dv_n), n)
     if r % 16:
         split = sent.reshape(3, n // 2, 2, r, width)
         sums = jnp.broadcast_to(kept, (n // 2, EXTRA, width))
@@ -927,23 +918,46 @@
             for c in (1 - (f & 1), f & 1)
         )
         sent = sent.astype(BF)
-    sent = after(sent, from_below, from_above)
-    early_own, early = early[0], spread(early, t)
     got = lax.ppermute(sent, "fsdp", partner(1))
-    near = (kept + after(got, early[0]).astype(F32)).astype(BF)
+    near = (kept + got.astype(F32)).astype(BF)
+    rx, ry = (a.astype(F32) for a in after((rx, ry), sent))
+    up_x = (dx_a.astype(F32) + jnp.where(t == 1, rx, ry)).astype(BF)
+    down_x = jnp.where(t == 3, dx_a.astype(F32), dx_b.astype(F32) + jnp.where(t == 1, ry, rx)).astype(BF)
+    from_below = lax.ppermute(up_x, "tensor", [(0, 1), (1, 2), (2, 3)])
+    from_above = lax.ppermute(down_x, "tensor", [(1, 0), (2, 1), (3, 2)])
+
+    d_one, d_two = add_low(halves[0], after(halves[1], sent))
+    for pair in steps[2:]:
+        halves, _ = start_halving([d_one, d_two], halves[2], pair)
+        d_one, d_two = add_low(halves[0], halves[1])
+    early = jnp.stack(
+        [
+            jnp.concatenate(
+                [
+                    d_one[:, i * units : (i + 1) * units],
+                    d_two[:, i * units : (i + 1) * units],
+                    d_two[:, 4 * units + i * cols : 4 * units + (i + 1) * cols],
+                ],
+                axis=1,
+            )
+            for i in range(4)
+        ]
+    )
+
+    early_own, early = early[0], spread(early, goals)
     same_core = [list(range(c, n, 2)) for c in range(2)]
     arrived = lax.all_to_all(near, "fsdp", split_axis=0, concat_axis=0, axis_index_groups=same_core, tiled=True)
     arrived = after(arrived, *early)
     late = jnp.sum(arrived.astype(F32), axis=0).astype(BF)
     count = 12
     by_head = jnp.stack([late[3 * r : 3 * r + 2, i * cols : (i + 1) * cols] for i in range(4)])
-    by_head = in_line_order(by_head, t).reshape(8, cols)
+    by_head = in_line_order(by_head, slot_of).reshape(8, cols)
     whole = [late[3 * r + 2 : 3 * r + count, i * cols : (i + 1) * cols] for i in range(4)]
     below = jnp.concatenate([by_head, *whole])
     late = jnp.stack(
         [jnp.concatenate([late[: 3 * r, i * cols : (i + 1) * cols], below]) for i in range(4)]
     )
-    late = total(late[0], spread(late, t))
+    late = total(late[0], spread(late, goals))
     early = total(early_own, early)
     tokens_grad = dx_own + from_below.astype(F32) + from_above.astype(F32)
     qv = late[3 * r : 3 * r + 8].reshape(4, 2, cols).transpose(1, 0, 2).reshape(2, width)

time: 433 us -> 402 us (0.928)
  waiting for transfers between devices: 130 us -> 116 us
  Pallas kernels: 136 us -> 126 us
  between operations: 9.6 us -> 1.91 us
  starting transfers between devices: 93 us -> 86.3 us
    ppermute x6, waiting for transfers between devices: 42.3 us -> 28.4 us  [spread(): lax.ppermute(block, 'tensor', [(i, (i + shift) % 4) for i in range(4)])]
    ppermute x2, starting transfers between devices: 2.21 us -> 14.5 us  [on_device(): got = lax.ppermute(sent, 'fsdp', partner(1))]
    ppermute x2, waiting for transfers between devices: 27.1 us -> 15.5 us  [on_device(): lax.ppermute(own[i], 'fsdp', partner(orders[i][1]))]
    pallas_call x2 -> x1, Pallas kernels: 24.6 us -> 13.7 us  [ffn_grads(): pl.pallas_call(partial(ffn_grad_kernel, n=n), out_shape=(out_shape, out_s...]
    ppermute x2, waiting for transfers between devices: 9.63 us -> 18.2 us  [on_device(): lax.ppermute(held[i][orders[i][0] >> 1], 'fsdp', partner(orders[i][1]))]
    ppermute x1, waiting for transfers between devices: 4.98 us -> 12.7 us  [on_device(): from_above = lax.ppermute(down_x, 'tensor', [(1, 0), (2, 1), (3, 2)])]
    ppermute x2, waiting for transfers between devices: 11.2 us -> 4.04 us  [line_second(): above2 = lax.ppermute(above, 'tensor', [(2, 1), (1, 0)])]
    ppermute x1, starting transfers between devices: 21.4 us -> 15.1 us  [on_device(): r1 = lax.ppermute(dx_b, 'tensor', [(0, 1), (3, 2)])]
  transfers between devices with their start and end apart: 42 -> 42, of which waited for: 19 -> 16; matrix products, arithmetic and copies ran while one was open for 9% -> 11% of each run, Pallas kernels for 13% -> 14%
where the time goes in v1:
time: 402 us; the launch traced here: 399 us
  Pallas kernels  126 us (31%)
  waiting for transfers between devices  116 us (29%)
  starting transfers between devices  86.3 us (21%)
  local copies, waits for them, and re-layouts  36.3 us (9%)
  other arithmetic  32.5 us (8%)
    pallas_call x2, Pallas kernels, attend_backward(): pl.pallas_call(partial(backward_kernel, slots=slots, first=first, last=la...  42.2 us
    pallas_call x1, Pallas kernels, middle(): pl.pallas_call(partial(middle_kernel, count=count), out_shape=tuple((jax....  29.1 us
    pallas_call x1, Pallas kernels, attend_forward(): pl.pallas_call(partial(forward_kernel, slots=slots, count=count), out_sha...  28.5 us
    ppermute x6, waiting for transfers between devices, spread(): lax.ppermute(block, 'tensor', [(i, (i + shift) % 4) for i in range(4)])  28.4 us
    ppermute x2, waiting for transfers between devices, on_device(): lax.ppermute(held[i][orders[i][0] >> 1], 'fsdp', partner(orders[i][1]))  18.2 us
    ppermute x2, waiting for transfers between devices, line_first(): above = lax.ppermute(own, 'tensor', [(1, 0), (2, 1), (3, 2)])  15.6 us
    ppermute x2, waiting for transfers between devices, on_device(): lax.ppermute(own[i], 'fsdp', partner(orders[i][1]))  15.5 us
    ppermute x1, starting transfers between devices, on_device(): r1 = lax.ppermute(dx_b, 'tensor', [(0, 1), (3, 2)])  15.1 us
  transfers between devices with their start and end apart: 42, of which 16 were waited for; matrix products, arithmetic and copies ran while one was open for 11% of the time, Pallas kernels for 14%

profile of v1, /device:TPU:0, one launch (start us, length us, event | category | flops | bytes accessed | tf_op | source)
XLA Modules:
  0.0 399.2 jit_solution(15030806439800104879)
XLA Ops:
  5.0 5.6 %collective-permute-start.1 = (bf16[3,96,768]{2,1,0:T(8,128)(2,1)S(1)}, bf16[3,96,768]{2,1,0:T(8,128)(2,1)S(1)}, u32[]{:S(2)}, u32[]{:S(2)}) collective-permute-start(bf16[3,96,768]{2,1,0:T(8,128)(2,1)S(1)} %pad_maximum_fusion.2), channel_id=1, source_target_pairs={{0,1},{1,2},{2,3},{4,5},{5,6},{6,7},{8,9},{9,10},{10,11},{12,13},{... | collective-permute-start | bytes 1327112 | tf_op jit(solution)/shard_map/ppermute | solution.py:37
  10.6 8.2 %collective-permute-done = bf16[3,96,768]{2,1,0:T(8,128)(2,1)S(1)} collective-permute-done((bf16[3,96,768]{2,1,0:T(8,128)(2,1)S(1)}, bf16[3,96,768]{2,1,0:T(8,128)(2,1)S(1)}, u32[]{:S(2)}, u32[]{:S(2)}) %collective-permute-start) | collective-permute-done | bytes 442400 | tf_op jit(solution)/shard_map/ppermute | solution.py:38
  28.0 4.0 %collective-permute-done.2 = bf16[3,96,768]{2,1,0:T(8,128)(2,1)S(1)} collective-permute-done((bf16[3,96,768]{2,1,0:T(8,128)(2,1)S(1)}, bf16[3,96,768]{2,1,0:T(8,128)(2,1)S(1)}, u32[]{:S(2)}, u32[]{:S(2)}) %collective-permute-start.2) | collective-permute-done | bytes 442400 | tf_op jit(solution)/shard_map/ppermute | solution.py:44
  34.7 6.1 %collective-permute-start.8 = (bf16[512,768]{1,0:T(8,128)(2,1)S(1)}, bf16[512,768]{1,0:T(8,128)(2,1)}, u32[]{:S(2)}, u32[]{:S(2)}) collective-permute-start(bf16[512,768]{1,0:T(8,128)(2,1)S(1)} %copy-done.6), channel_id=1, source_target_pairs={{0,1},{1,2},{2,3},{4,5},{5,6},{6,7},{8,9},{9,10},{10,11},{12,13},{... | collective-permute-start | bytes 2359304 | tf_op jit(solution)/shard_map/ppermute | solution.py:37
  41.6 5.5 %collective-permute-done.4 = bf16[3,96,768]{2,1,0:T(8,128)(2,1)S(1)} collective-permute-done((bf16[3,96,768]{2,1,0:T(8,128)(2,1)S(1)}, bf16[3,96,768]{2,1,0:T(8,128)(2,1)S(1)}, u32[]{:S(2)}, u32[]{:S(2)}) %collective-permute-start.4) | collective-permute-done | bytes 442400 | tf_op jit(solution)/shard_map/ppermute | solution.py:50
  50.4 1.6 concatenate.60.refs_8_.refs_0_
  52.4 1.5 collective-permute-start.6
  53.9 7.4 %collective-permute-done.7 = bf16[512,768]{1,0:T(8,128)(2,1)} collective-permute-done((bf16[512,768]{1,0:T(8,128)(2,1)S(1)}, bf16[512,768]{1,0:T(8,128)(2,1)}, u32[]{:S(2)}, u32[]{:S(2)}) %collective-permute-start.7) | collective-permute-done | bytes 786464 | tf_op jit(solution)/shard_map/ppermute | solution.py:38
  65.4 8.8 %collective-permute-done.6.refs_18_.refs_10_ = bf16[96,4608]{1,0:T(8,128)(2,1)S(1)} collective-permute-done((bf16[96,4608]{1,0:T(8,128)(2,1)S(1)}, bf16[96,4608]{1,0:T(8,128)(2,1)S(1)}, u32[]{:S(2)}, u32[]{:S(2)}) %collective-permute-start.6) | collective-permute-done | bytes 884768 | tf_op jit(solution)/shard_map/ppermute | solution.py:808
  74.2 1.5 collective-permute-start.9
  75.7 2.1 broadcast_select_fusion.2.refs_1_.refs_3_
  77.8 6.1 %collective-permute-done.5.refs_9_.refs_1_ = bf16[96,4608]{1,0:T(8,128)(2,1)S(1)} collective-permute-done((bf16[96,4608]{1,0:T(8,128)(2,1)S(1)}, bf16[96,4608]{1,0:T(8,128)(2,1)S(1)}, u32[]{:S(2)}, u32[]{:S(2)}) %collective-permute-start.5) | collective-permute-done | bytes 884768 | tf_op jit(solution)/shard_map/ppermute | solution.py:808
  83.9 15.5 %collective-permute-done.10.refs_17_.refs_9_ = bf16[96,4608]{1,0:T(8,128)(2,1)} collective-permute-done((bf16[96,4608]{1,0:T(8,128)(2,1)S(1)}, bf16[96,4608]{1,0:T(8,128)(2,1)}, u32[]{:S(2)}, u32[]{:S(2)}) %collective-permute-start.10) | collective-permute-done | bytes 884768 | tf_op jit(solution)/shard_map/ppermute | solution.py:825
  104.0 17.6 %collective-permute-done.15.refs_11_.refs_3_ = bf16[96,4608]{1,0:T(8,128)(2,1)} collective-permute-done((bf16[96,4608]{1,0:T(8,128)(2,1)S(1)}, bf16[96,4608]{1,0:T(8,128)(2,1)}, u32[]{:S(2)}, u32[]{:S(2)}) %collective-permute-start.15) | collective-permute-done | bytes 884768 | tf_op jit(solution)/shard_map/ppermute | solution.py:832
  124.0 2.1 broadcast_select_fusion.refs_3_.refs_1_
  127.3 28.5 %attend_forward.1 = (bf16[512,768]{1,0:T(8,128)(2,1)}, bf16[2048,768]{1,0:T(8,128)(2,1)}, bf16[2048,768]{1,0:T(8,128)(2,1)}, bf16[512,768]{1,0:T(8,128)(2,1)}, f...) custom-call(s32[2048]{0:T(1024)} %bitcast.124, s32[7]{0:T(128)} %concatenate.55.where, bf16[512,768]{1,0:T(8,128)(2,1)} %refs_0_.3, ...), custom_call_target="tpu_custom_call" | custom-call | flops 1000 | bytes 1000 | tf_op jit(solution)/shard_map/attend_forward/pallas_call | solution.py:279
  155.8 29.1 %middle.1 = (bf16[512,768]{1,0:T(8,128)(2,1)}, f32[512,768]{1,0:T(8,128)}, bf16[512,768]{1,0:T(8,128)(2,1)}, bf16[3,512,768]{2,1,0:T(8,128)(2,1)}, bf16[512,6912]{1,0:T(8,128)(2,1)}, /*index=5*/f32[10,768]{1,0:T(8,128)}) custom-call(s32[6]{0:T(128)} %concatenate.56.known, bf16[96,4608]{1,0:T(8,128)(2,1)} %copy-done.5, bf16[96,4608]{1,0:T(8,128)(2,1)} %copy-done.15, ...), custom_call_target="tpu_custom_call" | custom-call | flops 1000 | bytes 1000 | tf_op jit(solution)/shard_map/middle/pallas_call | solution.py:671
  184.9 13.7 %ffn_grads.1 = (bf16[384,6912]{1,0:T(8,128)(2,1)}, bf16[384,6912]{1,0:T(8,128)(2,1)}) custom-call(s32[1]{0:T(128)} %bitcast.5.place, bf16[3,512,768]{2,1,0:T(8,128)(2,1)} %get-tuple-element.101.left_ref, bf16[512,6912]{1,0:T(8,128)(2,1)} %get-tuple-element.102.right_ref), custom_call_target="tpu_custom_call" | custom-call | flops 1000 | bytes 1000 | tf_op jit(solution)/shard_map/ffn_grads/pallas_call | solution.py:717
  199.1 21.9 %attend_backward.2 = (bf16[1536,768]{1,0:T(8,128)(2,1)}, bf16[1536,768]{1,0:T(8,128)(2,1)}, f32[768,512]{1,0:T(8,128)}, bf16[1536,768]{1,0:T(8,128)(2,1)}) custom-call(s32[2048]{0:T(1024)} %bitcast.125, s32[7]{0:T(128)} %concatenate.55.where, bf16[512,768]{1,0:T(8,128)(2,1)} %get-tuple-element.99.refs_0_, bf16[512,768]{1,0:T(8,128)(2,1)} %get-tuple-element.104.refs_1_, ...), custom_call_target="tpu_custom_call" | custom-call | flops 1000 | bytes 1000 | tf_op jit(solution)/shard_map/attend_backward/pallas_call | solution.py:457
  221.1 1.8 slice.297
  222.9 5.3 %convert_add_fusion = (f32[192,3840]{1,0:T(8,128)S(1)}, bf16[192,3840]{1,0:T(8,128)(2,1)}) fusion(bf16[384,6912]{1,0:T(8,128)(2,1)} %collective-permute-done.24, bf16[384,6912]{1,0:T(8,128)(2,1)} %get-tuple-element.111), kind=kLoop, calls=%fused_computation.2 | loop fusion | flops 5160960 | bytes 10321920 | tf_op jit(solution)/shard_map/add | solution.py:896
  228.2 1.8 slice.299
  230.1 1.7 fusion.5
  231.8 5.7 %collective-permute-start.28 = (bf16[2,96,3072]{2,1,0:T(8,128)(2,1)}, bf16[2,96,3072]{2,1,0:T(8,128)(2,1)}, u32[]{:S(2)}, u32[]{:S(2)}) collective-permute-start(bf16[2,96,3072]{2,1,0:T(8,128)(2,1)} %fusion.5), channel_id=1, source_target_pairs={{0,8},{4,12},{8,0},{12,4},{16,24},{20,28},{24,16},{28,20},{1,9},{5... | collective-permute-start | bytes 3538952 | tf_op jit(solution)/shard_map/ppermute | solution.py:886
  237.6 2.1 slice.296
  239.7 15.1 %collective-permute-start.25 = (bf16[512,768]{1,0:T(8,128)(2,1)}, bf16[512,768]{1,0:T(8,128)(2,1)}, u32[]{:S(2)}, u32[]{:S(2)}) collective-permute-start(bf16[512,768]{1,0:T(8,128)(2,1)} %slice.296), channel_id=1, source_target_pairs={{0,1},{3,2},{4,5},{7,6},{8,9},{11,10},{12,13},{15,14},{16,17},{19,... | collective-permute-start | bytes 2359304 | tf_op jit(solution)/shard_map/ppermute | solution.py:873
  254.8 20.3 %attend_backward.3 = (bf16[512,768]{1,0:T(8,128)(2,1)}, bf16[512,768]{1,0:T(8,128)(2,1)}, bf16[512,768]{1,0:T(8,128)(2,1)}, f32[512,768]{1,0:T(8,128)}) custom-call(s32[2048]{0:T(1024)} %bitcast.126, s32[7]{0:T(128)} %concatenate.55.where, bf16[512,768]{1,0:T(8,128)(2,1)} %get-tuple-element.99.refs_0_, bf16[512,768]{1,0:T(8,128)(2,1)} %get-tuple-element.104.refs_1_, ...), custom_call_target="tpu_custom_call" | custom-call | flops 1000 | bytes 1000 | tf_op jit(solution)/shard_map/attend_backward/pallas_call | solution.py:457
  275.1 2.5 add_convert_fusion.4
  277.6 2.2 collective-permute-start.26
  279.8 1.6 collective-permute-start.27
  281.3 1.8 add_convert_fusion.1
  284.3 1.8 fusion
  286.2 2.2 collective-permute-start.34
  290.1 12.6 %attn_grads.1 = (bf16[4,304,768]{2,1,0:T(8,128)(2,1)}, f32[4,304,768]{2,1,0:T(8,128)}) custom-call(s32[1]{0:T(128)} %slice.305.core_ref, bf16[512,768]{1,0:T(8,128)(2,1)} %refs_0_.3, bf16[512,768]{1,0:T(8,128)(2,1)} %broadcast_select_fusion.refs_3_.refs_1_, bf16[512,768]{1,0:T(8,128)(2,1)} %copy-done.7, ...), custom_call_target="tpu_custom_call" | custom-call | flops 1000 | bytes 1000 | tf_op jit(solution)/shard_map/attn_grads/pallas_call | solution.py:535
  302.8 14.0 %collective-permute-start.32 = (bf16[4,304,768]{2,1,0:T(8,128)(2,1)}, bf16[4,304,768]{2,1,0:T(8,128)(2,1)S(1)}, u32[]{:S(2)}, u32[]{:S(2)}) collective-permute-start(bf16[4,304,768]{2,1,0:T(8,128)(2,1)} %get-tuple-element.126), channel_id=1, source_target_pairs={{0,4},{4,0},{8,12},{12,8},{16,20},{20,16},{24,28},{28,24},{1,5},{5... | collective-permute-start | bytes 5603336 | tf_op jit(solution)/shard_map/ppermute | solution.py:921
  316.8 3.1 fusion.1
  319.9 2.2 collective-permute-start.30
  326.3 1.8 copy-done.11
  328.1 1.7 add_convert_fusion
  329.8 3.6 all-to-all-start
  333.7 2.7 collective-permute-start.35
  339.3 12.7 %collective-permute-done.31 = bf16[512,768]{1,0:T(8,128)(2,1)} collective-permute-done((bf16[512,768]{1,0:T(8,128)(2,1)}, bf16[512,768]{1,0:T(8,128)(2,1)}, u32[]{:S(2)}, u32[]{:S(2)}) %collective-permute-start.31) | collective-permute-done | bytes 786464 | tf_op jit(solution)/shard_map/ppermute | solution.py:927
  352.0 2.8 convert_add_fusion.2
  354.8 4.2 %collective-permute-done.36 = bf16[96,1728]{1,0:T(8,128)(2,1)S(1)} collective-permute-done((bf16[96,1728]{1,0:T(8,128)(2,1)S(1)}, bf16[96,1728]{1,0:T(8,128)(2,1)S(1)}, u32[]{:S(2)}, u32[]{:S(2)}) %collective-permute-start.36) | collective-permute-done | bytes 331808 | tf_op jit(solution)/shard_map/ppermute | solution.py:72
  359.0 12.9 %collective-permute-done.37 = bf16[96,1728]{1,0:T(8,128)(2,1)S(1)} collective-permute-done((bf16[96,1728]{1,0:T(8,128)(2,1)S(1)}, bf16[96,1728]{1,0:T(8,128)(2,1)S(1)}, u32[]{:S(2)}, u32[]{:S(2)}) %collective-permute-start.37) | collective-permute-done | bytes 331808 | tf_op jit(solution)/shard_map/ppermute | solution.py:72
  376.0 3.8 collective-permute-start.39
  380.7 4.4 %collective-permute-done.38 = bf16[336,192]{1,0:T(8,128)(2,1)S(1)} collective-permute-done((bf16[336,192]{1,0:T(8,128)(2,1)S(1)}, bf16[336,192]{1,0:T(8,128)(2,1)S(1)}, u32[]{:S(2)}, u32[]{:S(2)}) %collective-permute-start.38) | collective-permute-done | bytes 129056 | tf_op jit(solution)/shard_map/ppermute | solution.py:72
  385.9 6.1 %collective-permute-done.40 = bf16[336,192]{1,0:T(8,128)(2,1)S(1)} collective-permute-done((bf16[336,192]{1,0:T(8,128)(2,1)S(1)}, bf16[336,192]{1,0:T(8,128)(2,1)S(1)}, u32[]{:S(2)}, u32[]{:S(2)}) %collective-permute-start.40) | collective-permute-done | bytes 129056 | tf_op jit(solution)/shard_map/ppermute | solution.py:72
  (203 shorter events, 55.9 us)
Async XLA Ops:
  0.7 32.7 %copy-start.6 = (bf16[512,768]{1,0:T(8,128)(2,1)S(1)}, bf16[512,768]{1,0:T(8,128)(2,1)}, u32[]{:S(2)}) copy-start(bf16[512,768]{1,0:T(8,128)(2,1)} %refs_0_.3) | copy-start | bytes 2359300
  3.7 15.1 %collective-permute-start = (bf16[3,96,768]{2,1,0:T(8,128)(2,1)S(1)}, bf16[3,96,768]{2,1,0:T(8,128)(2,1)S(1)}, u32[]{:S(2)}, u32[]{:S(2)}) collective-permute-start(bf16[3,96,768]{2,1,0:T(8,128)(2,1)S(1)} %pad_maximum_fusion.2), channel_id=1, source_target_pairs={{1,0},{2,1},{3,2},{5,4},{6,5},{7,6},{9,8},{10,9},{11,10},{13,12},{... | collective-permute-start | bytes 1327112 | tf_op jit(solution)/shard_map/ppermute | solution.py:38
  5.0 15.1 %collective-permute-start.1 = (bf16[3,96,768]{2,1,0:T(8,128)(2,1)S(1)}, bf16[3,96,768]{2,1,0:T(8,128)(2,1)S(1)}, u32[]{:S(2)}, u32[]{:S(2)}) collective-permute-start(bf16[3,96,768]{2,1,0:T(8,128)(2,1)S(1)} %pad_maximum_fusion.2), channel_id=1, source_target_pairs={{0,1},{1,2},{2,3},{4,5},{5,6},{6,7},{8,9},{9,10},{10,11},{12,13},{... | collective-permute-start | bytes 1327112 | tf_op jit(solution)/shard_map/ppermute | solution.py:37
  18.8 13.2 %collective-permute-start.2 = (bf16[3,96,768]{2,1,0:T(8,128)(2,1)S(1)}, bf16[3,96,768]{2,1,0:T(8,128)(2,1)S(1)}, u32[]{:S(2)}, u32[]{:S(2)}) collective-permute-start(bf16[3,96,768]{2,1,0:T(8,128)(2,1)S(1)} %collective-permute-done), channel_id=1, source_target_pairs={{2,1},{1,0},{6,5},{5,4},{10,9},{9,8},{14,13},{13,12},{18,17},{17,1... | collective-permute-start | bytes 1327112 | tf_op jit(solution)/shard_map/ppermute | solution.py:44
  20.1 11.9 %collective-permute-start.3 = (bf16[3,96,768]{2,1,0:T(8,128)(2,1)S(1)}, bf16[3,96,768]{2,1,0:T(8,128)(2,1)S(1)}, u32[]{:S(2)}, u32[]{:S(2)}) collective-permute-start(bf16[3,96,768]{2,1,0:T(8,128)(2,1)S(1)} %collective-permute-done.1), channel_id=1, source_target_pairs={{1,2},{2,3},{5,6},{6,7},{9,10},{10,11},{13,14},{14,15},{17,18},{18... | collective-permute-start | bytes 1327112 | tf_op jit(solution)/shard_map/ppermute | solution.py:43
  32.1 15.0 %collective-permute-start.4 = (bf16[3,96,768]{2,1,0:T(8,128)(2,1)S(1)}, bf16[3,96,768]{2,1,0:T(8,128)(2,1)S(1)}, u32[]{:S(2)}, u32[]{:S(2)}) collective-permute-start(bf16[3,96,768]{2,1,0:T(8,128)(2,1)S(1)} %broadcast_select_fusion.4), channel_id=1, source_target_pairs={{1,0},{2,3},{5,4},{6,7},{9,8},{10,11},{13,12},{14,15},{17,16},{18,... | collective-permute-start | bytes 1327112 | tf_op jit(solution)/shard_map/ppermute | solution.py:50
  33.4 28.0 %collective-permute-start.7 = (bf16[512,768]{1,0:T(8,128)(2,1)S(1)}, bf16[512,768]{1,0:T(8,128)(2,1)}, u32[]{:S(2)}, u32[]{:S(2)}) collective-permute-start(bf16[512,768]{1,0:T(8,128)(2,1)S(1)} %copy-done.6), channel_id=1, source_target_pairs={{1,0},{2,1},{3,2},{5,4},{6,5},{7,6},{9,8},{10,9},{11,10},{13,12},{... | collective-permute-start | bytes 2359304 | tf_op jit(solution)/shard_map/ppermute | solution.py:38
  34.7 27.8 %collective-permute-start.8 = (bf16[512,768]{1,0:T(8,128)(2,1)S(1)}, bf16[512,768]{1,0:T(8,128)(2,1)}, u32[]{:S(2)}, u32[]{:S(2)}) collective-permute-start(bf16[512,768]{1,0:T(8,128)(2,1)S(1)} %copy-done.6), channel_id=1, source_target_pairs={{0,1},{1,2},{2,3},{4,5},{5,6},{6,7},{8,9},{9,10},{10,11},{12,13},{... | collective-permute-start | bytes 2359304 | tf_op jit(solution)/shard_map/ppermute | solution.py:37
  50.3 13.0 %collective-permute-start.12 = (bf16[96,4608]{1,0:T(8,128)(2,1)S(1)}, bf16[96,4608]{1,0:T(8,128)(2,1)S(1)}, u32[]{:S(2)}, u32[]{:S(2)}) collective-permute-start(bf16[96,4608]{1,0:T(8,128)(2,1)S(1)} %concatenate.61.refs_16_.refs_8_), channel_id=1, source_target_pairs={{0,4},{4,0},{8,12},{12,8},{16,20},{20,16},{24,28},{28,24},{1,5},{5... | collective-permute-start | bytes 2654216 | tf_op jit(solution)/shard_map/ppermute | solution.py:819
  52.0 49.8 %copy-start.5 = (bf16[96,4608]{1,0:T(8,128)(2,1)}, bf16[96,4608]{1,0:T(8,128)(2,1)S(1)}, u32[]{:S(2)}) copy-start(bf16[96,4608]{1,0:T(8,128)(2,1)S(1)} %concatenate.60.refs_8_.refs_0_) | copy-start | bytes 2654212
  52.1 11.3 %collective-permute-start.11 = (bf16[96,4608]{1,0:T(8,128)(2,1)S(1)}, bf16[96,4608]{1,0:T(8,128)(2,1)S(1)}, u32[]{:S(2)}, u32[]{:S(2)}) collective-permute-start(bf16[96,4608]{1,0:T(8,128)(2,1)S(1)} %concatenate.60.refs_8_.refs_0_), channel_id=1, source_target_pairs={{0,4},{4,0},{8,12},{12,8},{16,20},{20,16},{24,28},{28,24},{1,5},{5... | collective-permute-start | bytes 2654216 | tf_op jit(solution)/shard_map/ppermute | solution.py:819
  52.4 21.8 %collective-permute-start.6 = (bf16[96,4608]{1,0:T(8,128)(2,1)S(1)}, bf16[96,4608]{1,0:T(8,128)(2,1)S(1)}, u32[]{:S(2)}, u32[]{:S(2)}) collective-permute-start(bf16[96,4608]{1,0:T(8,128)(2,1)S(1)} %concatenate.61.refs_16_.refs_8_), channel_id=1, source_target_pairs={{0,16},{4,20},{8,24},{12,28},{16,0},{20,4},{24,8},{28,12},{1,17},{... | collective-permute-start | bytes 2654216 | tf_op jit(solution)/shard_map/ppermute | solution.py:808
  61.3 22.6 %collective-permute-start.5 = (bf16[96,4608]{1,0:T(8,128)(2,1)S(1)}, bf16[96,4608]{1,0:T(8,128)(2,1)S(1)}, u32[]{:S(2)}, u32[]{:S(2)}) collective-permute-start(bf16[96,4608]{1,0:T(8,128)(2,1)S(1)} %concatenate.60.refs_8_.refs_0_), channel_id=1, source_target_pairs={{0,8},{4,12},{8,0},{12,4},{16,24},{20,28},{24,16},{28,20},{1,9},{5... | collective-permute-start | bytes 2654216 | tf_op jit(solution)/shard_map/ppermute | solution.py:808
  62.5 36.9 %collective-permute-start.10 = (bf16[96,4608]{1,0:T(8,128)(2,1)S(1)}, bf16[96,4608]{1,0:T(8,128)(2,1)}, u32[]{:S(2)}, u32[]{:S(2)}) collective-permute-start(bf16[96,4608]{1,0:T(8,128)(2,1)S(1)} %concatenate.61.refs_16_.refs_8_), channel_id=1, source_target_pairs={{0,8},{4,12},{8,0},{12,4},{16,24},{20,28},{24,16},{28,20},{1,9},{5... | collective-permute-start | bytes 2654216 | tf_op jit(solution)/shard_map/ppermute | solution.py:825
  63.4 38.5 %copy-start.12 = (bf16[96,4608]{1,0:T(8,128)(2,1)}, bf16[96,4608]{1,0:T(8,128)(2,1)S(1)}, u32[]{:S(2)}) copy-start(bf16[96,4608]{1,0:T(8,128)(2,1)S(1)} %collective-permute-done.12.refs_20_.refs_12_) | copy-start | bytes 2654212
  63.4 36.0 %collective-permute-start.13 = (bf16[512,768]{1,0:T(8,128)(2,1)}, bf16[512,768]{1,0:T(8,128)(2,1)S(1)}, u32[]{:S(2)}, u32[]{:S(2)}) collective-permute-start(bf16[512,768]{1,0:T(8,128)(2,1)} %collective-permute-done.7), channel_id=1, source_target_pairs={{2,1},{1,0},{6,5},{5,4},{10,9},{9,8},{14,13},{13,12},{18,17},{17,1... | collective-permute-start | bytes 2359304 | tf_op jit(solution)/shard_map/ppermute | solution.py:44
  64.7 35.6 %collective-permute-start.14 = (bf16[512,768]{1,0:T(8,128)(2,1)}, bf16[512,768]{1,0:T(8,128)(2,1)S(1)}, u32[]{:S(2)}, u32[]{:S(2)}) collective-permute-start(bf16[512,768]{1,0:T(8,128)(2,1)} %collective-permute-done.8), channel_id=1, source_target_pairs={{1,2},{2,3},{5,6},{6,7},{9,10},{10,11},{13,14},{14,15},{17,18},{18... | collective-permute-start | bytes 2359304 | tf_op jit(solution)/shard_map/ppermute | solution.py:43
  74.2 27.7 %collective-permute-start.9 = (bf16[96,4608]{1,0:T(8,128)(2,1)S(1)}, bf16[96,4608]{1,0:T(8,128)(2,1)}, u32[]{:S(2)}, u32[]{:S(2)}) collective-permute-start(bf16[96,4608]{1,0:T(8,128)(2,1)S(1)} %concatenate.60.refs_8_.refs_0_), channel_id=1, source_target_pairs={{0,16},{4,20},{8,24},{12,28},{16,0},{20,4},{24,8},{28,12},{1,17},{... | collective-permute-start | bytes 2654216 | tf_op jit(solution)/shard_map/ppermute | solution.py:825
  77.8 45.5 %copy-start.26 = (f32[3072]{0:T(1024)S(1)}, f32[3072]{0:T(1024)}, u32[]{:S(2)}) copy-start(f32[3072]{0:T(1024)} %param.30) | copy-start | bytes 36868
  83.9 38.2 %copy-start.15 = (bf16[96,4608]{1,0:T(8,128)(2,1)}, bf16[96,4608]{1,0:T(8,128)(2,1)S(1)}, u32[]{:S(2)}) copy-start(bf16[96,4608]{1,0:T(8,128)(2,1)S(1)} %collective-permute-done.5.refs_9_.refs_1_) | copy-start | bytes 2654212
  83.9 19.5 %collective-permute-start.16 = (bf16[96,4608]{1,0:T(8,128)(2,1)S(1)}, bf16[96,4608]{1,0:T(8,128)(2,1)S(1)}, u32[]{:S(2)}, u32[]{:S(2)}) collective-permute-start(bf16[96,4608]{1,0:T(8,128)(2,1)S(1)} %collective-permute-done.5.refs_9_.refs_1_), channel_id=1, source_target_pairs={{0,4},{4,0},{8,12},{12,8},{16,20},{20,16},{24,28},{28,24},{1,5},{5... | collective-permute-start | bytes 2654216 | tf_op jit(solution)/shard_map/ppermute | solution.py:819
  99.4 4.1 %collective-permute-start.21 = (bf16[96,4608]{1,0:T(8,128)(2,1)S(1)}, bf16[96,4608]{1,0:T(8,128)(2,1)S(1)}, u32[]{:S(2)}, u32[]{:S(2)}) collective-permute-start(bf16[96,4608]{1,0:T(8,128)(2,1)S(1)} %collective-permute-done.6.refs_18_.refs_10_), channel_id=1, source_target_pairs={{0,4},{4,0},{8,12},{12,8},{16,20},{20,16},{24,28},{28,24},{1,5},{5... | collective-permute-start | bytes 2654216 | tf_op jit(solution)/shard_map/ppermute | solution.py:819
  99.4 22.2 %collective-permute-start.15 = (bf16[96,4608]{1,0:T(8,128)(2,1)S(1)}, bf16[96,4608]{1,0:T(8,128)(2,1)}, u32[]{:S(2)}, u32[]{:S(2)}) collective-permute-start(bf16[96,4608]{1,0:T(8,128)(2,1)S(1)} %collective-permute-done.5.refs_9_.refs_1_), channel_id=1, source_target_pairs={{0,16},{4,20},{8,24},{12,28},{16,0},{20,4},{24,8},{28,12},{1,17},{... | collective-permute-start | bytes 2654216 | tf_op jit(solution)/shard_map/ppermute | solution.py:832
  100.3 21.9 %collective-permute-start.19 = (bf16[96,4608]{1,0:T(8,128)(2,1)S(1)}, bf16[96,4608]{1,0:T(8,128)(2,1)}, u32[]{:S(2)}, u32[]{:S(2)}) collective-permute-start(bf16[96,4608]{1,0:T(8,128)(2,1)S(1)} %collective-permute-done.6.refs_18_.refs_10_), channel_id=1, source_target_pairs={{0,8},{4,12},{8,0},{12,4},{16,24},{20,28},{24,16},{28,20},{1,9},{5... | collective-permute-start | bytes 2654216 | tf_op jit(solution)/shard_map/ppermute | solution.py:832
  101.9 22.0 %collective-permute-start.23 = (bf16[512,768]{1,0:T(8,128)(2,1)S(1)}, bf16[512,768]{1,0:T(8,128)(2,1)}, u32[]{:S(2)}, u32[]{:S(2)}) collective-permute-start(bf16[512,768]{1,0:T(8,128)(2,1)S(1)} %broadcast_select_fusion.1.refs_2_), channel_id=1, source_target_pairs={{1,0},{2,3},{5,4},{6,7},{9,8},{10,11},{13,12},{14,15},{17,16},{18,... | collective-permute-start | bytes 2359304 | tf_op jit(solution)/shard_map/ppermute | solution.py:50
  103.4 22.7 %collective-permute-start.17 = (bf16[96,4608]{1,0:T(8,128)(2,1)}, bf16[96,4608]{1,0:T(8,128)(2,1)S(1)}, u32[]{:S(2)}, u32[]{:S(2)}) collective-permute-start(bf16[96,4608]{1,0:T(8,128)(2,1)} %collective-permute-done.9.refs_10_.refs_2_), channel_id=1, source_target_pairs={{0,4},{4,0},{8,12},{12,8},{16,20},{20,16},{24,28},{28,24},{1,5},{5... | collective-permute-start | bytes 2654216 | tf_op jit(solution)/shard_map/ppermute | solution.py:819
  103.5 22.6 %collective-permute-start.20 = (bf16[96,4608]{1,0:T(8,128)(2,1)}, bf16[96,4608]{1,0:T(8,128)(2,1)S(1)}, u32[]{:S(2)}, u32[]{:S(2)}) collective-permute-start(bf16[96,4608]{1,0:T(8,128)(2,1)} %collective-permute-done.10.refs_17_.refs_9_), channel_id=1, source_target_pairs={{0,4},{4,0},{8,12},{12,8},{16,20},{20,16},{24,28},{28,24},{1,5},{5... | collective-permute-start | bytes 2654216 | tf_op jit(solution)/shard_map/ppermute | solution.py:819
  121.6 4.5 %collective-permute-start.18 = (bf16[96,4608]{1,0:T(8,128)(2,1)}, bf16[96,4608]{1,0:T(8,128)(2,1)}, u32[]{:S(2)}, u32[]{:S(2)}) collective-permute-start(bf16[96,4608]{1,0:T(8,128)(2,1)} %collective-permute-done.15.refs_11_.refs_3_), channel_id=1, source_target_pairs={{0,4},{4,0},{8,12},{12,8},{16,20},{20,16},{24,28},{28,24},{1,5},{5... | collective-permute-start | bytes 2654216 | tf_op jit(solution)/shard_map/ppermute | solution.py:819
  122.2 4.0 collective-permute-start.22
  198.6 24.3 %collective-permute-start.24 = (bf16[384,6912]{1,0:T(8,128)(2,1)}, bf16[384,6912]{1,0:T(8,128)(2,1)}, u32[]{:S(2)}, u32[]{:S(2)}) collective-permute-start(bf16[384,6912]{1,0:T(8,128)(2,1)} %get-tuple-element.103), channel_id=1, source_target_pairs={{0,4},{4,0},{8,12},{12,8},{16,20},{20,16},{24,28},{28,24},{1,5},{5... | collective-permute-start | bytes 15925256 | tf_op jit(solution)/shard_map/ppermute | solution.py:867
  230.0 51.3 %collective-permute-start.29 = (bf16[2,96,3840]{2,1,0:T(8,128)(2,1)}, bf16[2,96,3840]{2,1,0:T(8,128)(2,1)}, u32[]{:S(2)}, u32[]{:S(2)}) collective-permute-start(bf16[2,96,3840]{2,1,0:T(8,128)(2,1)} %bitcast.33), channel_id=1, source_target_pairs={{0,16},{4,20},{8,24},{12,28},{16,0},{20,4},{24,8},{28,12},{1,17},{... | collective-permute-start | bytes 4423688 | tf_op jit(solution)/shard_map/ppermute | solution.py:886
  231.8 49.5 %collective-permute-start.28 = (bf16[2,96,3072]{2,1,0:T(8,128)(2,1)}, bf16[2,96,3072]{2,1,0:T(8,128)(2,1)}, u32[]{:S(2)}, u32[]{:S(2)}) collective-permute-start(bf16[2,96,3072]{2,1,0:T(8,128)(2,1)} %fusion.5), channel_id=1, source_target_pairs={{0,8},{4,12},{8,0},{12,4},{16,24},{20,28},{24,16},{28,20},{1,9},{5... | collective-permute-start | bytes 3538952 | tf_op jit(solution)/shard_map/ppermute | solution.py:886
  239.7 35.4 %collective-permute-start.25 = (bf16[512,768]{1,0:T(8,128)(2,1)}, bf16[512,768]{1,0:T(8,128)(2,1)}, u32[]{:S(2)}, u32[]{:S(2)}) collective-permute-start(bf16[512,768]{1,0:T(8,128)(2,1)} %slice.296), channel_id=1, source_target_pairs={{0,1},{3,2},{4,5},{7,6},{8,9},{11,10},{12,13},{15,14},{16,17},{19,... | collective-permute-start | bytes 2359304 | tf_op jit(solution)/shard_map/ppermute | solution.py:873
  277.6 39.1 %collective-permute-start.26 = (bf16[512,768]{1,0:T(8,128)(2,1)}, bf16[512,768]{1,0:T(8,128)(2,1)}, u32[]{:S(2)}, u32[]{:S(2)}) collective-permute-start(bf16[512,768]{1,0:T(8,128)(2,1)} %add_convert_fusion.4), channel_id=1, source_target_pairs={{0,1},{3,2},{4,5},{7,6},{8,9},{11,10},{12,13},{15,14},{16,17},{19,... | collective-permute-start | bytes 2359304 | tf_op jit(solution)/shard_map/ppermute | solution.py:891
  279.8 37.0 %collective-permute-start.27 = (bf16[512,768]{1,0:T(8,128)(2,1)}, bf16[512,768]{1,0:T(8,128)(2,1)}, u32[]{:S(2)}, u32[]{:S(2)}) collective-permute-start(bf16[512,768]{1,0:T(8,128)(2,1)} %add_convert_fusion.4), channel_id=1, source_target_pairs={{1,2},{2,1},{5,6},{6,5},{9,10},{10,9},{13,14},{14,13},{17,18},{18,... | collective-permute-start | bytes 2359304 | tf_op jit(solution)/shard_map/ppermute | solution.py:892
  286.2 37.2 %collective-permute-start.34 = (bf16[96,3840]{1,0:T(8,128)(2,1)}, bf16[96,3840]{1,0:T(8,128)(2,1)}, u32[]{:S(2)}, u32[]{:S(2)}) collective-permute-start(bf16[96,3840]{1,0:T(8,128)(2,1)} %slice_bitcast_fusion.5), channel_id=1, source_target_pairs={{0,8},{4,12},{8,0},{12,4},{16,24},{20,28},{24,16},{28,20},{1,9},{5... | collective-permute-start | bytes 2211848 | tf_op jit(solution)/shard_map/ppermute | solution.py:114
  289.3 34.1 %collective-permute-start.33 = (bf16[96,3072]{1,0:T(8,128)(2,1)}, bf16[96,3072]{1,0:T(8,128)(2,1)}, u32[]{:S(2)}, u32[]{:S(2)}) collective-permute-start(bf16[96,3072]{1,0:T(8,128)(2,1)} %slice_bitcast_fusion.7), channel_id=1, source_target_pairs={{0,16},{4,20},{8,24},{12,28},{16,0},{20,4},{24,8},{28,12},{1,17},{... | collective-permute-start | bytes 1769480 | tf_op jit(solution)/shard_map/ppermute | solution.py:114
  302.8 23.5 %collective-permute-start.32 = (bf16[4,304,768]{2,1,0:T(8,128)(2,1)}, bf16[4,304,768]{2,1,0:T(8,128)(2,1)S(1)}, u32[]{:S(2)}, u32[]{:S(2)}) collective-permute-start(bf16[4,304,768]{2,1,0:T(8,128)(2,1)} %get-tuple-element.126), channel_id=1, source_target_pairs={{0,4},{4,0},{8,12},{12,8},{16,20},{20,16},{24,28},{28,24},{1,5},{5... | collective-permute-start | bytes 5603336 | tf_op jit(solution)/shard_map/ppermute | solution.py:921
  319.9 19.5 %collective-permute-start.30 = (bf16[512,768]{1,0:T(8,128)(2,1)}, bf16[512,768]{1,0:T(8,128)(2,1)}, u32[]{:S(2)}, u32[]{:S(2)}) collective-permute-start(bf16[512,768]{1,0:T(8,128)(2,1)} %get-tuple-element.177), channel_id=1, source_target_pairs={{0,1},{1,2},{2,3},{4,5},{5,6},{6,7},{8,9},{9,10},{10,11},{12,13},{... | collective-permute-start | bytes 2359304 | tf_op jit(solution)/shard_map/ppermute | solution.py:926
  322.1 30.0 %collective-permute-start.31 = (bf16[512,768]{1,0:T(8,128)(2,1)}, bf16[512,768]{1,0:T(8,128)(2,1)}, u32[]{:S(2)}, u32[]{:S(2)}) collective-permute-start(bf16[512,768]{1,0:T(8,128)(2,1)} %get-tuple-element.178), channel_id=1, source_target_pairs={{1,0},{2,1},{3,2},{5,4},{6,5},{7,6},{9,8},{10,9},{11,10},{13,12},{... | collective-permute-start | bytes 2359304 | tf_op jit(solution)/shard_map/ppermute | solution.py:927
  329.8 43.0 %all-to-all-start = ((bf16[4,304,768]{2,1,0:T(8,128)(2,1)}), bf16[4,304,768]{2,1,0:T(8,128)(2,1)S(1)}, u32[]{:S(2)}, u32[]{:S(2)}) async-start(bf16[4,304,768]{2,1,0:T(8,128)(2,1)} %add_convert_fusion), calls=%async_computation | async-start | bytes 3735552 | tf_op jit(solution)/shard_map/all_to_all | solution.py:949
  333.7 21.1 %collective-permute-start.35 = (bf16[96,1728]{1,0:T(8,128)(2,1)S(1)}, bf16[96,1728]{1,0:T(8,128)(2,1)S(1)}, u32[]{:S(2)}, u32[]{:S(2)}) collective-permute-start(bf16[96,1728]{1,0:T(8,128)(2,1)S(1)} %get-tuple-element.181), channel_id=1, source_target_pairs={{0,1},{1,2},{2,3},{3,0},{4,5},{5,6},{6,7},{7,4},{8,9},{9,10},{10,1... | collective-permute-start | bytes 995336 | tf_op jit(solution)/shard_map/ppermute | solution.py:72
  336.4 22.6 %collective-permute-start.36 = (bf16[96,1728]{1,0:T(8,128)(2,1)S(1)}, bf16[96,1728]{1,0:T(8,128)(2,1)S(1)}, u32[]{:S(2)}, u32[]{:S(2)}) collective-permute-start(bf16[96,1728]{1,0:T(8,128)(2,1)S(1)} %get-tuple-element.180), channel_id=1, source_target_pairs={{0,3},{1,0},{2,1},{3,2},{4,7},{5,4},{6,5},{7,6},{8,11},{9,8},{10,9... | collective-permute-start | bytes 995336 | tf_op jit(solution)/shard_map/ppermute | solution.py:72
  337.7 34.2 %copy-start.24 = (bf16[96,192]{1,0:T(8,128)(2,1)S(1)}, bf16[96,192]{1,0:T(8,128)(2,1)}, u32[]{:S(2)}) copy-start(bf16[96,192]{1,0:T(8,128)(2,1)} %copy-done.23) | copy-start | bytes 110596
  337.7 34.2 %collective-permute-start.37 = (bf16[96,1728]{1,0:T(8,128)(2,1)S(1)}, bf16[96,1728]{1,0:T(8,128)(2,1)S(1)}, u32[]{:S(2)}, u32[]{:S(2)}) collective-permute-start(bf16[96,1728]{1,0:T(8,128)(2,1)S(1)} %get-tuple-element.179), channel_id=1, source_target_pairs={{0,2},{1,3},{2,0},{3,1},{4,6},{5,7},{6,4},{7,5},{8,10},{9,11},{10,... | collective-permute-start | bytes 995336 | tf_op jit(solution)/shard_map/ppermute | solution.py:72
  376.0 9.2 %collective-permute-start.38 = (bf16[336,192]{1,0:T(8,128)(2,1)S(1)}, bf16[336,192]{1,0:T(8,128)(2,1)S(1)}, u32[]{:S(2)}, u32[]{:S(2)}) collective-permute-start(bf16[336,192]{1,0:T(8,128)(2,1)S(1)} %get-tuple-element.192), channel_id=1, source_target_pairs={{0,1},{1,2},{2,3},{3,0},{4,5},{5,6},{6,7},{7,4},{8,9},{9,10},{10,1... | collective-permute-start | bytes 387080 | tf_op jit(solution)/shard_map/ppermute | solution.py:72
  376.0 9.9 %collective-permute-start.39 = (bf16[336,192]{1,0:T(8,128)(2,1)S(1)}, bf16[336,192]{1,0:T(8,128)(2,1)S(1)}, u32[]{:S(2)}, u32[]{:S(2)}) collective-permute-start(bf16[336,192]{1,0:T(8,128)(2,1)S(1)} %get-tuple-element.194), channel_id=1, source_target_pairs={{0,3},{1,0},{2,1},{3,2},{4,7},{5,4},{6,5},{7,6},{8,11},{9,8},{10,9... | collective-permute-start | bytes 387080 | tf_op jit(solution)/shard_map/ppermute | solution.py:72
  379.8 12.2 %collective-permute-start.40 = (bf16[336,192]{1,0:T(8,128)(2,1)S(1)}, bf16[336,192]{1,0:T(8,128)(2,1)S(1)}, u32[]{:S(2)}, u32[]{:S(2)}) collective-permute-start(bf16[336,192]{1,0:T(8,128)(2,1)S(1)} %get-tuple-element.193), channel_id=1, source_target_pairs={{0,2},{1,3},{2,0},{3,1},{4,6},{5,7},{6,4},{7,5},{8,10},{9,11},{10,... | collective-permute-start | bytes 387080 | tf_op jit(solution)/shard_map/ppermute | solution.py:72
  (26 other events, 362.6 us)

commit v2 on v1

--- a/solution.py
+++ b/solution.py
@@ -166,15 +166,20 @@
         lax.fori_loop(0, per * per, step, 0)
 
 
-def piece_copy(pieces, j, f, column, width, target, sem):
+def split_pieces(pieces):
+    return [[p[0] for p in half] for half in pieces], tuple(tuple(p[1] for p in half) for half in pieces)
+
+
+def piece_copy(pieces, offsets, j, f, column, width, target, sem):
     r = pieces[0].shape[0]
     place = 0
     if len(pieces) > 1:
         core, outer = j // (len(pieces) // 2), j % (len(pieces) // 2)
         place = f ^ (2 * outer + core)
     rows = pl.ds(pl.multiple_of(place * r, r), r)
+    start = offsets[j] + column * width
     return pltpu.make_async_copy(
-        pieces[j].at[:, column * width : (column + 1) * width], target.at[rows, :], sem
+        pieces[j].at[:, start : start + width], target.at[rows, :], sem
     )
 
 
@@ -182,7 +187,7 @@
     return pl.ds(pl.multiple_of(index * size, size), size)
 
 
-def forward_kernel(seg, where, *refs, slots, count):
+def forward_kernel(seg, where, *refs, slots, count, offsets):
     refs = list(refs)
 
     def take(count):
@@ -198,7 +203,7 @@
     @pl.when(pl.program_id(0) == 0)
     def _():
         copies = [
-            piece_copy(pieces[m // 2], j, where[6], m % 2, w_s.shape[2], w_s.at[m], sems.at[m, j])
+            piece_copy(pieces[m // 2], offsets[m // 2], j, where[6], m % 2, w_s.shape[2], w_s.at[m], sems.at[m, j])
             for m in range(3)
             for j in range(count)
         ]
@@ -263,6 +268,7 @@
     slots = tuple(range(len(xs)))
     keys = rows * len(xs)
     count = len(pieces[0])
+    pieces, offsets = split_pieces(pieces)
     groups, wide = width // GROUP, GROUP // HD * rows
     block_spec = pl.BlockSpec((rows, GROUP), lambda i, s, w: (0, i))
     keys_spec = pl.BlockSpec((keys, GROUP), lambda i, s, w: (0, i))
@@ -277,7 +283,7 @@
     in_specs = [pl.BlockSpec((rows, width), lambda i, s, w: (0, 0))] * len(xs)
     in_specs += [ids_spec(1 + s) for s in slots] + [pl.BlockSpec(memory_space=pl.ANY)] * (2 * count) + [b_spec] * 2 + [ids_spec(0)]
     return pl.pallas_call(
-        partial(forward_kernel, slots=slots, count=count),
+        partial(forward_kernel, slots=slots, count=count, offsets=offsets),
         out_shape=(
             block_shape,
             keys_shape,
@@ -573,7 +579,7 @@
     return jnp.sum(x, axis=0, keepdims=True)
 
 
-def middle_kernel(known, *refs, count):
+def middle_kernel(known, *refs, count, offsets):
     w_refs, refs = (refs[:count], refs[count : 2 * count]), refs[2 * count :]
     ctx_ref, x_ref, grad_ref, vec_ref, bias_ref = refs[:5]
     out_ref, first_ref, gctx_ref, lefts_ref, rights_ref, sums_ref = refs[5:11]
@@ -583,11 +589,11 @@
 
     def copy(which, t, j):
         return piece_copy(
-            w_refs[which], j, known[1], 2 * width // units + t, units, w_s.at[which, t], sems.at[which, t, j]
+            w_refs[which], offsets[which], j, known[1], 2 * width // units + t, units, w_s.at[which, t], sems.at[which, t, j]
         )
 
     mix_copies = [
-        piece_copy(w_refs[1], j, known[1], 1, width, mix_ref, mix_sems.at[j]) for j in range(count)
+        piece_copy(w_refs[1], offsets[1], j, known[1], 1, width, mix_ref, mix_sems.at[j]) for j in range(count)
     ]
     for mix_copy in mix_copies:
         mix_copy.start()
@@ -659,6 +665,7 @@
     rows, width = x.shape
     parts, units = bias.shape
     count = len(pieces[0])
+    pieces, offsets = split_pieces(pieces)
     vmem = pl.BlockSpec(memory_space=pltpu.VMEM)
     shapes = [
         ((rows, width), BF),
@@ -669,7 +676,7 @@
         ((6 + parts, width), F32),
     ]
     return pl.pallas_call(
-        partial(middle_kernel, count=count),
+        partial(middle_kernel, count=count, offsets=offsets),
         out_shape=tuple(jax.ShapeDtypeStruct(*s) for s in shapes),
         in_specs=[pl.BlockSpec(memory_space=pltpu.SMEM)] + [pl.BlockSpec(memory_space=pl.ANY)] * (2 * count) + [vmem] * 5,
         out_specs=[vmem] * len(shapes),
@@ -730,6 +737,37 @@
         cost_estimate=pl.CostEstimate(flops=FEW, bytes_accessed=FEW, transcendentals=0),
         name="ffn_grads",
     )(place, lefts, rights)
+
+
+def finish_kernel(*refs, r):
+    terms, refs = refs[:4], refs[4:]
+    total = sum(t[...].astype(F32) for t in terms)
+    for m in range(3):
+        refs[m][...] = total[m * r : (m + 1) * r]
+    base = 3 * r
+
+    def row(*at):
+        return jnp.concatenate([total[base + i : base + i + 1] for i in at], axis=1)[0]
+
+    for w in range(2):
+        refs[3 + w][...] = row(*(2 * i + w for i in range(4)))
+    for j in range(6):
+        refs[5 + j][...] = row(*(8 + 10 * i + j for i in range(4)))
+    refs[11][...] = row(*(8 + 10 * i + j for j in range(6, 10) for i in range(4)))
+
+
+def finish(terms, r, width, units):
+    cols = terms[0].shape[1]
+    shapes = [(r, cols)] * 3 + [(width,)] * 8 + [(4 * units,)]
+    vmem = pl.BlockSpec(memory_space=pltpu.VMEM)
+    return pl.pallas_call(
+        partial(finish_kernel, r=r),
+        out_shape=tuple(jax.ShapeDtypeStruct(x, F32) for x in shapes),
+        in_specs=[vmem] * 4,
+        out_specs=[vmem] * len(shapes),
+        cost_estimate=pl.CostEstimate(flops=FEW, bytes_accessed=FEW, transcendentals=0),
+        name="finish",
+    )(*terms)
 
 
 def on_device(
@@ -790,64 +828,45 @@
     w_slots = (shard, w_a, w_c, w_b)
     x_a, x_below, x_above = line_first(after(tokens, w_c))
 
-    def half(first, last):
-        line = [w[0][:, m * cols : (m + 1) * cols] for m in (first, first + 1) for w in w_slots]
-        return jnp.concatenate(line + [w[last] for w in w_slots], axis=1)
-
-    own = (half(0, 1), half(2, 2))
+    line = []
+    for first, last in ((0, 1), (2, 2)):
+        line += [w[0][:, m * cols : (m + 1) * cols] for m in (first, first + 1) for w in w_slots]
+        line += [w[last] for w in w_slots]
+    own = jnp.concatenate(line, axis=1)
+    wide = own.shape[1] // 2
     bits = outer_bits()
-    orders = (bits, bits[::-1])
-    held = [{0: own[0]}, {0: own[1]}]
-    passed = []
-
-    def pass_on(step):
-        arrived = []
-        for i in range(2):
-            bit = orders[i][step]
-            for place in sorted(held[i]):
-                got = lax.ppermute(held[i][place], "fsdp", partner(bit))
-                arrived.append((i, place | (bit >> 1), got))
-        return arrived
-
-    def keep(arrived, *gate):
-        values = after(tuple(a[2] for a in arrived), *gate)
-        for (i, place, _), value in zip(arrived, values):
-            held[i][place] = value
-        passed.append(values)
-
-    def to_partner(values, *gate):
-        return after(tuple(lax.ppermute(v, "fsdp", partner(1)) for v in values), *gate)
-
-    first = pass_on(0)
-    direct = []
+
+    def over(block, bit):
+        return lax.ppermute(block, "fsdp", partner(bit))
+
     if len(bits) == 2:
-        direct = [
-            (i, orders[i][1] >> 1, lax.ppermute(own[i], "fsdp", partner(orders[i][1]))) for i in range(2)
+        beside = [over(own, bit) for bit in bits]
+        far_own = over(own, 1)
+        x_c = line_second(*after((x_below, x_above), far_own))
+        beside = after(beside, x_a, x_c)
+        across = [over(beside[0][:, :wide], bits[1]), over(beside[1][:, wide:], bits[0])]
+        far_beside = [over(b, 1) for b in beside]
+        x_b = line_third(x_c, x_below, *far_beside)
+        far_across = [over(a, 1) for a in across]
+        pieces = [
+            [
+                piece
+                for o, b, a in ((own, beside, across), (far_own, far_beside, far_across))
+                for piece in ((o, i * wide), (b[0], i * wide), (b[1], i * wide), (a[i], 0))
+            ]
+            for i in range(2)
         ]
-    far_own = to_partner(own)
-    keep(first, x_a)
-    x_c = line_second(*after((x_below, x_above), *far_own))
-    if direct:
-        forwarded = [
-            (i, 3, lax.ppermute(held[i][orders[i][0] >> 1], "fsdp", partner(orders[i][1]))) for i in range(2)
-        ]
-        far_first = to_partner(passed[0])
-        keep(direct, x_c, *far_own)
-        x_b = line_third(x_c, x_below, *far_first)
-        far_direct = to_partner(passed[1])
-        keep(forwarded)
-        far_last = to_partner(passed[2])
-        far = [{0: far_own[i], orders[i][0] >> 1: far_first[i]} for i in range(2)]
-        for i in range(2):
-            far[i][orders[i][1] >> 1], far[i][3] = far_direct[i], far_last[i]
     else:
+        x_c = line_second(x_below, x_above)
         x_b = line_third(x_c, x_below)
-        for step in range(1, len(bits)):
-            keep(pass_on(step))
-        far = [dict(zip(sorted(h), to_partner([h[p] for p in sorted(h)]))) for h in held]
-    pieces = [[h[p] for h in (near, away) for p in sorted(near)] for near, away in zip(held, far)]
+        held = {0: after(own, x_a)}
+        for bit in bits:
+            held.update({place | (bit >> 1): over(block, bit) for place, block in sorted(held.items())})
+        near = [held[p] for p in sorted(held)]
+        far = [over(block, 1) for block in near]
+        pieces = [[(block, i * wide) for block in near + far] for i in range(2)]
     if r % 16:
-        pieces = [[assembled(p)] for p in pieces]
+        pieces = [[(assembled([p[0][:, p[1] : p[1] + wide] for p in half]), 0)] for half in pieces]
 
     xs = (tokens, x_a, x_c, x_b)
     q, k, v, ctx, lse, w_all = attend_forward(xs, pieces, shifts, seg, where)
@@ -957,32 +976,28 @@
     late = jnp.stack(
         [jnp.concatenate([late[: 3 * r, i * cols : (i + 1) * cols], below]) for i in range(4)]
     )
-    late = total(late[0], spread(late, goals))
+    *late, qb, vb, b0, b1, b2, b3, b4, b5, up_sums = finish((late[0], *spread(late, goals)), r, width, units)
     early = total(early_own, early)
     tokens_grad = dx_own + from_below.astype(F32) + from_above.astype(F32)
-    qv = late[3 * r : 3 * r + 8].reshape(4, 2, cols).transpose(1, 0, 2).reshape(2, width)
-    sums = late[3 * r + 8 :].reshape(4, count - 2, cols).transpose(1, 0, 2).reshape(count - 2, width)
-    up_sums = sums[6:].reshape(-1)
-    late = late[: 3 * r].reshape(3, r, cols)
 
     return (
         layer_out,
         tokens_grad,
         late[0],
-        qv[0],
+        qb,
         late[1],
         late[2],
-        qv[1],
+        vb,
         early[:, 2 * units :].T,
-        sums[0],
-        sums[1],
-        sums[2],
+        b0,
+        b1,
+        b2,
         early[:, units : 2 * units],
         up_sums,
         early[:, :units].T,
-        sums[3],
-        sums[4],
-        sums[5],
+        b3,
+        b4,
+        b5,
     )
 
 

time: 402 us -> 408 us (1.015)
  Pallas kernels: 126 us -> 147 us
  starting transfers between devices: 86.3 us -> 75.1 us
  local copies, waits for them, and re-layouts: 36.3 us -> 30.4 us
    ppermute x14 -> x9, waiting for transfers between devices: 48.5 us -> 19.3 us  [over(): return lax.ppermute(block, 'fsdp', partner(bit))]
    ppermute x2, waiting for transfers between devices: 4.04 us -> 22.4 us  [line_second(): above2 = lax.ppermute(above, 'tensor', [(2, 1), (1, 0)])]
    ppermute x2, starting transfers between devices: 14.5 us -> 0.49 us  [on_device(): got = lax.ppermute(sent, 'fsdp', partner(1))]
    pallas_call x2 -> x3, Pallas kernels: 57.6 us -> 68.2 us  [the longest x1 37.1 us: attend_forward(): pl.pallas_call(partial(forward_kernel, slots=slots, count=count, offsets=...]
    ppermute x6, waiting for transfers between devices: 28.4 us -> 38.5 us  [spread(): lax.ppermute(block, 'tensor', [(i, (i + shift) % 4) for i in range(4)])]
    pallas_call x2, Pallas kernels: 42.2 us -> 52 us  [attend_backward(): pl.pallas_call(partial(backward_kernel, slots=slots, first=first, last=la...]
    ppermute x1, starting transfers between devices: 15.1 us -> 23.9 us  [on_device(): r1 = lax.ppermute(dx_b, 'tensor', [(0, 1), (3, 2)])]
    ppermute x1, waiting for transfers between devices: 12.7 us -> 4.15 us  [on_device(): from_above = lax.ppermute(down_x, 'tensor', [(1, 0), (2, 1), (3, 2)])]
  transfers between devices with their start and end apart: 42 -> 37, of which waited for: 16 -> 16; matrix products, arithmetic and copies ran while one was open for 11% -> 11% of each run, Pallas kernels for 14% -> 16%
where the time goes in v2:
time: 408 us; the launch traced here: 404 us
  Pallas kernels  147 us (36%)
  waiting for transfers between devices  118 us (29%)
  starting transfers between devices  75.1 us (18%)
  other arithmetic  32.8 us (8%)
  local copies, waits for them, and re-layouts  30.4 us (7%)
    pallas_call x2, Pallas kernels, attend_backward(): pl.pallas_call(partial(backward_kernel, slots=slots, first=first, last=la...  52 us
    ppermute x6, waiting for transfers between devices, spread(): lax.ppermute(block, 'tensor', [(i, (i + shift) % 4) for i in range(4)])  38.5 us
    pallas_call x1, Pallas kernels, attend_forward(): pl.pallas_call(partial(forward_kernel, slots=slots, count=count, offsets=...  37.1 us
    pallas_call x1, Pallas kernels, middle(): pl.pallas_call(partial(middle_kernel, count=count, offsets=offsets), out_...  29.1 us
    ppermute x1, starting transfers between devices, on_device(): r1 = lax.ppermute(dx_b, 'tensor', [(0, 1), (3, 2)])  23.9 us
    ppermute x2, waiting for transfers between devices, line_second(): above2 = lax.ppermute(above, 'tensor', [(2, 1), (1, 0)])  22.4 us
    ppermute x2, waiting for transfers between devices, line_first(): above = lax.ppermute(own, 'tensor', [(1, 0), (2, 1), (3, 2)])  21.6 us
    ppermute x9, waiting for transfers between devices, over(): return lax.ppermute(block, 'fsdp', partner(bit))  19.3 us
  transfers between devices with their start and end apart: 37, of which 16 were waited for; matrix products, arithmetic and copies ran while one was open for 11% of the time, Pallas kernels for 16%

profile of v2, /device:TPU:0, one launch (start us, length us, event | category | flops | bytes accessed | tf_op | source)
XLA Modules:
  0.0 404.2 jit_solution(5373495328785214991)
XLA Ops:
  4.9 5.6 %collective-permute-start.1 = (bf16[3,96,768]{2,1,0:T(8,128)(2,1)S(1)}, bf16[3,96,768]{2,1,0:T(8,128)(2,1)S(1)}, u32[]{:S(2)}, u32[]{:S(2)}) collective-permute-start(bf16[3,96,768]{2,1,0:T(8,128)(2,1)S(1)} %pad_maximum_fusion.2), channel_id=1, source_target_pairs={{0,1},{1,2},{2,3},{4,5},{5,6},{6,7},{8,9},{9,10},{10,11},{12,13},{... | collective-permute-start | bytes 1327112 | tf_op jit(solution)/shard_map/ppermute | solution.py:37
  10.5 8.2 %collective-permute-done = bf16[3,96,768]{2,1,0:T(8,128)(2,1)S(1)} collective-permute-done((bf16[3,96,768]{2,1,0:T(8,128)(2,1)S(1)}, bf16[3,96,768]{2,1,0:T(8,128)(2,1)S(1)}, u32[]{:S(2)}, u32[]{:S(2)}) %collective-permute-start) | collective-permute-done | bytes 442400 | tf_op jit(solution)/shard_map/ppermute | solution.py:38
  27.9 4.0 collective-permute-done.2
  34.1 10.2 %collective-permute-done.4 = bf16[3,96,768]{2,1,0:T(8,128)(2,1)S(1)} collective-permute-done((bf16[3,96,768]{2,1,0:T(8,128)(2,1)S(1)}, bf16[3,96,768]{2,1,0:T(8,128)(2,1)S(1)}, u32[]{:S(2)}, u32[]{:S(2)}) %collective-permute-start.4) | collective-permute-done | bytes 442400 | tf_op jit(solution)/shard_map/ppermute | solution.py:50
  45.4 2.0 concatenate.57.refs_8_.refs_16_.refs_0_
  48.8 4.6 %collective-permute-start.8 = (bf16[512,768]{1,0:T(8,128)(2,1)}, bf16[512,768]{1,0:T(8,128)(2,1)S(1)}, u32[]{:S(2)}, u32[]{:S(2)}) collective-permute-start(bf16[512,768]{1,0:T(8,128)(2,1)} %refs_0_.3), channel_id=1, source_target_pairs={{0,1},{1,2},{2,3},{4,5},{5,6},{6,7},{8,9},{9,10},{10,11},{12,13},{... | collective-permute-start | bytes 2359304 | tf_op jit(solution)/shard_map/ppermute | solution.py:37
  54.6 1.5 collective-permute-start.6
  56.1 13.4 %collective-permute-done.7 = bf16[512,768]{1,0:T(8,128)(2,1)S(1)} collective-permute-done((bf16[512,768]{1,0:T(8,128)(2,1)}, bf16[512,768]{1,0:T(8,128)(2,1)S(1)}, u32[]{:S(2)}, u32[]{:S(2)}) %collective-permute-start.7) | collective-permute-done | bytes 786464 | tf_op jit(solution)/shard_map/ppermute | solution.py:38
  75.2 18.4 %collective-permute-done.10 = bf16[512,768]{1,0:T(8,128)(2,1)S(1)} collective-permute-done((bf16[512,768]{1,0:T(8,128)(2,1)S(1)}, bf16[512,768]{1,0:T(8,128)(2,1)S(1)}, u32[]{:S(2)}, u32[]{:S(2)}) %collective-permute-start.10) | collective-permute-done | bytes 786464 | tf_op jit(solution)/shard_map/ppermute | solution.py:44
  95.5 1.6 collective-permute-start.12
  100.8 16.4 %collective-permute-done.12.refs_11_.refs_3_ = bf16[96,4608]{1,0:T(8,128)(2,1)} collective-permute-done((bf16[96,4608]{1,0:T(8,128)(2,1)S(1)}, bf16[96,4608]{1,0:T(8,128)(2,1)}, u32[]{:S(2)}, u32[]{:S(2)}) %collective-permute-start.12) | collective-permute-done | bytes 884768 | tf_op jit(solution)/shard_map/ppermute | solution.py:840
  117.2 2.5 collective-permute-done.16.refs_19_.refs_11_
  122.2 2.7 broadcast_select_fusion.refs_3_.refs_1_
  125.0 37.1 %attend_forward.1 = (bf16[512,768]{1,0:T(8,128)(2,1)}, bf16[2048,768]{1,0:T(8,128)(2,1)}, bf16[2048,768]{1,0:T(8,128)(2,1)}, bf16[512,768]{1,0:T(8,128)(2,1)}, f...) custom-call(s32[2048]{0:T(1024)} %bitcast.122, s32[7]{0:T(128)} %concatenate.52.where, bf16[512,768]{1,0:T(8,128)(2,1)} %refs_0_.3, ...), custom_call_target="tpu_custom_call" | custom-call | flops 1000 | bytes 1000 | tf_op jit(solution)/shard_map/attend_forward/pallas_call | solution.py:285
  162.1 29.1 %middle.1 = (bf16[512,768]{1,0:T(8,128)(2,1)}, f32[512,768]{1,0:T(8,128)}, bf16[512,768]{1,0:T(8,128)(2,1)}, bf16[3,512,768]{2,1,0:T(8,128)(2,1)}, bf16[512,6912]{1,0:T(8,128)(2,1)}, /*index=5*/f32[10,768]{1,0:T(8,128)}) custom-call(s32[6]{0:T(128)} %concatenate.53.known, bf16[96,9216]{1,0:T(8,128)(2,1)} %copy-done, bf16[96,9216]{1,0:T(8,128)(2,1)} %copy-done.1, ...), custom_call_target="tpu_custom_call" | custom-call | flops 1000 | bytes 1000 | tf_op jit(solution)/shard_map/middle/pallas_call | solution.py:678
  191.3 13.7 %ffn_grads.1 = (bf16[384,6912]{1,0:T(8,128)(2,1)}, bf16[384,6912]{1,0:T(8,128)(2,1)}) custom-call(s32[1]{0:T(128)} %bitcast.5.place, bf16[3,512,768]{2,1,0:T(8,128)(2,1)} %get-tuple-element.109.left_ref, bf16[512,6912]{1,0:T(8,128)(2,1)} %get-tuple-element.110.right_ref), custom_call_target="tpu_custom_call" | custom-call | flops 1000 | bytes 1000 | tf_op jit(solution)/shard_map/ffn_grads/pallas_call | solution.py:724
  205.4 31.9 %attend_backward.2 = (bf16[1536,768]{1,0:T(8,128)(2,1)}, bf16[1536,768]{1,0:T(8,128)(2,1)}, f32[768,512]{1,0:T(8,128)}, bf16[1536,768]{1,0:T(8,128)(2,1)}) custom-call(s32[2048]{0:T(1024)} %bitcast.123, s32[7]{0:T(128)} %concatenate.52.where, bf16[512,768]{1,0:T(8,128)(2,1)} %get-tuple-element.107.refs_0_, bf16[512,768]{1,0:T(8,128)(2,1)} %get-tuple-element.112.refs_1_, ...), custom_call_target="tpu_custom_call" | custom-call | flops 1000 | bytes 1000 | tf_op jit(solution)/shard_map/attend_backward/pallas_call | solution.py:463
  237.3 1.8 slice.247
  239.2 5.3 %convert_add_fusion = (f32[192,3840]{1,0:T(8,128)S(1)}, bf16[192,3840]{1,0:T(8,128)(2,1)}) fusion(bf16[384,6912]{1,0:T(8,128)(2,1)} %collective-permute-done.19, bf16[384,6912]{1,0:T(8,128)(2,1)} %get-tuple-element.119), kind=kLoop, calls=%fused_computation.2 | loop fusion | flops 5160960 | bytes 10321920 | tf_op jit(solution)/shard_map/add | solution.py:915
  244.5 1.8 slice.249
  246.4 1.7 fusion.5
  248.1 2.1 slice.246
  250.3 23.9 %collective-permute-start.20 = (bf16[512,768]{1,0:T(8,128)(2,1)}, bf16[512,768]{1,0:T(8,128)(2,1)}, u32[]{:S(2)}, u32[]{:S(2)}) collective-permute-start(bf16[512,768]{1,0:T(8,128)(2,1)} %slice.246), channel_id=1, source_target_pairs={{0,1},{3,2},{4,5},{7,6},{8,9},{11,10},{12,13},{15,14},{16,17},{19,... | collective-permute-start | bytes 2359304 | tf_op jit(solution)/shard_map/ppermute | solution.py:892
  274.2 20.0 %attend_backward.3 = (bf16[512,768]{1,0:T(8,128)(2,1)}, bf16[512,768]{1,0:T(8,128)(2,1)}, bf16[512,768]{1,0:T(8,128)(2,1)}, f32[512,768]{1,0:T(8,128)}) custom-call(s32[2048]{0:T(1024)} %bitcast.124, s32[7]{0:T(128)} %concatenate.52.where, bf16[512,768]{1,0:T(8,128)(2,1)} %get-tuple-element.107.refs_0_, bf16[512,768]{1,0:T(8,128)(2,1)} %get-tuple-element.112.refs_1_, ...), custom_call_target="tpu_custom_call" | custom-call | flops 1000 | bytes 1000 | tf_op jit(solution)/shard_map/attend_backward/pallas_call | solution.py:463
  294.2 2.5 add_convert_fusion.4
  296.8 2.1 collective-permute-start.21
  298.9 1.6 collective-permute-start.22
  300.5 1.8 add_convert_fusion.1
  303.5 1.8 fusion
  305.3 2.1 collective-permute-start.29
  309.6 12.7 %attn_grads.1 = (bf16[4,304,768]{2,1,0:T(8,128)(2,1)}, f32[4,304,768]{2,1,0:T(8,128)}) custom-call(s32[1]{0:T(128)} %slice.255.core_ref, bf16[512,768]{1,0:T(8,128)(2,1)} %refs_0_.3, bf16[512,768]{1,0:T(8,128)(2,1)} %broadcast_select_fusion.refs_3_.refs_1_, bf16[512,768]{1,0:T(8,128)(2,1)} %broadcast_select_fusion.1.refs_2_, ...), custom_call_target="tpu_custom_call" | custom-call | flops 1000 | bytes 1000 | tf_op jit(solution)/shard_map/attn_grads/pallas_call | solution.py:541
  322.4 3.2 fusion.1
  325.6 3.1 collective-permute-start.25
  332.9 1.8 copy-done.11
  334.8 1.6 add_convert_fusion
  336.4 3.6 all-to-all-start
  340.3 2.7 collective-permute-start.30
  343.0 3.6 collective-permute-start.31
  347.1 4.2 %collective-permute-done.26 = bf16[512,768]{1,0:T(8,128)(2,1)} collective-permute-done((bf16[512,768]{1,0:T(8,128)(2,1)}, bf16[512,768]{1,0:T(8,128)(2,1)}, u32[]{:S(2)}, u32[]{:S(2)}) %collective-permute-start.26) | collective-permute-done | bytes 786464 | tf_op jit(solution)/shard_map/ppermute | solution.py:946
  351.3 2.8 convert_add_fusion.2
  354.1 7.0 %collective-permute-done.30 = bf16[96,1728]{1,0:T(8,128)(2,1)S(1)} collective-permute-done((bf16[96,1728]{1,0:T(8,128)(2,1)S(1)}, bf16[96,1728]{1,0:T(8,128)(2,1)S(1)}, u32[]{:S(2)}, u32[]{:S(2)}) %collective-permute-start.30) | collective-permute-done | bytes 331808 | tf_op jit(solution)/shard_map/ppermute | solution.py:72
  361.0 4.0 collective-permute-done.31
  365.0 16.0 %collective-permute-done.32 = bf16[96,1728]{1,0:T(8,128)(2,1)S(1)} collective-permute-done((bf16[96,1728]{1,0:T(8,128)(2,1)S(1)}, bf16[96,1728]{1,0:T(8,128)(2,1)S(1)}, u32[]{:S(2)}, u32[]{:S(2)}) %collective-permute-start.32) | collective-permute-done | bytes 331808 | tf_op jit(solution)/shard_map/ppermute | solution.py:72
  385.2 3.8 collective-permute-start.34
  389.9 4.4 %collective-permute-done.33.refs_1_ = bf16[336,192]{1,0:T(8,128)(2,1)S(1)} collective-permute-done((bf16[336,192]{1,0:T(8,128)(2,1)S(1)}, bf16[336,192]{1,0:T(8,128)(2,1)S(1)}, u32[]{:S(2)}, u32[]{:S(2)}) %collective-permute-start.33) | collective-permute-done | bytes 129056 | tf_op jit(solution)/shard_map/ppermute | solution.py:72
  394.3 2.4 collective-permute-done.34.refs_2_
  396.7 4.6 %collective-permute-done.35.refs_3_ = bf16[336,192]{1,0:T(8,128)(2,1)S(1)} collective-permute-done((bf16[336,192]{1,0:T(8,128)(2,1)S(1)}, bf16[336,192]{1,0:T(8,128)(2,1)S(1)}, u32[]{:S(2)}, u32[]{:S(2)}) %collective-permute-start.35) | collective-permute-done | bytes 129056 | tf_op jit(solution)/shard_map/ppermute | solution.py:72
  402.1 1.9 finish.1
  (176 shorter events, 47.0 us)
Async XLA Ops:
  0.7 26.3 %copy-start.28 = (f32[768]{0:T(1024)S(1)}, f32[768]{0:T(1024)}, u32[]{:S(2)}) copy-start(f32[768]{0:T(1024)} %param.34) | copy-start | bytes 9220
  0.7 26.3 %copy-start.29 = (f32[768]{0:T(1024)S(1)}, f32[768]{0:T(1024)}, u32[]{:S(2)}) copy-start(f32[768]{0:T(1024)} %param.26) | copy-start | bytes 9220
  0.7 26.3 %copy-start.30 = (f32[768]{0:T(1024)S(1)}, f32[768]{0:T(1024)}, u32[]{:S(2)}) copy-start(f32[768]{0:T(1024)} %param.27) | copy-start | bytes 9220
  0.7 26.3 %copy-start.31 = (f32[768]{0:T(1024)S(1)}, f32[768]{0:T(1024)}, u32[]{:S(2)}) copy-start(f32[768]{0:T(1024)} %param.28) | copy-start | bytes 9220
  3.6 15.1 %collective-permute-start = (bf16[3,96,768]{2,1,0:T(8,128)(2,1)S(1)}, bf16[3,96,768]{2,1,0:T(8,128)(2,1)S(1)}, u32[]{:S(2)}, u32[]{:S(2)}) collective-permute-start(bf16[3,96,768]{2,1,0:T(8,128)(2,1)S(1)} %pad_maximum_fusion.2), channel_id=1, source_target_pairs={{1,0},{2,1},{3,2},{5,4},{6,5},{7,6},{9,8},{10,9},{11,10},{13,12},{... | collective-permute-start | bytes 1327112 | tf_op jit(solution)/shard_map/ppermute | solution.py:38
  4.9 15.1 %collective-permute-start.1 = (bf16[3,96,768]{2,1,0:T(8,128)(2,1)S(1)}, bf16[3,96,768]{2,1,0:T(8,128)(2,1)S(1)}, u32[]{:S(2)}, u32[]{:S(2)}) collective-permute-start(bf16[3,96,768]{2,1,0:T(8,128)(2,1)S(1)} %pad_maximum_fusion.2), channel_id=1, source_target_pairs={{0,1},{1,2},{2,3},{4,5},{5,6},{6,7},{8,9},{9,10},{10,11},{12,13},{... | collective-permute-start | bytes 1327112 | tf_op jit(solution)/shard_map/ppermute | solution.py:37
  18.7 13.2 %collective-permute-start.2 = (bf16[3,96,768]{2,1,0:T(8,128)(2,1)S(1)}, bf16[3,96,768]{2,1,0:T(8,128)(2,1)S(1)}, u32[]{:S(2)}, u32[]{:S(2)}) collective-permute-start(bf16[3,96,768]{2,1,0:T(8,128)(2,1)S(1)} %collective-permute-done), channel_id=1, source_target_pairs={{2,1},{1,0},{6,5},{5,4},{10,9},{9,8},{14,13},{13,12},{18,17},{17,1... | collective-permute-start | bytes 1327112 | tf_op jit(solution)/shard_map/ppermute | solution.py:44
  20.0 11.9 %collective-permute-start.3 = (bf16[3,96,768]{2,1,0:T(8,128)(2,1)S(1)}, bf16[3,96,768]{2,1,0:T(8,128)(2,1)S(1)}, u32[]{:S(2)}, u32[]{:S(2)}) collective-permute-start(bf16[3,96,768]{2,1,0:T(8,128)(2,1)S(1)} %collective-permute-done.1), channel_id=1, source_target_pairs={{1,2},{2,3},{5,6},{6,7},{9,10},{10,11},{13,14},{14,15},{17,18},{18... | collective-permute-start | bytes 1327112 | tf_op jit(solution)/shard_map/ppermute | solution.py:43
  21.4 23.0 %copy-start.13 = (s32[1,2048]{1,0:T(1,128)}, s32[1,2048]{1,0:T(1,128)S(1)}, u32[]{:S(2)}) copy-start(s32[1,2048]{1,0:T(1,128)S(1)} %compare_select_fusion.refs_4_.refs_5_.refs_6_.refs_7_.refs_26_.refs_13_.refs_14_.refs_15_.refs_9_) | copy-start | bytes 24580
  32.0 12.3 %collective-permute-start.4 = (bf16[3,96,768]{2,1,0:T(8,128)(2,1)S(1)}, bf16[3,96,768]{2,1,0:T(8,128)(2,1)S(1)}, u32[]{:S(2)}, u32[]{:S(2)}) collective-permute-start(bf16[3,96,768]{2,1,0:T(8,128)(2,1)S(1)} %broadcast_select_fusion.4), channel_id=1, source_target_pairs={{1,0},{2,3},{5,4},{6,7},{9,8},{10,11},{13,12},{14,15},{17,16},{18,... | collective-permute-start | bytes 1327112 | tf_op jit(solution)/shard_map/ppermute | solution.py:50
  47.4 47.2 %copy-start = (bf16[96,9216]{1,0:T(8,128)(2,1)}, bf16[96,9216]{1,0:T(8,128)(2,1)S(1)}, u32[]{:S(2)}) copy-start(bf16[96,9216]{1,0:T(8,128)(2,1)S(1)} %concatenate.57.refs_8_.refs_16_.refs_0_) | copy-start | bytes 5308420
  47.4 23.4 %collective-permute-start.9 = (bf16[96,9216]{1,0:T(8,128)(2,1)S(1)}, bf16[96,9216]{1,0:T(8,128)(2,1)S(1)}, u32[]{:S(2)}, u32[]{:S(2)}) collective-permute-start(bf16[96,9216]{1,0:T(8,128)(2,1)S(1)} %concatenate.57.refs_8_.refs_16_.refs_0_), channel_id=1, source_target_pairs={{0,4},{4,0},{8,12},{12,8},{16,20},{20,16},{24,28},{28,24},{1,5},{5... | collective-permute-start | bytes 5308424 | tf_op jit(solution)/shard_map/ppermute | solution.py:840
  47.5 22.0 %collective-permute-start.7 = (bf16[512,768]{1,0:T(8,128)(2,1)}, bf16[512,768]{1,0:T(8,128)(2,1)S(1)}, u32[]{:S(2)}, u32[]{:S(2)}) collective-permute-start(bf16[512,768]{1,0:T(8,128)(2,1)} %refs_0_.3), channel_id=1, source_target_pairs={{1,0},{2,1},{3,2},{5,4},{6,5},{7,6},{9,8},{10,9},{11,10},{13,12},{... | collective-permute-start | bytes 2359304 | tf_op jit(solution)/shard_map/ppermute | solution.py:38
  48.8 22.0 %collective-permute-start.8 = (bf16[512,768]{1,0:T(8,128)(2,1)}, bf16[512,768]{1,0:T(8,128)(2,1)S(1)}, u32[]{:S(2)}, u32[]{:S(2)}) collective-permute-start(bf16[512,768]{1,0:T(8,128)(2,1)} %refs_0_.3), channel_id=1, source_target_pairs={{0,1},{1,2},{2,3},{4,5},{5,6},{6,7},{8,9},{9,10},{10,11},{12,13},{... | collective-permute-start | bytes 2359304 | tf_op jit(solution)/shard_map/ppermute | solution.py:37
  53.4 41.2 %collective-permute-start.5 = (bf16[96,9216]{1,0:T(8,128)(2,1)S(1)}, bf16[96,9216]{1,0:T(8,128)(2,1)S(1)}, u32[]{:S(2)}, u32[]{:S(2)}) collective-permute-start(bf16[96,9216]{1,0:T(8,128)(2,1)S(1)} %concatenate.57.refs_8_.refs_16_.refs_0_), channel_id=1, source_target_pairs={{0,8},{4,12},{8,0},{12,4},{16,24},{20,28},{24,16},{28,20},{1,9},{5... | collective-permute-start | bytes 5308424 | tf_op jit(solution)/shard_map/ppermute | solution.py:840
  54.6 40.3 %collective-permute-start.6 = (bf16[96,9216]{1,0:T(8,128)(2,1)S(1)}, bf16[96,9216]{1,0:T(8,128)(2,1)}, u32[]{:S(2)}, u32[]{:S(2)}) collective-permute-start(bf16[96,9216]{1,0:T(8,128)(2,1)S(1)} %concatenate.57.refs_8_.refs_16_.refs_0_), channel_id=1, source_target_pairs={{0,16},{4,20},{8,24},{12,28},{16,0},{20,4},{24,8},{28,12},{1,17},{... | collective-permute-start | bytes 5308424 | tf_op jit(solution)/shard_map/ppermute | solution.py:840
  70.8 28.5 %copy-start.12 = (bf16[512,768]{1,0:T(8,128)(2,1)}, bf16[512,768]{1,0:T(8,128)(2,1)S(1)}, u32[]{:S(2)}) copy-start(bf16[512,768]{1,0:T(8,128)(2,1)S(1)} %collective-permute-done.8) | copy-start | bytes 2359300
  72.2 21.5 %collective-permute-start.10 = (bf16[512,768]{1,0:T(8,128)(2,1)S(1)}, bf16[512,768]{1,0:T(8,128)(2,1)S(1)}, u32[]{:S(2)}, u32[]{:S(2)}) collective-permute-start(bf16[512,768]{1,0:T(8,128)(2,1)S(1)} %collective-permute-done.7), channel_id=1, source_target_pairs={{2,1},{1,0},{6,5},{5,4},{10,9},{9,8},{14,13},{13,12},{18,17},{17,1... | collective-permute-start | bytes 2359304 | tf_op jit(solution)/shard_map/ppermute | solution.py:44
  73.4 20.2 %collective-permute-start.11 = (bf16[512,768]{1,0:T(8,128)(2,1)S(1)}, bf16[512,768]{1,0:T(8,128)(2,1)S(1)}, u32[]{:S(2)}, u32[]{:S(2)}) collective-permute-start(bf16[512,768]{1,0:T(8,128)(2,1)S(1)} %collective-permute-done.8), channel_id=1, source_target_pairs={{1,2},{2,3},{5,6},{6,7},{9,10},{10,11},{13,14},{14,15},{17,18},{18... | collective-permute-start | bytes 2359304 | tf_op jit(solution)/shard_map/ppermute | solution.py:43
  94.9 27.3 %collective-permute-start.13 = (bf16[96,9216]{1,0:T(8,128)(2,1)S(1)}, bf16[96,9216]{1,0:T(8,128)(2,1)S(1)}, u32[]{:S(2)}, u32[]{:S(2)}) collective-permute-start(bf16[96,9216]{1,0:T(8,128)(2,1)S(1)} %collective-permute-done.5.refs_9_.refs_17_.refs_1_), channel_id=1, source_target_pairs={{0,4},{4,0},{8,12},{12,8},{16,20},{20,16},{24,28},{28,24},{1,5},{5... | collective-permute-start | bytes 5308424 | tf_op jit(solution)/shard_map/ppermute | solution.py:840
  94.9 27.3 %collective-permute-start.14 = (bf16[96,9216]{1,0:T(8,128)(2,1)}, bf16[96,9216]{1,0:T(8,128)(2,1)}, u32[]{:S(2)}, u32[]{:S(2)}) collective-permute-start(bf16[96,9216]{1,0:T(8,128)(2,1)} %collective-permute-done.6.refs_10_.refs_18_.refs_2_), channel_id=1, source_target_pairs={{0,4},{4,0},{8,12},{12,8},{16,20},{20,16},{24,28},{28,24},{1,5},{5... | collective-permute-start | bytes 5308424 | tf_op jit(solution)/shard_map/ppermute | solution.py:840
  95.5 21.7 %collective-permute-start.12 = (bf16[96,4608]{1,0:T(8,128)(2,1)S(1)}, bf16[96,4608]{1,0:T(8,128)(2,1)}, u32[]{:S(2)}, u32[]{:S(2)}) collective-permute-start(bf16[96,4608]{1,0:T(8,128)(2,1)S(1)} %slice.244), channel_id=1, source_target_pairs={{0,16},{4,20},{8,24},{12,28},{16,0},{20,4},{24,8},{28,12},{1,17},{... | collective-permute-start | bytes 2654216 | tf_op jit(solution)/shard_map/ppermute | solution.py:840
  98.3 21.4 %collective-permute-start.16 = (bf16[96,4608]{1,0:T(8,128)(2,1)S(1)}, bf16[96,4608]{1,0:T(8,128)(2,1)}, u32[]{:S(2)}, u32[]{:S(2)}) collective-permute-start(bf16[96,4608]{1,0:T(8,128)(2,1)S(1)} %slice.245), channel_id=1, source_target_pairs={{0,8},{4,12},{8,0},{12,4},{16,24},{20,28},{24,16},{28,20},{1,9},{5... | collective-permute-start | bytes 2654216 | tf_op jit(solution)/shard_map/ppermute | solution.py:840
  99.3 22.9 %collective-permute-start.18 = (bf16[512,768]{1,0:T(8,128)(2,1)}, bf16[512,768]{1,0:T(8,128)(2,1)}, u32[]{:S(2)}, u32[]{:S(2)}) collective-permute-start(bf16[512,768]{1,0:T(8,128)(2,1)} %broadcast_select_fusion.1.refs_2_), channel_id=1, source_target_pairs={{1,0},{2,3},{5,4},{6,7},{9,8},{10,11},{13,12},{14,15},{17,16},{18,... | collective-permute-start | bytes 2359304 | tf_op jit(solution)/shard_map/ppermute | solution.py:50
  117.2 7.8 %collective-permute-start.15 = (bf16[96,4608]{1,0:T(8,128)(2,1)}, bf16[96,4608]{1,0:T(8,128)(2,1)}, u32[]{:S(2)}, u32[]{:S(2)}) collective-permute-start(bf16[96,4608]{1,0:T(8,128)(2,1)} %collective-permute-done.12.refs_11_.refs_3_), channel_id=1, source_target_pairs={{0,4},{4,0},{8,12},{12,8},{16,20},{20,16},{24,28},{28,24},{1,5},{5... | collective-permute-start | bytes 2654216 | tf_op jit(solution)/shard_map/ppermute | solution.py:840
  119.7 5.3 %collective-permute-start.17 = (bf16[96,4608]{1,0:T(8,128)(2,1)}, bf16[96,4608]{1,0:T(8,128)(2,1)}, u32[]{:S(2)}, u32[]{:S(2)}) collective-permute-start(bf16[96,4608]{1,0:T(8,128)(2,1)} %collective-permute-done.16.refs_19_.refs_11_), channel_id=1, source_target_pairs={{0,4},{4,0},{8,12},{12,8},{16,20},{20,16},{24,28},{28,24},{1,5},{5... | collective-permute-start | bytes 2654216 | tf_op jit(solution)/shard_map/ppermute | solution.py:840
  205.0 34.2 %collective-permute-start.19 = (bf16[384,6912]{1,0:T(8,128)(2,1)}, bf16[384,6912]{1,0:T(8,128)(2,1)}, u32[]{:S(2)}, u32[]{:S(2)}) collective-permute-start(bf16[384,6912]{1,0:T(8,128)(2,1)} %get-tuple-element.111), channel_id=1, source_target_pairs={{0,4},{4,0},{8,12},{12,8},{16,20},{20,16},{24,28},{28,24},{1,5},{5... | collective-permute-start | bytes 15925256 | tf_op jit(solution)/shard_map/ppermute | solution.py:886
  246.3 54.2 %collective-permute-start.24 = (bf16[2,96,3840]{2,1,0:T(8,128)(2,1)}, bf16[2,96,3840]{2,1,0:T(8,128)(2,1)}, u32[]{:S(2)}, u32[]{:S(2)}) collective-permute-start(bf16[2,96,3840]{2,1,0:T(8,128)(2,1)} %bitcast.33), channel_id=1, source_target_pairs={{0,16},{4,20},{8,24},{12,28},{16,0},{20,4},{24,8},{28,12},{1,17},{... | collective-permute-start | bytes 4423688 | tf_op jit(solution)/shard_map/ppermute | solution.py:905
  248.1 52.4 %collective-permute-start.23 = (bf16[2,96,3072]{2,1,0:T(8,128)(2,1)}, bf16[2,96,3072]{2,1,0:T(8,128)(2,1)}, u32[]{:S(2)}, u32[]{:S(2)}) collective-permute-start(bf16[2,96,3072]{2,1,0:T(8,128)(2,1)} %fusion.5), channel_id=1, source_target_pairs={{0,8},{4,12},{8,0},{12,4},{16,24},{20,28},{24,16},{28,20},{1,9},{5... | collective-permute-start | bytes 3538952 | tf_op jit(solution)/shard_map/ppermute | solution.py:905
  250.3 44.0 %collective-permute-start.20 = (bf16[512,768]{1,0:T(8,128)(2,1)}, bf16[512,768]{1,0:T(8,128)(2,1)}, u32[]{:S(2)}, u32[]{:S(2)}) collective-permute-start(bf16[512,768]{1,0:T(8,128)(2,1)} %slice.246), channel_id=1, source_target_pairs={{0,1},{3,2},{4,5},{7,6},{8,9},{11,10},{12,13},{15,14},{16,17},{19,... | collective-permute-start | bytes 2359304 | tf_op jit(solution)/shard_map/ppermute | solution.py:892
  296.8 25.6 %collective-permute-start.21 = (bf16[512,768]{1,0:T(8,128)(2,1)}, bf16[512,768]{1,0:T(8,128)(2,1)}, u32[]{:S(2)}, u32[]{:S(2)}) collective-permute-start(bf16[512,768]{1,0:T(8,128)(2,1)} %add_convert_fusion.4), channel_id=1, source_target_pairs={{0,1},{3,2},{4,5},{7,6},{8,9},{11,10},{12,13},{15,14},{16,17},{19,... | collective-permute-start | bytes 2359304 | tf_op jit(solution)/shard_map/ppermute | solution.py:910
  298.9 23.5 %collective-permute-start.22 = (bf16[512,768]{1,0:T(8,128)(2,1)}, bf16[512,768]{1,0:T(8,128)(2,1)}, u32[]{:S(2)}, u32[]{:S(2)}) collective-permute-start(bf16[512,768]{1,0:T(8,128)(2,1)} %add_convert_fusion.4), channel_id=1, source_target_pairs={{1,2},{2,1},{5,6},{6,5},{9,10},{10,9},{13,14},{14,13},{17,18},{18,... | collective-permute-start | bytes 2359304 | tf_op jit(solution)/shard_map/ppermute | solution.py:911
  305.3 24.6 %collective-permute-start.29 = (bf16[96,3840]{1,0:T(8,128)(2,1)}, bf16[96,3840]{1,0:T(8,128)(2,1)}, u32[]{:S(2)}, u32[]{:S(2)}) collective-permute-start(bf16[96,3840]{1,0:T(8,128)(2,1)} %slice_bitcast_fusion.5), channel_id=1, source_target_pairs={{0,8},{4,12},{8,0},{12,4},{16,24},{20,28},{24,16},{28,20},{1,9},{5... | collective-permute-start | bytes 2211848 | tf_op jit(solution)/shard_map/ppermute | solution.py:114
  308.3 21.7 %collective-permute-start.28 = (bf16[96,3072]{1,0:T(8,128)(2,1)}, bf16[96,3072]{1,0:T(8,128)(2,1)}, u32[]{:S(2)}, u32[]{:S(2)}) collective-permute-start(bf16[96,3072]{1,0:T(8,128)(2,1)} %slice_bitcast_fusion.7), channel_id=1, source_target_pairs={{0,16},{4,20},{8,24},{12,28},{16,0},{20,4},{24,8},{28,12},{1,17},{... | collective-permute-start | bytes 1769480 | tf_op jit(solution)/shard_map/ppermute | solution.py:114
  309.6 12.8 %copy-start.10 = (bf16[1536,768]{1,0:T(8,128)(2,1)S(1)}, bf16[1536,768]{1,0:T(8,128)(2,1)}, u32[]{:S(2)}) copy-start(bf16[1536,768]{1,0:T(8,128)(2,1)} %get-tuple-element.118) | copy-start | bytes 7077892
  322.3 7.7 %copy-start.9 = (bf16[2,96,3840]{2,1,0:T(8,128)(2,1)S(1)}, bf16[2,96,3840]{2,1,0:T(8,128)(2,1)}, u32[]{:S(2)}) copy-start(bf16[2,96,3840]{2,1,0:T(8,128)(2,1)} %copy-done.8) | copy-start | bytes 4423684
  322.3 10.7 %collective-permute-start.27 = (bf16[4,304,768]{2,1,0:T(8,128)(2,1)}, bf16[4,304,768]{2,1,0:T(8,128)(2,1)S(1)}, u32[]{:S(2)}, u32[]{:S(2)}) collective-permute-start(bf16[4,304,768]{2,1,0:T(8,128)(2,1)} %get-tuple-element.134), channel_id=1, source_target_pairs={{0,4},{4,0},{8,12},{12,8},{16,20},{20,16},{24,28},{28,24},{1,5},{5... | collective-permute-start | bytes 5603336 | tf_op jit(solution)/shard_map/ppermute | solution.py:940
  325.6 21.6 %collective-permute-start.25 = (bf16[512,768]{1,0:T(8,128)(2,1)}, bf16[512,768]{1,0:T(8,128)(2,1)}, u32[]{:S(2)}, u32[]{:S(2)}) collective-permute-start(bf16[512,768]{1,0:T(8,128)(2,1)} %get-tuple-element.172), channel_id=1, source_target_pairs={{0,1},{1,2},{2,3},{4,5},{5,6},{6,7},{8,9},{9,10},{10,11},{12,13},{... | collective-permute-start | bytes 2359304 | tf_op jit(solution)/shard_map/ppermute | solution.py:945
  328.7 22.6 %collective-permute-start.26 = (bf16[512,768]{1,0:T(8,128)(2,1)}, bf16[512,768]{1,0:T(8,128)(2,1)}, u32[]{:S(2)}, u32[]{:S(2)}) collective-permute-start(bf16[512,768]{1,0:T(8,128)(2,1)} %get-tuple-element.173), channel_id=1, source_target_pairs={{1,0},{2,1},{3,2},{5,4},{6,5},{7,6},{9,8},{10,9},{11,10},{13,12},{... | collective-permute-start | bytes 2359304 | tf_op jit(solution)/shard_map/ppermute | solution.py:946
  336.4 45.6 %all-to-all-start = ((bf16[4,304,768]{2,1,0:T(8,128)(2,1)}), bf16[4,304,768]{2,1,0:T(8,128)(2,1)S(1)}, u32[]{:S(2)}, u32[]{:S(2)}) async-start(bf16[4,304,768]{2,1,0:T(8,128)(2,1)} %add_convert_fusion), calls=%async_computation | async-start | bytes 3735552 | tf_op jit(solution)/shard_map/all_to_all | solution.py:968
  340.2 11.1 %copy-start.14 = (f32[512,768]{1,0:T(8,128)S(1)}, f32[512,768]{1,0:T(8,128)}, u32[]{:S(2)}) copy-start(f32[512,768]{1,0:T(8,128)} %get-tuple-element.123) | copy-start | bytes 4718596
  340.3 20.8 %collective-permute-start.30 = (bf16[96,1728]{1,0:T(8,128)(2,1)S(1)}, bf16[96,1728]{1,0:T(8,128)(2,1)S(1)}, u32[]{:S(2)}, u32[]{:S(2)}) collective-permute-start(bf16[96,1728]{1,0:T(8,128)(2,1)S(1)} %get-tuple-element.176), channel_id=1, source_target_pairs={{0,1},{1,2},{2,3},{3,0},{4,5},{5,6},{6,7},{7,4},{8,9},{9,10},{10,1... | collective-permute-start | bytes 995336 | tf_op jit(solution)/shard_map/ppermute | solution.py:72
  343.0 22.1 %collective-permute-start.31 = (bf16[96,1728]{1,0:T(8,128)(2,1)S(1)}, bf16[96,1728]{1,0:T(8,128)(2,1)S(1)}, u32[]{:S(2)}, u32[]{:S(2)}) collective-permute-start(bf16[96,1728]{1,0:T(8,128)(2,1)S(1)} %get-tuple-element.175), channel_id=1, source_target_pairs={{0,3},{1,0},{2,1},{3,2},{4,7},{5,4},{6,5},{7,6},{8,11},{9,8},{10,9... | collective-permute-start | bytes 995336 | tf_op jit(solution)/shard_map/ppermute | solution.py:72
  346.5 34.5 %copy-start.19 = (bf16[96,192]{1,0:T(8,128)(2,1)S(1)}, bf16[96,192]{1,0:T(8,128)(2,1)}, u32[]{:S(2)}) copy-start(bf16[96,192]{1,0:T(8,128)(2,1)} %copy-done.18) | copy-start | bytes 110596
  346.6 34.5 %collective-permute-start.32 = (bf16[96,1728]{1,0:T(8,128)(2,1)S(1)}, bf16[96,1728]{1,0:T(8,128)(2,1)S(1)}, u32[]{:S(2)}, u32[]{:S(2)}) collective-permute-start(bf16[96,1728]{1,0:T(8,128)(2,1)S(1)} %get-tuple-element.174), channel_id=1, source_target_pairs={{0,2},{1,3},{2,0},{3,1},{4,6},{5,7},{6,4},{7,5},{8,10},{9,11},{10,... | collective-permute-start | bytes 995336 | tf_op jit(solution)/shard_map/ppermute | solution.py:72
  385.1 9.2 %collective-permute-start.33 = (bf16[336,192]{1,0:T(8,128)(2,1)S(1)}, bf16[336,192]{1,0:T(8,128)(2,1)S(1)}, u32[]{:S(2)}, u32[]{:S(2)}) collective-permute-start(bf16[336,192]{1,0:T(8,128)(2,1)S(1)} %get-tuple-element.189), channel_id=1, source_target_pairs={{0,1},{1,2},{2,3},{3,0},{4,5},{5,6},{6,7},{7,4},{8,9},{9,10},{10,1... | collective-permute-start | bytes 387080 | tf_op jit(solution)/shard_map/ppermute | solution.py:72
  385.2 11.5 %collective-permute-start.34 = (bf16[336,192]{1,0:T(8,128)(2,1)S(1)}, bf16[336,192]{1,0:T(8,128)(2,1)S(1)}, u32[]{:S(2)}, u32[]{:S(2)}) collective-permute-start(bf16[336,192]{1,0:T(8,128)(2,1)S(1)} %get-tuple-element.188), channel_id=1, source_target_pairs={{0,3},{1,0},{2,1},{3,2},{4,7},{5,4},{6,5},{7,6},{8,11},{9,8},{10,9... | collective-permute-start | bytes 387080 | tf_op jit(solution)/shard_map/ppermute | solution.py:72
  389.0 12.3 %collective-permute-start.35 = (bf16[336,192]{1,0:T(8,128)(2,1)S(1)}, bf16[336,192]{1,0:T(8,128)(2,1)S(1)}, u32[]{:S(2)}, u32[]{:S(2)}) collective-permute-start(bf16[336,192]{1,0:T(8,128)(2,1)S(1)} %get-tuple-element.187), channel_id=1, source_target_pairs={{0,2},{1,3},{2,0},{3,1},{4,6},{5,7},{6,4},{7,5},{8,10},{9,11},{10,... | collective-permute-start | bytes 387080 | tf_op jit(solution)/shard_map/ppermute | solution.py:72
  (21 other events, 57.6 us)

commit v3 on v2

--- a/solution.py
+++ b/solution.py
@@ -154,16 +154,17 @@
 
 def each_block(seg, where, slots, rows, visit):
     per = rows // BLOCK
-    for j, slot in enumerate(slots):
-
-        def step(i, _, j=j, slot=slot):
-            kb, qb = i // per, lax.rem(i, per)
-            at = pl.ds(pl.multiple_of(kb * BLOCK, BLOCK), BLOCK)
-            kind = block_kind(seg, where[0] * rows + qb * BLOCK, where[1 + slot] * rows + kb * BLOCK)
-            visit(j, at, kb, qb, kind)
-            return 0
-
-        lax.fori_loop(0, per * per, step, 0)
+    stride = slots[1] - slots[0] if len(slots) > 1 else 0
+
+    def step(i, _):
+        j, pair = i // (per * per), lax.rem(i, per * per)
+        kb, qb = pair // per, lax.rem(pair, per)
+        slot = slots[0] + stride * j
+        kind = block_kind(seg, where[0] * rows + qb * BLOCK, where[1 + slot] * rows + kb * BLOCK)
+        visit(j, slot, kb, qb, kind)
+        return 0
+
+    lax.fori_loop(0, len(slots) * per * per, step, 0)
 
 
 def split_pieces(pieces):
@@ -324,7 +325,7 @@
         return taken
 
     q_ref, do_ref, o_ref, lse_ref, wk_ref, wv_ref, sq_ref = take(7)
-    k_refs, v_refs, ids_refs = take(len(slots)), take(len(slots)), take(len(slots))
+    (k_ref, v_ref), ids_refs = take(2), take(len(slots))
     if not first:
         (dq_in,) = take(1)
     if last:
@@ -349,14 +350,14 @@
 
     def block(j, at, out_at, qb, masked):
         stacked, part = lanes(qb, wide), lanes(qb, BLOCK)
-        k = k_refs[j][at, :]
+        k = k_ref[at, :]
         k_t = k.T
         s = nt(k, q_s[stacked, :]) * SCORE - lse_ref[0, :, stacked]
         if masked:
             same = col_s[out_at, 0:1] == ids_s[:, part]
             s = jnp.where(jnp.concatenate([same] * heads, axis=1), s, MASKED)
         p = jnp.exp2(s)
-        dp = nt(v_refs[j][at, :], do_s[stacked, :])
+        dp = nt(v_ref[at, :], do_s[stacked, :])
         ds = (p * (dp - delta_s[:, stacked])).astype(BF)
         dv = nn(p.astype(BF), do_s[stacked, :])
         dk = nn(ds, q_s[stacked, :])
@@ -365,7 +366,9 @@
             dq_s[hs, part] += nn(k_t[hs], ds[:, h * BLOCK : (h + 1) * BLOCK])
         return dk, dv
 
-    def visit(j, at, kb, qb, kind):
+    def visit(j, slot, kb, qb, kind):
+        base = slot if len(slots) > 1 else 0
+        at = pl.ds(pl.multiple_of(base * rows + kb * BLOCK, BLOCK), BLOCK)
         out_at = pl.ds(pl.multiple_of(j * rows + kb * BLOCK, BLOCK), BLOCK)
 
         @pl.when(qb == 0)
@@ -396,19 +399,22 @@
 
     if last:
         dq_ref[...] = (dq_s[...] * HD**-0.5).T.astype(BF)
-    for j in range(len(slots)):
-        at = slice(j * rows, (j + 1) * rows)
-        dx = nt(dk_s[at, :], wk_ref[...]) + nt(dv_s[at, :], wv_ref[...])
-        if last and j == 0:
-            dx = dx + nt(dq_ref[...], wq_ref[...])
-
-        @pl.when(g == 0)
-        def _(at=at, dx=dx, j=j):
-            dx_s[at, :] = dx + base_ref[...] if last and j == 0 else dx
-
-        @pl.when(g > 0)
-        def _(at=at, dx=dx):
-            dx_s[at, :] += dx
+
+    @pl.when(g == 0)
+    def _():
+        if last:
+            dx_s[:rows, :] = base_ref[...]
+        else:
+            dx_s[...] = jnp.zeros(dx_s.shape, F32)
+
+    def back(j, _):
+        at = pl.ds(pl.multiple_of(j * rows, rows), rows)
+        dx_s[at, :] += nt(dk_s[at, :], wk_ref[...]) + nt(dv_s[at, :], wv_ref[...])
+        return 0
+
+    lax.fori_loop(0, len(slots), back, 0)
+    if last:
+        dx_s[:rows, :] += nt(dq_ref[...], wq_ref[...])
 
     @pl.when(g == pl.num_programs(0) - 1)
     def _():
@@ -436,9 +442,10 @@
 
     wq, wk, wv = (a for a, _ in weights)
     count = len(slots)
-    ins = [q, do, o, lse, wk, wv, seg] + [k] * count + [v] * count + [seg] * count
+    ins = [q, do, o, lse, wk, wv, seg, k, v] + [seg] * count
     in_specs = [q_spec, q_spec, q_spec, row_spec, wk_spec, wv_spec, ids_spec(0)]
-    in_specs += [slot_spec(s) for s in slots] * 2 + [ids_spec(1 + s) for s in slots]
+    all_spec = pl.BlockSpec((k.shape[0], GROUP), lambda i, s, w: (0, i))
+    in_specs += [all_spec if count > 1 else slot_spec(slots[0])] * 2 + [ids_spec(1 + s) for s in slots]
     if not first:
         ins.append(dq)
         in_specs.append(acc_spec)

time: 408 us -> 395 us (0.968); the launches traced: 404 us -> 402 us
  Pallas kernels: 147 us -> 122 us
  starting transfers between devices: 75.1 us -> 98 us
    ppermute x2, starting transfers between devices: 0.07 us -> 42.1 us  [on_device(): lax.ppermute(o, 'fsdp', partner(bit))]
    ppermute x1, starting transfers between devices: 23.9 us -> 5.29 us  [on_device(): r1 = lax.ppermute(dx_b, 'tensor', [(0, 1), (3, 2)])]
    pallas_call x2, Pallas kernels: 52 us -> 37.9 us  [attend_backward(): pl.pallas_call(partial(backward_kernel, slots=slots, first=first, last=la...]
    pallas_call x1, Pallas kernels: 37.1 us -> 26.4 us  [attend_forward(): pl.pallas_call(partial(forward_kernel, slots=slots, count=count, offsets=...]
  transfers between devices with their start and end apart: 37 -> 37, of which waited for: 16 -> 16; matrix products, arithmetic and copies ran while one was open for 11% -> 11% of each run, Pallas kernels for 16% -> 13%
where the time goes in v3:
time: 395 us; the launch traced here: 402 us
  Pallas kernels  122 us (31%)
  waiting for transfers between devices  118 us (30%)
  starting transfers between devices  98 us (25%)
  other arithmetic  32.6 us (8%)
  local copies, waits for them, and re-layouts  30.4 us (8%)
    ppermute x2, starting transfers between devices, on_device(): lax.ppermute(o, 'fsdp', partner(bit))  42.1 us
    ppermute x6, waiting for transfers between devices, spread(): lax.ppermute(block, 'tensor', [(i, (i + shift) % 4) for i in range(4)])  38.2 us
    pallas_call x2, Pallas kernels, attend_backward(): pl.pallas_call(partial(backward_kernel, slots=slots, first=first, last=la...  37.9 us
    pallas_call x1, Pallas kernels, middle(): pl.pallas_call(partial(middle_kernel, count=count, offsets=offsets), out_...  28.9 us
    pallas_call x1, Pallas kernels, attend_forward(): pl.pallas_call(partial(forward_kernel, slots=slots, count=count, offsets=...  26.4 us
    ppermute x2, waiting for transfers between devices, line_second(): above2 = lax.ppermute(above, 'tensor', [(2, 1), (1, 0)])  22.4 us
    ppermute x2, waiting for transfers between devices, line_first(): above = lax.ppermute(own, 'tensor', [(1, 0), (2, 1), (3, 2)])  21.6 us
    ppermute x9, waiting for transfers between devices, over(): return lax.ppermute(block, 'fsdp', partner(bit))  19.3 us
  transfers between devices with their start and end apart: 37, of which 16 were waited for; matrix products, arithmetic and copies ran while one was open for 11% of the time, Pallas kernels for 13%

profile of v3, /device:TPU:0, one launch (start us, length us, event | category | flops | bytes accessed | tf_op | source)
XLA Modules:
  0.0 402.4 jit_solution(17087203159431376068)
XLA Ops:
  4.9 5.6 %collective-permute-start.1 = (bf16[3,96,768]{2,1,0:T(8,128)(2,1)S(1)}, bf16[3,96,768]{2,1,0:T(8,128)(2,1)S(1)}, u32[]{:S(2)}, u32[]{:S(2)}) collective-permute-start(bf16[3,96,768]{2,1,0:T(8,128)(2,1)S(1)} %pad_maximum_fusion.2), channel_id=1, source_target_pairs={{0,1},{1,2},{2,3},{4,5},{5,6},{6,7},{8,9},{9,10},{10,11},{12,13},{... | collective-permute-start | bytes 1327112 | tf_op jit(solution)/shard_map/ppermute | solution.py:37
  10.5 8.2 %collective-permute-done = bf16[3,96,768]{2,1,0:T(8,128)(2,1)S(1)} collective-permute-done((bf16[3,96,768]{2,1,0:T(8,128)(2,1)S(1)}, bf16[3,96,768]{2,1,0:T(8,128)(2,1)S(1)}, u32[]{:S(2)}, u32[]{:S(2)}) %collective-permute-start) | collective-permute-done | bytes 442400 | tf_op jit(solution)/shard_map/ppermute | solution.py:38
  27.9 4.0 collective-permute-done.2
  34.1 10.2 %collective-permute-done.4 = bf16[3,96,768]{2,1,0:T(8,128)(2,1)S(1)} collective-permute-done((bf16[3,96,768]{2,1,0:T(8,128)(2,1)S(1)}, bf16[3,96,768]{2,1,0:T(8,128)(2,1)S(1)}, u32[]{:S(2)}, u32[]{:S(2)}) %collective-permute-start.4) | collective-permute-done | bytes 442400 | tf_op jit(solution)/shard_map/ppermute | solution.py:50
  45.4 2.0 concatenate.57.refs_8_.refs_16_.refs_0_
  48.8 4.6 %collective-permute-start.8 = (bf16[512,768]{1,0:T(8,128)(2,1)}, bf16[512,768]{1,0:T(8,128)(2,1)S(1)}, u32[]{:S(2)}, u32[]{:S(2)}) collective-permute-start(bf16[512,768]{1,0:T(8,128)(2,1)} %refs_0_.3), channel_id=1, source_target_pairs={{0,1},{1,2},{2,3},{4,5},{5,6},{6,7},{8,9},{9,10},{10,11},{12,13},{... | collective-permute-start | bytes 2359304 | tf_op jit(solution)/shard_map/ppermute | solution.py:37
  54.6 1.5 collective-permute-start.6
  56.1 13.4 %collective-permute-done.7 = bf16[512,768]{1,0:T(8,128)(2,1)S(1)} collective-permute-done((bf16[512,768]{1,0:T(8,128)(2,1)}, bf16[512,768]{1,0:T(8,128)(2,1)S(1)}, u32[]{:S(2)}, u32[]{:S(2)}) %collective-permute-start.7) | collective-permute-done | bytes 786464 | tf_op jit(solution)/shard_map/ppermute | solution.py:38
  75.2 18.4 %collective-permute-done.10 = bf16[512,768]{1,0:T(8,128)(2,1)S(1)} collective-permute-done((bf16[512,768]{1,0:T(8,128)(2,1)S(1)}, bf16[512,768]{1,0:T(8,128)(2,1)S(1)}, u32[]{:S(2)}, u32[]{:S(2)}) %collective-permute-start.10) | collective-permute-done | bytes 786464 | tf_op jit(solution)/shard_map/ppermute | solution.py:44
  95.5 1.6 collective-permute-start.12
  100.8 16.4 %collective-permute-done.12.refs_11_.refs_3_ = bf16[96,4608]{1,0:T(8,128)(2,1)} collective-permute-done((bf16[96,4608]{1,0:T(8,128)(2,1)S(1)}, bf16[96,4608]{1,0:T(8,128)(2,1)}, u32[]{:S(2)}, u32[]{:S(2)}) %collective-permute-start.12) | collective-permute-done | bytes 884768 | tf_op jit(solution)/shard_map/ppermute | solution.py:847
  117.2 2.5 collective-permute-done.16.refs_19_.refs_11_
  122.2 2.7 broadcast_select_fusion.refs_3_.refs_1_
  125.0 26.4 %attend_forward.1 = (bf16[512,768]{1,0:T(8,128)(2,1)}, bf16[2048,768]{1,0:T(8,128)(2,1)}, bf16[2048,768]{1,0:T(8,128)(2,1)}, bf16[512,768]{1,0:T(8,128)(2,1)}, f...) custom-call(s32[2048]{0:T(1024)} %bitcast.122, s32[7]{0:T(128)} %concatenate.52.where, bf16[512,768]{1,0:T(8,128)(2,1)} %refs_0_.3, ...), custom_call_target="tpu_custom_call" | custom-call | flops 1000 | bytes 1000 | tf_op jit(solution)/shard_map/attend_forward/pallas_call | solution.py:286
  151.4 28.9 %middle.1 = (bf16[512,768]{1,0:T(8,128)(2,1)}, f32[512,768]{1,0:T(8,128)}, bf16[512,768]{1,0:T(8,128)(2,1)}, bf16[3,512,768]{2,1,0:T(8,128)(2,1)}, bf16[512,6912]{1,0:T(8,128)(2,1)}, /*index=5*/f32[10,768]{1,0:T(8,128)}) custom-call(s32[6]{0:T(128)} %concatenate.53.known, bf16[96,9216]{1,0:T(8,128)(2,1)} %copy-done, bf16[96,9216]{1,0:T(8,128)(2,1)} %copy-done.1, ...), custom_call_target="tpu_custom_call" | custom-call | flops 1000 | bytes 1000 | tf_op jit(solution)/shard_map/middle/pallas_call | solution.py:685
  180.3 13.7 %ffn_grads.1 = (bf16[384,6912]{1,0:T(8,128)(2,1)}, bf16[384,6912]{1,0:T(8,128)(2,1)}) custom-call(s32[1]{0:T(128)} %bitcast.5.place, bf16[3,512,768]{2,1,0:T(8,128)(2,1)} %get-tuple-element.109.left_ref, bf16[512,6912]{1,0:T(8,128)(2,1)} %get-tuple-element.110.right_ref), custom_call_target="tpu_custom_call" | custom-call | flops 1000 | bytes 1000 | tf_op jit(solution)/shard_map/ffn_grads/pallas_call | solution.py:731
  194.6 17.8 %attend_backward.2 = (bf16[1536,768]{1,0:T(8,128)(2,1)}, bf16[1536,768]{1,0:T(8,128)(2,1)}, f32[768,512]{1,0:T(8,128)}, bf16[1536,768]{1,0:T(8,128)(2,1)}) custom-call(s32[2048]{0:T(1024)} %bitcast.123, s32[7]{0:T(128)} %concatenate.52.where, bf16[512,768]{1,0:T(8,128)(2,1)} %get-tuple-element.107.refs_0_, bf16[512,768]{1,0:T(8,128)(2,1)} %get-tuple-element.112.refs_1_, ...), custom_call_target="tpu_custom_call" | custom-call | flops 1000 | bytes 1000 | tf_op jit(solution)/shard_map/attend_backward/pallas_call | solution.py:470
  212.4 1.8 slice.247
  214.3 5.3 %convert_add_fusion = (f32[192,3840]{1,0:T(8,128)S(1)}, bf16[192,3840]{1,0:T(8,128)(2,1)}) fusion(bf16[384,6912]{1,0:T(8,128)(2,1)} %collective-permute-done.19, bf16[384,6912]{1,0:T(8,128)(2,1)} %get-tuple-element.119), kind=kLoop, calls=%fused_computation.2 | loop fusion | flops 5160960 | bytes 10321920 | tf_op jit(solution)/shard_map/add | solution.py:922
  219.6 1.8 slice.249
  221.4 42.1 %collective-permute-start.24 = (bf16[2,96,3840]{2,1,0:T(8,128)(2,1)}, bf16[2,96,3840]{2,1,0:T(8,128)(2,1)}, u32[]{:S(2)}, u32[]{:S(2)}) collective-permute-start(bf16[2,96,3840]{2,1,0:T(8,128)(2,1)} %bitcast.33), channel_id=1, source_target_pairs={{0,16},{4,20},{8,24},{12,28},{16,0},{20,4},{24,8},{28,12},{1,17},{... | collective-permute-start | bytes 4423688 | tf_op jit(solution)/shard_map/ppermute | solution.py:912
  264.9 2.1 slice.246
  267.1 5.3 %collective-permute-start.20 = (bf16[512,768]{1,0:T(8,128)(2,1)}, bf16[512,768]{1,0:T(8,128)(2,1)}, u32[]{:S(2)}, u32[]{:S(2)}) collective-permute-start(bf16[512,768]{1,0:T(8,128)(2,1)} %slice.246), channel_id=1, source_target_pairs={{0,1},{3,2},{4,5},{7,6},{8,9},{11,10},{12,13},{15,14},{16,17},{19,... | collective-permute-start | bytes 2359304 | tf_op jit(solution)/shard_map/ppermute | solution.py:899
  272.4 20.1 %attend_backward.3 = (bf16[512,768]{1,0:T(8,128)(2,1)}, bf16[512,768]{1,0:T(8,128)(2,1)}, bf16[512,768]{1,0:T(8,128)(2,1)}, f32[512,768]{1,0:T(8,128)}) custom-call(s32[2048]{0:T(1024)} %bitcast.124, s32[7]{0:T(128)} %concatenate.52.where, bf16[512,768]{1,0:T(8,128)(2,1)} %get-tuple-element.107.refs_0_, bf16[512,768]{1,0:T(8,128)(2,1)} %get-tuple-element.112.refs_1_, ...), custom_call_target="tpu_custom_call" | custom-call | flops 1000 | bytes 1000 | tf_op jit(solution)/shard_map/attend_backward/pallas_call | solution.py:470
  292.5 2.5 add_convert_fusion.4
  295.0 2.1 collective-permute-start.21
  297.1 1.6 collective-permute-start.22
  298.7 1.8 add_convert_fusion.1
  301.7 1.8 fusion
  303.6 2.2 collective-permute-start.29
  307.5 12.9 %attn_grads.1 = (bf16[4,304,768]{2,1,0:T(8,128)(2,1)}, f32[4,304,768]{2,1,0:T(8,128)}) custom-call(s32[1]{0:T(128)} %slice.255.core_ref, bf16[512,768]{1,0:T(8,128)(2,1)} %refs_0_.3, bf16[512,768]{1,0:T(8,128)(2,1)} %broadcast_select_fusion.refs_3_.refs_1_, bf16[512,768]{1,0:T(8,128)(2,1)} %broadcast_select_fusion.1.refs_2_, ...), custom_call_target="tpu_custom_call" | custom-call | flops 1000 | bytes 1000 | tf_op jit(solution)/shard_map/attn_grads/pallas_call | solution.py:548
  320.5 3.2 fusion.1
  323.7 3.4 collective-permute-start.25
  331.4 1.8 copy-done.11
  333.3 1.6 add_convert_fusion
  334.9 3.6 all-to-all-start
  338.8 2.7 collective-permute-start.30
  341.5 3.1 collective-permute-start.31
  345.1 4.7 %collective-permute-done.26 = bf16[512,768]{1,0:T(8,128)(2,1)} collective-permute-done((bf16[512,768]{1,0:T(8,128)(2,1)}, bf16[512,768]{1,0:T(8,128)(2,1)}, u32[]{:S(2)}, u32[]{:S(2)}) %collective-permute-start.26) | collective-permute-done | bytes 786464 | tf_op jit(solution)/shard_map/ppermute | solution.py:953
  349.8 2.8 convert_add_fusion.2
  352.6 6.7 %collective-permute-done.30 = bf16[96,1728]{1,0:T(8,128)(2,1)S(1)} collective-permute-done((bf16[96,1728]{1,0:T(8,128)(2,1)S(1)}, bf16[96,1728]{1,0:T(8,128)(2,1)S(1)}, u32[]{:S(2)}, u32[]{:S(2)}) %collective-permute-start.30) | collective-permute-done | bytes 331808 | tf_op jit(solution)/shard_map/ppermute | solution.py:72
  359.2 4.3 %collective-permute-done.31 = bf16[96,1728]{1,0:T(8,128)(2,1)S(1)} collective-permute-done((bf16[96,1728]{1,0:T(8,128)(2,1)S(1)}, bf16[96,1728]{1,0:T(8,128)(2,1)S(1)}, u32[]{:S(2)}, u32[]{:S(2)}) %collective-permute-start.31) | collective-permute-done | bytes 331808 | tf_op jit(solution)/shard_map/ppermute | solution.py:72
  363.5 15.7 %collective-permute-done.32 = bf16[96,1728]{1,0:T(8,128)(2,1)S(1)} collective-permute-done((bf16[96,1728]{1,0:T(8,128)(2,1)S(1)}, bf16[96,1728]{1,0:T(8,128)(2,1)S(1)}, u32[]{:S(2)}, u32[]{:S(2)}) %collective-permute-start.32) | collective-permute-done | bytes 331808 | tf_op jit(solution)/shard_map/ppermute | solution.py:72
  383.4 3.8 collective-permute-start.34
  388.0 4.4 %collective-permute-done.33.refs_1_ = bf16[336,192]{1,0:T(8,128)(2,1)S(1)} collective-permute-done((bf16[336,192]{1,0:T(8,128)(2,1)S(1)}, bf16[336,192]{1,0:T(8,128)(2,1)S(1)}, u32[]{:S(2)}, u32[]{:S(2)}) %collective-permute-start.33) | collective-permute-done | bytes 129056 | tf_op jit(solution)/shard_map/ppermute | solution.py:72
  392.5 2.4 collective-permute-done.34.refs_2_
  394.9 4.6 %collective-permute-done.35.refs_3_ = bf16[336,192]{1,0:T(8,128)(2,1)S(1)} collective-permute-done((bf16[336,192]{1,0:T(8,128)(2,1)S(1)}, bf16[336,192]{1,0:T(8,128)(2,1)S(1)}, u32[]{:S(2)}, u32[]{:S(2)}) %collective-permute-start.35) | collective-permute-done | bytes 129056 | tf_op jit(solution)/shard_map/ppermute | solution.py:72
  400.2 1.9 finish.1
  (176 shorter events, 48.0 us)
Async XLA Ops:
  0.7 26.3 %copy-start.28 = (f32[768]{0:T(1024)S(1)}, f32[768]{0:T(1024)}, u32[]{:S(2)}) copy-start(f32[768]{0:T(1024)} %param.34) | copy-start | bytes 9220
  0.7 26.3 %copy-start.29 = (f32[768]{0:T(1024)S(1)}, f32[768]{0:T(1024)}, u32[]{:S(2)}) copy-start(f32[768]{0:T(1024)} %param.26) | copy-start | bytes 9220
  0.7 26.3 %copy-start.30 = (f32[768]{0:T(1024)S(1)}, f32[768]{0:T(1024)}, u32[]{:S(2)}) copy-start(f32[768]{0:T(1024)} %param.27) | copy-start | bytes 9220
  0.7 26.3 %copy-start.31 = (f32[768]{0:T(1024)S(1)}, f32[768]{0:T(1024)}, u32[]{:S(2)}) copy-start(f32[768]{0:T(1024)} %param.28) | copy-start | bytes 9220
  3.6 15.1 %collective-permute-start = (bf16[3,96,768]{2,1,0:T(8,128)(2,1)S(1)}, bf16[3,96,768]{2,1,0:T(8,128)(2,1)S(1)}, u32[]{:S(2)}, u32[]{:S(2)}) collective-permute-start(bf16[3,96,768]{2,1,0:T(8,128)(2,1)S(1)} %pad_maximum_fusion.2), channel_id=1, source_target_pairs={{1,0},{2,1},{3,2},{5,4},{6,5},{7,6},{9,8},{10,9},{11,10},{13,12},{... | collective-permute-start | bytes 1327112 | tf_op jit(solution)/shard_map/ppermute | solution.py:38
  4.9 15.1 %collective-permute-start.1 = (bf16[3,96,768]{2,1,0:T(8,128)(2,1)S(1)}, bf16[3,96,768]{2,1,0:T(8,128)(2,1)S(1)}, u32[]{:S(2)}, u32[]{:S(2)}) collective-permute-start(bf16[3,96,768]{2,1,0:T(8,128)(2,1)S(1)} %pad_maximum_fusion.2), channel_id=1, source_target_pairs={{0,1},{1,2},{2,3},{4,5},{5,6},{6,7},{8,9},{9,10},{10,11},{12,13},{... | collective-permute-start | bytes 1327112 | tf_op jit(solution)/shard_map/ppermute | solution.py:37
  18.7 13.2 %collective-permute-start.2 = (bf16[3,96,768]{2,1,0:T(8,128)(2,1)S(1)}, bf16[3,96,768]{2,1,0:T(8,128)(2,1)S(1)}, u32[]{:S(2)}, u32[]{:S(2)}) collective-permute-start(bf16[3,96,768]{2,1,0:T(8,128)(2,1)S(1)} %collective-permute-done), channel_id=1, source_target_pairs={{2,1},{1,0},{6,5},{5,4},{10,9},{9,8},{14,13},{13,12},{18,17},{17,1... | collective-permute-start | bytes 1327112 | tf_op jit(solution)/shard_map/ppermute | solution.py:44
  20.0 11.9 %collective-permute-start.3 = (bf16[3,96,768]{2,1,0:T(8,128)(2,1)S(1)}, bf16[3,96,768]{2,1,0:T(8,128)(2,1)S(1)}, u32[]{:S(2)}, u32[]{:S(2)}) collective-permute-start(bf16[3,96,768]{2,1,0:T(8,128)(2,1)S(1)} %collective-permute-done.1), channel_id=1, source_target_pairs={{1,2},{2,3},{5,6},{6,7},{9,10},{10,11},{13,14},{14,15},{17,18},{18... | collective-permute-start | bytes 1327112 | tf_op jit(solution)/shard_map/ppermute | solution.py:43
  21.4 23.0 %copy-start.13 = (s32[1,2048]{1,0:T(1,128)}, s32[1,2048]{1,0:T(1,128)S(1)}, u32[]{:S(2)}) copy-start(s32[1,2048]{1,0:T(1,128)S(1)} %compare_select_fusion.refs_4_.refs_5_.refs_6_.refs_7_.refs_26_.refs_9_.refs_10_.refs_11_) | copy-start | bytes 24580
  32.0 12.3 %collective-permute-start.4 = (bf16[3,96,768]{2,1,0:T(8,128)(2,1)S(1)}, bf16[3,96,768]{2,1,0:T(8,128)(2,1)S(1)}, u32[]{:S(2)}, u32[]{:S(2)}) collective-permute-start(bf16[3,96,768]{2,1,0:T(8,128)(2,1)S(1)} %broadcast_select_fusion.4), channel_id=1, source_target_pairs={{1,0},{2,3},{5,4},{6,7},{9,8},{10,11},{13,12},{14,15},{17,16},{18,... | collective-permute-start | bytes 1327112 | tf_op jit(solution)/shard_map/ppermute | solution.py:50
  47.4 47.2 %copy-start = (bf16[96,9216]{1,0:T(8,128)(2,1)}, bf16[96,9216]{1,0:T(8,128)(2,1)S(1)}, u32[]{:S(2)}) copy-start(bf16[96,9216]{1,0:T(8,128)(2,1)S(1)} %concatenate.57.refs_8_.refs_16_.refs_0_) | copy-start | bytes 5308420
  47.4 23.4 %collective-permute-start.9 = (bf16[96,9216]{1,0:T(8,128)(2,1)S(1)}, bf16[96,9216]{1,0:T(8,128)(2,1)S(1)}, u32[]{:S(2)}, u32[]{:S(2)}) collective-permute-start(bf16[96,9216]{1,0:T(8,128)(2,1)S(1)} %concatenate.57.refs_8_.refs_16_.refs_0_), channel_id=1, source_target_pairs={{0,4},{4,0},{8,12},{12,8},{16,20},{20,16},{24,28},{28,24},{1,5},{5... | collective-permute-start | bytes 5308424 | tf_op jit(solution)/shard_map/ppermute | solution.py:847
  47.5 22.0 %collective-permute-start.7 = (bf16[512,768]{1,0:T(8,128)(2,1)}, bf16[512,768]{1,0:T(8,128)(2,1)S(1)}, u32[]{:S(2)}, u32[]{:S(2)}) collective-permute-start(bf16[512,768]{1,0:T(8,128)(2,1)} %refs_0_.3), channel_id=1, source_target_pairs={{1,0},{2,1},{3,2},{5,4},{6,5},{7,6},{9,8},{10,9},{11,10},{13,12},{... | collective-permute-start | bytes 2359304 | tf_op jit(solution)/shard_map/ppermute | solution.py:38
  48.8 22.0 %collective-permute-start.8 = (bf16[512,768]{1,0:T(8,128)(2,1)}, bf16[512,768]{1,0:T(8,128)(2,1)S(1)}, u32[]{:S(2)}, u32[]{:S(2)}) collective-permute-start(bf16[512,768]{1,0:T(8,128)(2,1)} %refs_0_.3), channel_id=1, source_target_pairs={{0,1},{1,2},{2,3},{4,5},{5,6},{6,7},{8,9},{9,10},{10,11},{12,13},{... | collective-permute-start | bytes 2359304 | tf_op jit(solution)/shard_map/ppermute | solution.py:37
  53.4 41.2 %collective-permute-start.5 = (bf16[96,9216]{1,0:T(8,128)(2,1)S(1)}, bf16[96,9216]{1,0:T(8,128)(2,1)S(1)}, u32[]{:S(2)}, u32[]{:S(2)}) collective-permute-start(bf16[96,9216]{1,0:T(8,128)(2,1)S(1)} %concatenate.57.refs_8_.refs_16_.refs_0_), channel_id=1, source_target_pairs={{0,8},{4,12},{8,0},{12,4},{16,24},{20,28},{24,16},{28,20},{1,9},{5... | collective-permute-start | bytes 5308424 | tf_op jit(solution)/shard_map/ppermute | solution.py:847
  54.6 40.3 %collective-permute-start.6 = (bf16[96,9216]{1,0:T(8,128)(2,1)S(1)}, bf16[96,9216]{1,0:T(8,128)(2,1)}, u32[]{:S(2)}, u32[]{:S(2)}) collective-permute-start(bf16[96,9216]{1,0:T(8,128)(2,1)S(1)} %concatenate.57.refs_8_.refs_16_.refs_0_), channel_id=1, source_target_pairs={{0,16},{4,20},{8,24},{12,28},{16,0},{20,4},{24,8},{28,12},{1,17},{... | collective-permute-start | bytes 5308424 | tf_op jit(solution)/shard_map/ppermute | solution.py:847
  70.8 28.5 %copy-start.12 = (bf16[512,768]{1,0:T(8,128)(2,1)}, bf16[512,768]{1,0:T(8,128)(2,1)S(1)}, u32[]{:S(2)}) copy-start(bf16[512,768]{1,0:T(8,128)(2,1)S(1)} %collective-permute-done.8) | copy-start | bytes 2359300
  72.2 21.5 %collective-permute-start.10 = (bf16[512,768]{1,0:T(8,128)(2,1)S(1)}, bf16[512,768]{1,0:T(8,128)(2,1)S(1)}, u32[]{:S(2)}, u32[]{:S(2)}) collective-permute-start(bf16[512,768]{1,0:T(8,128)(2,1)S(1)} %collective-permute-done.7), channel_id=1, source_target_pairs={{2,1},{1,0},{6,5},{5,4},{10,9},{9,8},{14,13},{13,12},{18,17},{17,1... | collective-permute-start | bytes 2359304 | tf_op jit(solution)/shard_map/ppermute | solution.py:44
  73.4 20.2 %collective-permute-start.11 = (bf16[512,768]{1,0:T(8,128)(2,1)S(1)}, bf16[512,768]{1,0:T(8,128)(2,1)S(1)}, u32[]{:S(2)}, u32[]{:S(2)}) collective-permute-start(bf16[512,768]{1,0:T(8,128)(2,1)S(1)} %collective-permute-done.8), channel_id=1, source_target_pairs={{1,2},{2,3},{5,6},{6,7},{9,10},{10,11},{13,14},{14,15},{17,18},{18... | collective-permute-start | bytes 2359304 | tf_op jit(solution)/shard_map/ppermute | solution.py:43
  94.9 27.3 %collective-permute-start.13 = (bf16[96,9216]{1,0:T(8,128)(2,1)S(1)}, bf16[96,9216]{1,0:T(8,128)(2,1)S(1)}, u32[]{:S(2)}, u32[]{:S(2)}) collective-permute-start(bf16[96,9216]{1,0:T(8,128)(2,1)S(1)} %collective-permute-done.5.refs_9_.refs_17_.refs_1_), channel_id=1, source_target_pairs={{0,4},{4,0},{8,12},{12,8},{16,20},{20,16},{24,28},{28,24},{1,5},{5... | collective-permute-start | bytes 5308424 | tf_op jit(solution)/shard_map/ppermute | solution.py:847
  94.9 27.3 %collective-permute-start.14 = (bf16[96,9216]{1,0:T(8,128)(2,1)}, bf16[96,9216]{1,0:T(8,128)(2,1)}, u32[]{:S(2)}, u32[]{:S(2)}) collective-permute-start(bf16[96,9216]{1,0:T(8,128)(2,1)} %collective-permute-done.6.refs_10_.refs_18_.refs_2_), channel_id=1, source_target_pairs={{0,4},{4,0},{8,12},{12,8},{16,20},{20,16},{24,28},{28,24},{1,5},{5... | collective-permute-start | bytes 5308424 | tf_op jit(solution)/shard_map/ppermute | solution.py:847
  95.5 21.7 %collective-permute-start.12 = (bf16[96,4608]{1,0:T(8,128)(2,1)S(1)}, bf16[96,4608]{1,0:T(8,128)(2,1)}, u32[]{:S(2)}, u32[]{:S(2)}) collective-permute-start(bf16[96,4608]{1,0:T(8,128)(2,1)S(1)} %slice.244), channel_id=1, source_target_pairs={{0,16},{4,20},{8,24},{12,28},{16,0},{20,4},{24,8},{28,12},{1,17},{... | collective-permute-start | bytes 2654216 | tf_op jit(solution)/shard_map/ppermute | solution.py:847
  98.3 21.4 %collective-permute-start.16 = (bf16[96,4608]{1,0:T(8,128)(2,1)S(1)}, bf16[96,4608]{1,0:T(8,128)(2,1)}, u32[]{:S(2)}, u32[]{:S(2)}) collective-permute-start(bf16[96,4608]{1,0:T(8,128)(2,1)S(1)} %slice.245), channel_id=1, source_target_pairs={{0,8},{4,12},{8,0},{12,4},{16,24},{20,28},{24,16},{28,20},{1,9},{5... | collective-permute-start | bytes 2654216 | tf_op jit(solution)/shard_map/ppermute | solution.py:847
  99.3 22.9 %collective-permute-start.18 = (bf16[512,768]{1,0:T(8,128)(2,1)}, bf16[512,768]{1,0:T(8,128)(2,1)}, u32[]{:S(2)}, u32[]{:S(2)}) collective-permute-start(bf16[512,768]{1,0:T(8,128)(2,1)} %broadcast_select_fusion.1.refs_2_), channel_id=1, source_target_pairs={{1,0},{2,3},{5,4},{6,7},{9,8},{10,11},{13,12},{14,15},{17,16},{18,... | collective-permute-start | bytes 2359304 | tf_op jit(solution)/shard_map/ppermute | solution.py:50
  117.2 7.8 %collective-permute-start.15 = (bf16[96,4608]{1,0:T(8,128)(2,1)}, bf16[96,4608]{1,0:T(8,128)(2,1)}, u32[]{:S(2)}, u32[]{:S(2)}) collective-permute-start(bf16[96,4608]{1,0:T(8,128)(2,1)} %collective-permute-done.12.refs_11_.refs_3_), channel_id=1, source_target_pairs={{0,4},{4,0},{8,12},{12,8},{16,20},{20,16},{24,28},{28,24},{1,5},{5... | collective-permute-start | bytes 2654216 | tf_op jit(solution)/shard_map/ppermute | solution.py:847
  119.7 5.3 %collective-permute-start.17 = (bf16[96,4608]{1,0:T(8,128)(2,1)}, bf16[96,4608]{1,0:T(8,128)(2,1)}, u32[]{:S(2)}, u32[]{:S(2)}) collective-permute-start(bf16[96,4608]{1,0:T(8,128)(2,1)} %collective-permute-done.16.refs_19_.refs_11_), channel_id=1, source_target_pairs={{0,4},{4,0},{8,12},{12,8},{16,20},{20,16},{24,28},{28,24},{1,5},{5... | collective-permute-start | bytes 2654216 | tf_op jit(solution)/shard_map/ppermute | solution.py:847
  194.1 20.2 %collective-permute-start.19 = (bf16[384,6912]{1,0:T(8,128)(2,1)}, bf16[384,6912]{1,0:T(8,128)(2,1)}, u32[]{:S(2)}, u32[]{:S(2)}) collective-permute-start(bf16[384,6912]{1,0:T(8,128)(2,1)} %get-tuple-element.111), channel_id=1, source_target_pairs={{0,4},{4,0},{8,12},{12,8},{16,20},{20,16},{24,28},{28,24},{1,5},{5... | collective-permute-start | bytes 15925256 | tf_op jit(solution)/shard_map/ppermute | solution.py:893
  214.2 49.2 %copy-start.4 = (bf16[384,3072]{1,0:T(8,128)(2,1)}, bf16[384,3072]{1,0:T(8,128)(2,1)S(1)}, u32[]{:S(2)}) copy-start(bf16[384,3072]{1,0:T(8,128)(2,1)S(1)} %slice.247) | copy-start | bytes 7077892
  221.4 43.5 %copy-start.6 = (bf16[384,3072]{1,0:T(8,128)(2,1)}, bf16[384,3072]{1,0:T(8,128)(2,1)S(1)}, u32[]{:S(2)}) copy-start(bf16[384,3072]{1,0:T(8,128)(2,1)S(1)} %slice.249) | copy-start | bytes 7077892
  221.4 77.3 %collective-permute-start.24 = (bf16[2,96,3840]{2,1,0:T(8,128)(2,1)}, bf16[2,96,3840]{2,1,0:T(8,128)(2,1)}, u32[]{:S(2)}, u32[]{:S(2)}) collective-permute-start(bf16[2,96,3840]{2,1,0:T(8,128)(2,1)} %bitcast.33), channel_id=1, source_target_pairs={{0,16},{4,20},{8,24},{12,28},{16,0},{20,4},{24,8},{28,12},{1,17},{... | collective-permute-start | bytes 4423688 | tf_op jit(solution)/shard_map/ppermute | solution.py:912
  264.9 33.8 %collective-permute-start.23 = (bf16[2,96,3072]{2,1,0:T(8,128)(2,1)}, bf16[2,96,3072]{2,1,0:T(8,128)(2,1)}, u32[]{:S(2)}, u32[]{:S(2)}) collective-permute-start(bf16[2,96,3072]{2,1,0:T(8,128)(2,1)} %fusion.5), channel_id=1, source_target_pairs={{0,8},{4,12},{8,0},{12,4},{16,24},{20,28},{24,16},{28,20},{1,9},{5... | collective-permute-start | bytes 3538952 | tf_op jit(solution)/shard_map/ppermute | solution.py:912
  267.1 25.4 %collective-permute-start.20 = (bf16[512,768]{1,0:T(8,128)(2,1)}, bf16[512,768]{1,0:T(8,128)(2,1)}, u32[]{:S(2)}, u32[]{:S(2)}) collective-permute-start(bf16[512,768]{1,0:T(8,128)(2,1)} %slice.246), channel_id=1, source_target_pairs={{0,1},{3,2},{4,5},{7,6},{8,9},{11,10},{12,13},{15,14},{16,17},{19,... | collective-permute-start | bytes 2359304 | tf_op jit(solution)/shard_map/ppermute | solution.py:899
  295.0 25.5 %collective-permute-start.21 = (bf16[512,768]{1,0:T(8,128)(2,1)}, bf16[512,768]{1,0:T(8,128)(2,1)}, u32[]{:S(2)}, u32[]{:S(2)}) collective-permute-start(bf16[512,768]{1,0:T(8,128)(2,1)} %add_convert_fusion.4), channel_id=1, source_target_pairs={{0,1},{3,2},{4,5},{7,6},{8,9},{11,10},{12,13},{15,14},{16,17},{19,... | collective-permute-start | bytes 2359304 | tf_op jit(solution)/shard_map/ppermute | solution.py:917
  297.1 23.4 %collective-permute-start.22 = (bf16[512,768]{1,0:T(8,128)(2,1)}, bf16[512,768]{1,0:T(8,128)(2,1)}, u32[]{:S(2)}, u32[]{:S(2)}) collective-permute-start(bf16[512,768]{1,0:T(8,128)(2,1)} %add_convert_fusion.4), channel_id=1, source_target_pairs={{1,2},{2,1},{5,6},{6,5},{9,10},{10,9},{13,14},{14,13},{17,18},{18,... | collective-permute-start | bytes 2359304 | tf_op jit(solution)/shard_map/ppermute | solution.py:918
  303.6 24.9 %collective-permute-start.29 = (bf16[96,3840]{1,0:T(8,128)(2,1)}, bf16[96,3840]{1,0:T(8,128)(2,1)}, u32[]{:S(2)}, u32[]{:S(2)}) collective-permute-start(bf16[96,3840]{1,0:T(8,128)(2,1)} %slice_bitcast_fusion.5), channel_id=1, source_target_pairs={{0,8},{4,12},{8,0},{12,4},{16,24},{20,28},{24,16},{28,20},{1,9},{5... | collective-permute-start | bytes 2211848 | tf_op jit(solution)/shard_map/ppermute | solution.py:114
  306.7 21.8 %collective-permute-start.28 = (bf16[96,3072]{1,0:T(8,128)(2,1)}, bf16[96,3072]{1,0:T(8,128)(2,1)}, u32[]{:S(2)}, u32[]{:S(2)}) collective-permute-start(bf16[96,3072]{1,0:T(8,128)(2,1)} %slice_bitcast_fusion.7), channel_id=1, source_target_pairs={{0,16},{4,20},{8,24},{12,28},{16,0},{20,4},{24,8},{28,12},{1,17},{... | collective-permute-start | bytes 1769480 | tf_op jit(solution)/shard_map/ppermute | solution.py:114
  307.5 13.0 %copy-start.10 = (bf16[1536,768]{1,0:T(8,128)(2,1)S(1)}, bf16[1536,768]{1,0:T(8,128)(2,1)}, u32[]{:S(2)}) copy-start(bf16[1536,768]{1,0:T(8,128)(2,1)} %get-tuple-element.118) | copy-start | bytes 7077892
  320.4 11.0 %collective-permute-start.27 = (bf16[4,304,768]{2,1,0:T(8,128)(2,1)}, bf16[4,304,768]{2,1,0:T(8,128)(2,1)S(1)}, u32[]{:S(2)}, u32[]{:S(2)}) collective-permute-start(bf16[4,304,768]{2,1,0:T(8,128)(2,1)} %get-tuple-element.134), channel_id=1, source_target_pairs={{0,4},{4,0},{8,12},{12,8},{16,20},{20,16},{24,28},{28,24},{1,5},{5... | collective-permute-start | bytes 5603336 | tf_op jit(solution)/shard_map/ppermute | solution.py:947
  323.7 21.3 %collective-permute-start.25 = (bf16[512,768]{1,0:T(8,128)(2,1)}, bf16[512,768]{1,0:T(8,128)(2,1)}, u32[]{:S(2)}, u32[]{:S(2)}) collective-permute-start(bf16[512,768]{1,0:T(8,128)(2,1)} %get-tuple-element.172), channel_id=1, source_target_pairs={{0,1},{1,2},{2,3},{4,5},{5,6},{6,7},{8,9},{9,10},{10,11},{12,13},{... | collective-permute-start | bytes 2359304 | tf_op jit(solution)/shard_map/ppermute | solution.py:952
  327.2 22.6 %collective-permute-start.26 = (bf16[512,768]{1,0:T(8,128)(2,1)}, bf16[512,768]{1,0:T(8,128)(2,1)}, u32[]{:S(2)}, u32[]{:S(2)}) collective-permute-start(bf16[512,768]{1,0:T(8,128)(2,1)} %get-tuple-element.173), channel_id=1, source_target_pairs={{1,0},{2,1},{3,2},{5,4},{6,5},{7,6},{9,8},{10,9},{11,10},{13,12},{... | collective-permute-start | bytes 2359304 | tf_op jit(solution)/shard_map/ppermute | solution.py:953
  334.9 45.3 %all-to-all-start = ((bf16[4,304,768]{2,1,0:T(8,128)(2,1)}), bf16[4,304,768]{2,1,0:T(8,128)(2,1)S(1)}, u32[]{:S(2)}, u32[]{:S(2)}) async-start(bf16[4,304,768]{2,1,0:T(8,128)(2,1)} %add_convert_fusion), calls=%async_computation | async-start | bytes 3735552 | tf_op jit(solution)/shard_map/all_to_all | solution.py:975
  338.8 20.4 %collective-permute-start.30 = (bf16[96,1728]{1,0:T(8,128)(2,1)S(1)}, bf16[96,1728]{1,0:T(8,128)(2,1)S(1)}, u32[]{:S(2)}, u32[]{:S(2)}) collective-permute-start(bf16[96,1728]{1,0:T(8,128)(2,1)S(1)} %get-tuple-element.176), channel_id=1, source_target_pairs={{0,1},{1,2},{2,3},{3,0},{4,5},{5,6},{6,7},{7,4},{8,9},{9,10},{10,1... | collective-permute-start | bytes 995336 | tf_op jit(solution)/shard_map/ppermute | solution.py:72
  341.5 22.1 %collective-permute-start.31 = (bf16[96,1728]{1,0:T(8,128)(2,1)S(1)}, bf16[96,1728]{1,0:T(8,128)(2,1)S(1)}, u32[]{:S(2)}, u32[]{:S(2)}) collective-permute-start(bf16[96,1728]{1,0:T(8,128)(2,1)S(1)} %get-tuple-element.175), channel_id=1, source_target_pairs={{0,3},{1,0},{2,1},{3,2},{4,7},{5,4},{6,5},{7,6},{8,11},{9,8},{10,9... | collective-permute-start | bytes 995336 | tf_op jit(solution)/shard_map/ppermute | solution.py:72
  344.5 34.7 %copy-start.19 = (bf16[96,192]{1,0:T(8,128)(2,1)S(1)}, bf16[96,192]{1,0:T(8,128)(2,1)}, u32[]{:S(2)}) copy-start(bf16[96,192]{1,0:T(8,128)(2,1)} %copy-done.18) | copy-start | bytes 110596
  344.5 34.7 %collective-permute-start.32 = (bf16[96,1728]{1,0:T(8,128)(2,1)S(1)}, bf16[96,1728]{1,0:T(8,128)(2,1)S(1)}, u32[]{:S(2)}, u32[]{:S(2)}) collective-permute-start(bf16[96,1728]{1,0:T(8,128)(2,1)S(1)} %get-tuple-element.174), channel_id=1, source_target_pairs={{0,2},{1,3},{2,0},{3,1},{4,6},{5,7},{6,4},{7,5},{8,10},{9,11},{10,... | collective-permute-start | bytes 995336 | tf_op jit(solution)/shard_map/ppermute | solution.py:72
  383.3 9.2 %collective-permute-start.33 = (bf16[336,192]{1,0:T(8,128)(2,1)S(1)}, bf16[336,192]{1,0:T(8,128)(2,1)S(1)}, u32[]{:S(2)}, u32[]{:S(2)}) collective-permute-start(bf16[336,192]{1,0:T(8,128)(2,1)S(1)} %get-tuple-element.189), channel_id=1, source_target_pairs={{0,1},{1,2},{2,3},{3,0},{4,5},{5,6},{6,7},{7,4},{8,9},{9,10},{10,1... | collective-permute-start | bytes 387080 | tf_op jit(solution)/shard_map/ppermute | solution.py:72
  383.4 11.5 %collective-permute-start.34 = (bf16[336,192]{1,0:T(8,128)(2,1)S(1)}, bf16[336,192]{1,0:T(8,128)(2,1)S(1)}, u32[]{:S(2)}, u32[]{:S(2)}) collective-permute-start(bf16[336,192]{1,0:T(8,128)(2,1)S(1)} %get-tuple-element.188), channel_id=1, source_target_pairs={{0,3},{1,0},{2,1},{3,2},{4,7},{5,4},{6,5},{7,6},{8,11},{9,8},{10,9... | collective-permute-start | bytes 387080 | tf_op jit(solution)/shard_map/ppermute | solution.py:72
  387.2 12.3 %collective-permute-start.35 = (bf16[336,192]{1,0:T(8,128)(2,1)S(1)}, bf16[336,192]{1,0:T(8,128)(2,1)S(1)}, u32[]{:S(2)}, u32[]{:S(2)}) collective-permute-start(bf16[336,192]{1,0:T(8,128)(2,1)S(1)} %get-tuple-element.187), channel_id=1, source_target_pairs={{0,2},{1,3},{2,0},{3,1},{4,6},{5,7},{6,4},{7,5},{8,10},{9,11},{10,... | collective-permute-start | bytes 387080 | tf_op jit(solution)/shard_map/ppermute | solution.py:72
  (21 other events, 67.4 us)

commit v4 on v3

--- a/solution.py
+++ b/solution.py
@@ -330,9 +330,13 @@
         (dq_in,) = take(1)
     if last:
         wq_ref, base_ref = take(2)
-        dk_s, dv_s, dq_ref, dx_ref, q_s, do_s, delta_s, col_s, ids_s, dx_s, dq_s = refs
+        dk_s, dv_s, dq_ref = take(3)
+        dx_refs = take(len(slots))
+        q_s, do_s, delta_s, col_s, ids_s, dx_s, dq_s = refs
     else:
-        dk_s, dv_s, dq_s, dx_ref, q_s, do_s, delta_s, col_s, ids_s, dx_s = refs
+        dk_s, dv_s, dq_s = take(3)
+        dx_refs = take(len(slots))
+        q_s, do_s, delta_s, col_s, ids_s, dx_s = refs
     g = pl.program_id(0)
     ids_down(ids_refs, col_s)
     ids_s[...] = sq_ref[...].astype(F32)
@@ -418,7 +422,8 @@
 
     @pl.when(g == pl.num_programs(0) - 1)
     def _():
-        dx_ref[...] = dx_s[...].astype(dx_ref.dtype)
+        for j, dx_ref in enumerate(dx_refs):
+            dx_ref[...] = dx_s[j * rows : (j + 1) * rows, :].astype(dx_ref.dtype)
 
 
 def attend_backward(q, k, v, do, o, lse, slots, weights, seg, where, dq=None, base=None):
@@ -462,11 +467,13 @@
         (q_spec, jax.ShapeDtypeStruct((rows, width), BF))
         if last
         else (acc_spec, jax.ShapeDtypeStruct((width, rows), F32)),
+    ]
+    results += [
         (
-            pl.BlockSpec((keys, width), lambda i, s, w: (0, 0)),
-            jax.ShapeDtypeStruct((keys, width), F32 if last else BF),
-        ),
-    ]
+            pl.BlockSpec((rows, width), lambda i, s, w: (0, 0)),
+            jax.ShapeDtypeStruct((rows, width), F32 if last else BF),
+        )
+    ] * count
     return pl.pallas_call(
         partial(backward_kernel, slots=slots, first=first, last=last),
         out_shape=tuple(r[1] for r in results),
@@ -703,8 +710,8 @@
     )(known, *pieces[0], *pieces[1], ctx, x, grad, vectors, bias)
 
 
-def ffn_grad_kernel(place, left_ref, right_ref, kept_ref, sent_ref, left_s, chosen_s, *, n):
-    half = kept_ref.shape[0]
+def ffn_grad_kernel(place, left_ref, right_ref, kept_1, kept_2, sent_1, sent_2, left_s, chosen_s, *, n):
+    half = kept_1.shape[0]
 
     @pl.when(pl.program_id(0) % 4 == 0)
     def _():
@@ -719,18 +726,24 @@
                 chosen_s[j * size : (j + 1) * size, :] = left_s[pl.ds(pl.multiple_of(block * size, size), size), :]
 
     total = nn(chosen_s[...], right_ref[...])
-    kept_ref[...] = total[:half].astype(BF)
-    sent_ref[...] = total[half:].astype(BF)
+
+    def put(kept_ref, sent_ref):
+        kept_ref[...] = total[:half].astype(BF)
+        sent_ref[...] = total[half:].astype(BF)
+
+    pl.when(pl.program_id(0) < 4)(lambda: put(kept_1, sent_1))
+    pl.when(pl.program_id(0) >= 4)(lambda: put(kept_2, sent_2))
 
 
 def ffn_grads(place, lefts, rights, n):
     _, rows, width = lefts.shape
     units = rights.shape[1] // 9
-    out_spec = pl.BlockSpec((width // 2, units), lambda i, p: (0, i))
-    out_shape = jax.ShapeDtypeStruct((width // 2, rights.shape[1]), BF)
+    first_spec = pl.BlockSpec((width // 2, units), lambda i, p: (0, jnp.minimum(i, 3)))
+    second_spec = pl.BlockSpec((width // 2, units), lambda i, p: (0, jnp.maximum(i - 4, 0)))
+    first_shape, second_shape = (jax.ShapeDtypeStruct((width // 2, k * units), BF) for k in (4, 5))
     return pl.pallas_call(
         partial(ffn_grad_kernel, n=n),
-        out_shape=(out_shape, out_shape),
+        out_shape=(first_shape, second_shape) * 2,
         grid_spec=pltpu.PrefetchScalarGridSpec(
             num_scalar_prefetch=1,
             grid=(9,),
@@ -738,7 +751,7 @@
                 pl.BlockSpec((1, rows, width), lambda i, p: (i // 4, 0, 0)),
                 pl.BlockSpec((rows, units), lambda i, p: (0, i)),
             ],
-            out_specs=[out_spec, out_spec],
+            out_specs=[first_spec, second_spec] * 2,
             scratch_shapes=[pltpu.VMEM((width, rows), BF), pltpu.VMEM((width, rows), BF)],
         ),
         cost_estimate=pl.CostEstimate(flops=FEW, bytes_accessed=FEW, transcendentals=0),
@@ -883,24 +896,27 @@
         known, pieces, ctx, tokens, out_grad, vectors, up_bias.reshape(4, units)
     )
     place = f.astype(jnp.int32)[None]
-    kept, sent = ffn_grads(place, lefts, rights, n)
+    *kept, sent_1, sent_2 = ffn_grads(place, lefts, rights, n)
+    sent = [sent_1, sent_2]
     if r % 16:
-        full = jnp.concatenate([kept, sent]).reshape(n, r, -1)
+        full = [jnp.concatenate(pair).reshape(n, r, -1) for pair in zip(kept, sent)]
         kept, sent = (
-            jnp.concatenate([lax.dynamic_slice_in_dim(full, f ^ (2 * q + c), 1)[0] for q in range(n // 2)])
+            [
+                jnp.concatenate([lax.dynamic_slice_in_dim(x, f ^ (2 * q + c), 1)[0] for q in range(n // 2)])
+                for x in full
+            ]
             for c in range(2)
         )
-    got = lax.ppermute(sent, "fsdp", partner(1))
-    g_ctx = after(g_ctx, sent)
+    got = [lax.ppermute(x, "fsdp", partner(1)) for x in sent]
+    g_ctx = after(g_ctx, *sent)
 
     args = (q, k, v, g_ctx, ctx, lse)
-    dk_n, dv_n, dq, dx_n = attend_backward(*args, (3, 2, 1), weights, seg, where)
-    dx_b, dx_c, dx_a = (dx_n[i * rows : (i + 1) * rows] for i in range(3))
+    dk_n, dv_n, dq, dx_b, dx_c, dx_a = attend_backward(*args, (3, 2, 1), weights, seg, where)
     r1 = lax.ppermute(dx_b, "tensor", [(0, 1), (3, 2)])
     steps = list(zip(outer_bits(), outer_bits()[::-1]))
-    got = after(got, dx_n)
-    held = [outer_axes(kept[:, : 4 * units]), outer_axes(kept[:, 4 * units :])]
-    come = [outer_axes(got[:, : 4 * units])[0], outer_axes(got[:, 4 * units :])[0]]
+    got = after(got, dx_b)
+    held = [outer_axes(x) for x in kept]
+    come = [outer_axes(x)[0] for x in got]
     lefts = [h[1] for h in held]
     held = [h[0] for h in held]
     axes = [left.index(bit) for left, bit in zip(lefts, steps[0])]
@@ -917,7 +933,7 @@
     rx = lax.ppermute(middle_x, "tensor", [(0, 1), (3, 2)])
     ry = lax.ppermute(middle_x, "tensor", [(1, 2), (2, 1)])
 
-    arrived = after(arrived, dx_own)
+    arrived, held, come = after((arrived, held, come), dx_own)
     blocks = [
         (a.astype(F32) + b.astype(F32) + c.astype(F32)).astype(BF)
         for a, b, c in zip(at(held, 0), at(come, 0), arrived)

time: 395 us -> 386 us (0.977); the launches traced: 402 us -> 384 us
  starting transfers between devices: 98 us -> 80.6 us
  local copies, waits for them, and re-layouts: 30.4 us -> 24.3 us
  Pallas kernels: 122 us -> 128 us
    ppermute x2, starting transfers between devices: 42.1 us -> 2.48 us  [on_device(): lax.ppermute(o, 'fsdp', partner(bit))]
    ppermute x1, starting transfers between devices: 5.29 us -> 28.2 us  [on_device(): r1 = lax.ppermute(dx_b, 'tensor', [(0, 1), (3, 2)])]
    ppermute x6, waiting for transfers between devices: 38.2 us -> 28.5 us  [spread(): lax.ppermute(block, 'tensor', [(i, (i + shift) % 4) for i in range(4)])]
    ppermute x1, waiting for transfers between devices: 4.72 us -> 12.7 us  [on_device(): from_above = lax.ppermute(down_x, 'tensor', [(1, 0), (2, 1), (3, 2)])]
    slice x3 -> x0, local copies, waits for them, and re-layouts: 5.78 us -> none  [the longest x1 2.14 us: on_device(): dx_b, dx_c, dx_a = (dx_n[i * rows:(i + 1) * rows] for i in range(3))]
    add x1 -> x0, other arithmetic: 5.3 us -> none  [on_device(): a.astype(F32) + b.astype(F32) + c.astype(F32)]
  transfers between devices with their start and end apart: 37 -> 38, of which waited for: 16 -> 16; matrix products, arithmetic and copies ran while one was open for 11% -> 10% of each run, Pallas kernels for 13% -> 14%
where the time goes in v4:
time: 386 us; the launch traced here: 384 us
  Pallas kernels  128 us (33%)
  waiting for transfers between devices  118 us (31%)
  starting transfers between devices  80.6 us (21%)
  other arithmetic  31.5 us (8%)
  local copies, waits for them, and re-layouts  24.3 us (6%)
    pallas_call x2, Pallas kernels, attend_backward(): pl.pallas_call(partial(backward_kernel, slots=slots, first=first, last=la...  40.6 us
    pallas_call x1, Pallas kernels, middle(): pl.pallas_call(partial(middle_kernel, count=count, offsets=offsets), out_...  28.9 us
    pallas_call x1, Pallas kernels, attend_forward(): pl.pallas_call(partial(forward_kernel, slots=slots, count=count, offsets=...  28.9 us
    ppermute x6, waiting for transfers between devices, spread(): lax.ppermute(block, 'tensor', [(i, (i + shift) % 4) for i in range(4)])  28.5 us
    ppermute x1, starting transfers between devices, on_device(): r1 = lax.ppermute(dx_b, 'tensor', [(0, 1), (3, 2)])  28.2 us
    ppermute x2, waiting for transfers between devices, line_second(): above2 = lax.ppermute(above, 'tensor', [(2, 1), (1, 0)])  22.5 us
    ppermute x2, waiting for transfers between devices, line_first(): above = lax.ppermute(own, 'tensor', [(1, 0), (2, 1), (3, 2)])  21.6 us
    ppermute x9, waiting for transfers between devices, over(): return lax.ppermute(block, 'fsdp', partner(bit))  19.5 us
  transfers between devices with their start and end apart: 38, of which 16 were waited for; matrix products, arithmetic and copies ran while one was open for 10% of the time, Pallas kernels for 14%

profile of v4, /device:TPU:0, one launch (start us, length us, event | category | flops | bytes accessed | tf_op | source)
XLA Modules:
  0.0 384.4 jit_solution(17887596445109572679)
XLA Ops:
  4.9 5.6 %collective-permute-start.1 = (bf16[3,96,768]{2,1,0:T(8,128)(2,1)S(1)}, bf16[3,96,768]{2,1,0:T(8,128)(2,1)S(1)}, u32[]{:S(2)}, u32[]{:S(2)}) collective-permute-start(bf16[3,96,768]{2,1,0:T(8,128)(2,1)S(1)} %pad_maximum_fusion.2), channel_id=1, source_target_pairs={{0,1},{1,2},{2,3},{4,5},{5,6},{6,7},{8,9},{9,10},{10,11},{12,13},{... | collective-permute-start | bytes 1327112 | tf_op jit(solution)/shard_map/ppermute | solution.py:37
  10.5 8.2 %collective-permute-done = bf16[3,96,768]{2,1,0:T(8,128)(2,1)S(1)} collective-permute-done((bf16[3,96,768]{2,1,0:T(8,128)(2,1)S(1)}, bf16[3,96,768]{2,1,0:T(8,128)(2,1)S(1)}, u32[]{:S(2)}, u32[]{:S(2)}) %collective-permute-start) | collective-permute-done | bytes 442400 | tf_op jit(solution)/shard_map/ppermute | solution.py:38
  27.9 4.1 %collective-permute-done.2 = bf16[3,96,768]{2,1,0:T(8,128)(2,1)S(1)} collective-permute-done((bf16[3,96,768]{2,1,0:T(8,128)(2,1)S(1)}, bf16[3,96,768]{2,1,0:T(8,128)(2,1)S(1)}, u32[]{:S(2)}, u32[]{:S(2)}) %collective-permute-start.2) | collective-permute-done | bytes 442400 | tf_op jit(solution)/shard_map/ppermute | solution.py:44
  32.0 1.3 collective-permute-start.4
  34.1 10.2 %collective-permute-done.4 = bf16[3,96,768]{2,1,0:T(8,128)(2,1)S(1)} collective-permute-done((bf16[3,96,768]{2,1,0:T(8,128)(2,1)S(1)}, bf16[3,96,768]{2,1,0:T(8,128)(2,1)S(1)}, u32[]{:S(2)}, u32[]{:S(2)}) %collective-permute-start.4) | collective-permute-done | bytes 442400 | tf_op jit(solution)/shard_map/ppermute | solution.py:50
  45.4 2.0 concatenate.57.refs_8_.refs_16_.refs_0_
  48.8 4.6 %collective-permute-start.8 = (bf16[512,768]{1,0:T(8,128)(2,1)}, bf16[512,768]{1,0:T(8,128)(2,1)S(1)}, u32[]{:S(2)}, u32[]{:S(2)}) collective-permute-start(bf16[512,768]{1,0:T(8,128)(2,1)} %refs_0_.3), channel_id=1, source_target_pairs={{0,1},{1,2},{2,3},{4,5},{5,6},{6,7},{8,9},{9,10},{10,11},{12,13},{... | collective-permute-start | bytes 2359304 | tf_op jit(solution)/shard_map/ppermute | solution.py:37
  54.7 1.5 collective-permute-start.6
  56.2 13.4 %collective-permute-done.7 = bf16[512,768]{1,0:T(8,128)(2,1)S(1)} collective-permute-done((bf16[512,768]{1,0:T(8,128)(2,1)}, bf16[512,768]{1,0:T(8,128)(2,1)S(1)}, u32[]{:S(2)}, u32[]{:S(2)}) %collective-permute-start.7) | collective-permute-done | bytes 786464 | tf_op jit(solution)/shard_map/ppermute | solution.py:38
  70.9 1.3 copy-done.2
  75.2 18.5 %collective-permute-done.10 = bf16[512,768]{1,0:T(8,128)(2,1)S(1)} collective-permute-done((bf16[512,768]{1,0:T(8,128)(2,1)S(1)}, bf16[512,768]{1,0:T(8,128)(2,1)S(1)}, u32[]{:S(2)}, u32[]{:S(2)}) %collective-permute-start.10) | collective-permute-done | bytes 786464 | tf_op jit(solution)/shard_map/ppermute | solution.py:44
  95.5 1.6 collective-permute-start.12
  100.6 16.6 %collective-permute-done.12.refs_11_.refs_3_ = bf16[96,4608]{1,0:T(8,128)(2,1)} collective-permute-done((bf16[96,4608]{1,0:T(8,128)(2,1)S(1)}, bf16[96,4608]{1,0:T(8,128)(2,1)}, u32[]{:S(2)}, u32[]{:S(2)}) %collective-permute-start.12) | collective-permute-done | bytes 884768 | tf_op jit(solution)/shard_map/ppermute | solution.py:860
  117.2 2.5 collective-permute-done.16.refs_19_.refs_11_
  120.9 1.3 reshape.86.refs_20_
  122.3 2.7 broadcast_select_fusion.refs_3_.refs_1_
  125.0 28.9 %attend_forward.1 = (bf16[512,768]{1,0:T(8,128)(2,1)}, bf16[2048,768]{1,0:T(8,128)(2,1)}, bf16[2048,768]{1,0:T(8,128)(2,1)}, bf16[512,768]{1,0:T(8,128)(2,1)}, f...) custom-call(s32[2048]{0:T(1024)} %bitcast.117, s32[7]{0:T(128)} %concatenate.52.where, bf16[512,768]{1,0:T(8,128)(2,1)} %refs_0_.3, ...), custom_call_target="tpu_custom_call" | custom-call | flops 1000 | bytes 1000 | tf_op jit(solution)/shard_map/attend_forward/pallas_call | solution.py:286
  154.0 28.9 %middle.1 = (bf16[512,768]{1,0:T(8,128)(2,1)}, f32[512,768]{1,0:T(8,128)}, bf16[512,768]{1,0:T(8,128)(2,1)}, bf16[3,512,768]{2,1,0:T(8,128)(2,1)}, bf16[512,6912]{1,0:T(8,128)(2,1)}, /*index=5*/f32[10,768]{1,0:T(8,128)}) custom-call(s32[6]{0:T(128)} %concatenate.53.known, bf16[96,9216]{1,0:T(8,128)(2,1)} %copy-done, bf16[96,9216]{1,0:T(8,128)(2,1)} %copy-done.1, ...), custom_call_target="tpu_custom_call" | custom-call | flops 1000 | bytes 1000 | tf_op jit(solution)/shard_map/middle/pallas_call | solution.py:692
  182.9 15.1 %ffn_grads.1 = (bf16[384,3072]{1,0:T(8,128)(2,1)}, bf16[384,3840]{1,0:T(8,128)(2,1)}, bf16[384,3072]{1,0:T(8,128)(2,1)}, bf16[384,3840]{1,0:T(8,128)(2,1)}) custom-call(s32[1]{0:T(128)} %bitcast.5.place, bf16[3,512,768]{2,1,0:T(8,128)(2,1)} %get-tuple-element.118.left_ref, bf16[512,6912]{1,0:T(8,128)(2,1)} %get-tuple-element.119.right_ref), custom_call_target="tpu_custom_call" | custom-call | flops 1000 | bytes 1000 | tf_op jit(solution)/shard_map/ffn_grads/pallas_call | solution.py:744
  198.5 20.3 %attend_backward.2 = (bf16[1536,768]{1,0:T(8,128)(2,1)}, bf16[1536,768]{1,0:T(8,128)(2,1)}, f32[768,512]{1,0:T(8,128)}, bf16[512,768]{1,0:T(8,128)(2,1)}, bf16[5...) custom-call(s32[2048]{0:T(1024)} %bitcast.118, s32[7]{0:T(128)} %concatenate.52.where, ...), custom_call_target="tpu_custom_call" | custom-call | flops 1000 | bytes 1000 | tf_op jit(solution)/shard_map/attend_backward/pallas_call | solution.py:477
  218.9 3.0 add_convert_fusion.1
  221.9 2.4 collective-permute-start.25
  224.3 1.7 fusion.6
  226.0 28.2 %collective-permute-start.21 = (bf16[512,768]{1,0:T(8,128)(2,1)}, bf16[512,768]{1,0:T(8,128)(2,1)}, u32[]{:S(2)}, u32[]{:S(2)}) collective-permute-start(bf16[512,768]{1,0:T(8,128)(2,1)} %get-tuple-element.128), channel_id=1, source_target_pairs={{0,1},{3,2},{4,5},{7,6},{8,9},{11,10},{12,13},{15,14},{16,17},{19,... | collective-permute-start | bytes 2359304 | tf_op jit(solution)/shard_map/ppermute | solution.py:915
  254.3 20.3 %attend_backward.3 = (bf16[512,768]{1,0:T(8,128)(2,1)}, bf16[512,768]{1,0:T(8,128)(2,1)}, bf16[512,768]{1,0:T(8,128)(2,1)}, f32[512,768]{1,0:T(8,128)}) custom-call(s32[2048]{0:T(1024)} %bitcast.119, s32[7]{0:T(128)} %concatenate.52.where, bf16[512,768]{1,0:T(8,128)(2,1)} %get-tuple-element.116.refs_0_, bf16[512,768]{1,0:T(8,128)(2,1)} %get-tuple-element.122.refs_1_, ...), custom_call_target="tpu_custom_call" | custom-call | flops 1000 | bytes 1000 | tf_op jit(solution)/shard_map/attend_backward/pallas_call | solution.py:477
  274.6 2.4 add_convert_fusion.3
  277.0 2.2 collective-permute-start.22
  279.2 1.5 collective-permute-start.23
  280.8 2.5 fusion
  284.3 2.2 fusion.1
  287.4 1.5 collective-permute-start.29
  289.5 12.9 %attn_grads.1 = (bf16[4,304,768]{2,1,0:T(8,128)(2,1)}, f32[4,304,768]{2,1,0:T(8,128)}) custom-call(s32[1]{0:T(128)} %slice.227.core_ref, bf16[512,768]{1,0:T(8,128)(2,1)} %refs_0_.3, bf16[512,768]{1,0:T(8,128)(2,1)} %broadcast_select_fusion.refs_3_.refs_1_, bf16[512,768]{1,0:T(8,128)(2,1)} %broadcast_select_fusion.1.refs_2_, ...), custom_call_target="tpu_custom_call" | custom-call | flops 1000 | bytes 1000 | tf_op jit(solution)/shard_map/attn_grads/pallas_call | solution.py:555
  302.4 3.7 collective-permute-start.28
  306.1 3.3 fusion.2
  309.4 2.2 collective-permute-start.26
  315.8 1.8 copy-done.4
  317.7 1.7 add_convert_fusion
  319.3 3.6 all-to-all-start
  323.2 2.7 collective-permute-start.31
  327.4 1.5 collective-permute-done.26
  328.9 12.7 %collective-permute-done.27 = bf16[512,768]{1,0:T(8,128)(2,1)} collective-permute-done((bf16[512,768]{1,0:T(8,128)(2,1)}, bf16[512,768]{1,0:T(8,128)(2,1)}, u32[]{:S(2)}, u32[]{:S(2)}) %collective-permute-start.27) | collective-permute-done | bytes 786464 | tf_op jit(solution)/shard_map/ppermute | solution.py:969
  341.6 2.8 convert_add_fusion.1
  344.4 4.1 %collective-permute-done.32 = bf16[96,1728]{1,0:T(8,128)(2,1)S(1)} collective-permute-done((bf16[96,1728]{1,0:T(8,128)(2,1)S(1)}, bf16[96,1728]{1,0:T(8,128)(2,1)S(1)}, u32[]{:S(2)}, u32[]{:S(2)}) %collective-permute-start.32) | collective-permute-done | bytes 331808 | tf_op jit(solution)/shard_map/ppermute | solution.py:72
  348.5 13.0 %collective-permute-done.33 = bf16[96,1728]{1,0:T(8,128)(2,1)S(1)} collective-permute-done((bf16[96,1728]{1,0:T(8,128)(2,1)S(1)}, bf16[96,1728]{1,0:T(8,128)(2,1)S(1)}, u32[]{:S(2)}, u32[]{:S(2)}) %collective-permute-start.33) | collective-permute-done | bytes 331808 | tf_op jit(solution)/shard_map/ppermute | solution.py:72
  365.6 3.8 collective-permute-start.35
  370.3 4.4 %collective-permute-done.34.refs_1_ = bf16[336,192]{1,0:T(8,128)(2,1)S(1)} collective-permute-done((bf16[336,192]{1,0:T(8,128)(2,1)S(1)}, bf16[336,192]{1,0:T(8,128)(2,1)S(1)}, u32[]{:S(2)}, u32[]{:S(2)}) %collective-permute-start.34) | collective-permute-done | bytes 129056 | tf_op jit(solution)/shard_map/ppermute | solution.py:72
  375.4 6.3 %collective-permute-done.36.refs_3_ = bf16[336,192]{1,0:T(8,128)(2,1)S(1)} collective-permute-done((bf16[336,192]{1,0:T(8,128)(2,1)S(1)}, bf16[336,192]{1,0:T(8,128)(2,1)S(1)}, u32[]{:S(2)}, u32[]{:S(2)}) %collective-permute-start.36) | collective-permute-done | bytes 129056 | tf_op jit(solution)/shard_map/ppermute | solution.py:72
  382.3 1.9 finish.1
  (169 shorter events, 43.6 us)
Async XLA Ops:
  0.7 26.2 %copy-start.25 = (f32[768]{0:T(1024)S(1)}, f32[768]{0:T(1024)}, u32[]{:S(2)}) copy-start(f32[768]{0:T(1024)} %param.34) | copy-start | bytes 9220
  0.7 26.2 %copy-start.26 = (f32[768]{0:T(1024)S(1)}, f32[768]{0:T(1024)}, u32[]{:S(2)}) copy-start(f32[768]{0:T(1024)} %param.26) | copy-start | bytes 9220
  0.7 26.3 %copy-start.27 = (f32[768]{0:T(1024)S(1)}, f32[768]{0:T(1024)}, u32[]{:S(2)}) copy-start(f32[768]{0:T(1024)} %param.27) | copy-start | bytes 9220
  0.7 26.3 %copy-start.28 = (f32[768]{0:T(1024)S(1)}, f32[768]{0:T(1024)}, u32[]{:S(2)}) copy-start(f32[768]{0:T(1024)} %param.28) | copy-start | bytes 9220
  3.6 15.1 %collective-permute-start = (bf16[3,96,768]{2,1,0:T(8,128)(2,1)S(1)}, bf16[3,96,768]{2,1,0:T(8,128)(2,1)S(1)}, u32[]{:S(2)}, u32[]{:S(2)}) collective-permute-start(bf16[3,96,768]{2,1,0:T(8,128)(2,1)S(1)} %pad_maximum_fusion.2), channel_id=1, source_target_pairs={{1,0},{2,1},{3,2},{5,4},{6,5},{7,6},{9,8},{10,9},{11,10},{13,12},{... | collective-permute-start | bytes 1327112 | tf_op jit(solution)/shard_map/ppermute | solution.py:38
  4.9 15.1 %collective-permute-start.1 = (bf16[3,96,768]{2,1,0:T(8,128)(2,1)S(1)}, bf16[3,96,768]{2,1,0:T(8,128)(2,1)S(1)}, u32[]{:S(2)}, u32[]{:S(2)}) collective-permute-start(bf16[3,96,768]{2,1,0:T(8,128)(2,1)S(1)} %pad_maximum_fusion.2), channel_id=1, source_target_pairs={{0,1},{1,2},{2,3},{4,5},{5,6},{6,7},{8,9},{9,10},{10,11},{12,13},{... | collective-permute-start | bytes 1327112 | tf_op jit(solution)/shard_map/ppermute | solution.py:37
  18.7 13.2 %collective-permute-start.2 = (bf16[3,96,768]{2,1,0:T(8,128)(2,1)S(1)}, bf16[3,96,768]{2,1,0:T(8,128)(2,1)S(1)}, u32[]{:S(2)}, u32[]{:S(2)}) collective-permute-start(bf16[3,96,768]{2,1,0:T(8,128)(2,1)S(1)} %collective-permute-done), channel_id=1, source_target_pairs={{2,1},{1,0},{6,5},{5,4},{10,9},{9,8},{14,13},{13,12},{18,17},{17,1... | collective-permute-start | bytes 1327112 | tf_op jit(solution)/shard_map/ppermute | solution.py:44
  20.0 11.9 %collective-permute-start.3 = (bf16[3,96,768]{2,1,0:T(8,128)(2,1)S(1)}, bf16[3,96,768]{2,1,0:T(8,128)(2,1)S(1)}, u32[]{:S(2)}, u32[]{:S(2)}) collective-permute-start(bf16[3,96,768]{2,1,0:T(8,128)(2,1)S(1)} %collective-permute-done.1), channel_id=1, source_target_pairs={{1,2},{2,3},{5,6},{6,7},{9,10},{10,11},{13,14},{14,15},{17,18},{18... | collective-permute-start | bytes 1327112 | tf_op jit(solution)/shard_map/ppermute | solution.py:43
  21.4 23.0 %copy-start.9 = (s32[1,2048]{1,0:T(1,128)}, s32[1,2048]{1,0:T(1,128)S(1)}, u32[]{:S(2)}) copy-start(s32[1,2048]{1,0:T(1,128)S(1)} %compare_select_fusion.refs_4_.refs_5_.refs_6_.refs_7_.refs_26_.refs_9_.refs_10_.refs_11_) | copy-start | bytes 24580
  32.0 12.3 %collective-permute-start.4 = (bf16[3,96,768]{2,1,0:T(8,128)(2,1)S(1)}, bf16[3,96,768]{2,1,0:T(8,128)(2,1)S(1)}, u32[]{:S(2)}, u32[]{:S(2)}) collective-permute-start(bf16[3,96,768]{2,1,0:T(8,128)(2,1)S(1)} %broadcast_select_fusion.4), channel_id=1, source_target_pairs={{1,0},{2,3},{5,4},{6,7},{9,8},{10,11},{13,12},{14,15},{17,16},{18,... | collective-permute-start | bytes 1327112 | tf_op jit(solution)/shard_map/ppermute | solution.py:50
  47.4 47.2 %copy-start = (bf16[96,9216]{1,0:T(8,128)(2,1)}, bf16[96,9216]{1,0:T(8,128)(2,1)S(1)}, u32[]{:S(2)}) copy-start(bf16[96,9216]{1,0:T(8,128)(2,1)S(1)} %concatenate.57.refs_8_.refs_16_.refs_0_) | copy-start | bytes 5308420
  47.5 23.4 %collective-permute-start.9 = (bf16[96,9216]{1,0:T(8,128)(2,1)S(1)}, bf16[96,9216]{1,0:T(8,128)(2,1)S(1)}, u32[]{:S(2)}, u32[]{:S(2)}) collective-permute-start(bf16[96,9216]{1,0:T(8,128)(2,1)S(1)} %concatenate.57.refs_8_.refs_16_.refs_0_), channel_id=1, source_target_pairs={{0,4},{4,0},{8,12},{12,8},{16,20},{20,16},{24,28},{28,24},{1,5},{5... | collective-permute-start | bytes 5308424 | tf_op jit(solution)/shard_map/ppermute | solution.py:860
  47.5 22.0 %collective-permute-start.7 = (bf16[512,768]{1,0:T(8,128)(2,1)}, bf16[512,768]{1,0:T(8,128)(2,1)S(1)}, u32[]{:S(2)}, u32[]{:S(2)}) collective-permute-start(bf16[512,768]{1,0:T(8,128)(2,1)} %refs_0_.3), channel_id=1, source_target_pairs={{1,0},{2,1},{3,2},{5,4},{6,5},{7,6},{9,8},{10,9},{11,10},{13,12},{... | collective-permute-start | bytes 2359304 | tf_op jit(solution)/shard_map/ppermute | solution.py:38
  48.8 22.0 %collective-permute-start.8 = (bf16[512,768]{1,0:T(8,128)(2,1)}, bf16[512,768]{1,0:T(8,128)(2,1)S(1)}, u32[]{:S(2)}, u32[]{:S(2)}) collective-permute-start(bf16[512,768]{1,0:T(8,128)(2,1)} %refs_0_.3), channel_id=1, source_target_pairs={{0,1},{1,2},{2,3},{4,5},{5,6},{6,7},{8,9},{9,10},{10,11},{12,13},{... | collective-permute-start | bytes 2359304 | tf_op jit(solution)/shard_map/ppermute | solution.py:37
  53.4 41.2 %collective-permute-start.5 = (bf16[96,9216]{1,0:T(8,128)(2,1)S(1)}, bf16[96,9216]{1,0:T(8,128)(2,1)S(1)}, u32[]{:S(2)}, u32[]{:S(2)}) collective-permute-start(bf16[96,9216]{1,0:T(8,128)(2,1)S(1)} %concatenate.57.refs_8_.refs_16_.refs_0_), channel_id=1, source_target_pairs={{0,8},{4,12},{8,0},{12,4},{16,24},{20,28},{24,16},{28,20},{1,9},{5... | collective-permute-start | bytes 5308424 | tf_op jit(solution)/shard_map/ppermute | solution.py:860
  54.7 40.3 %collective-permute-start.6 = (bf16[96,9216]{1,0:T(8,128)(2,1)S(1)}, bf16[96,9216]{1,0:T(8,128)(2,1)}, u32[]{:S(2)}, u32[]{:S(2)}) collective-permute-start(bf16[96,9216]{1,0:T(8,128)(2,1)S(1)} %concatenate.57.refs_8_.refs_16_.refs_0_), channel_id=1, source_target_pairs={{0,16},{4,20},{8,24},{12,28},{16,0},{20,4},{24,8},{28,12},{1,17},{... | collective-permute-start | bytes 5308424 | tf_op jit(solution)/shard_map/ppermute | solution.py:860
  70.9 28.5 %copy-start.5 = (bf16[512,768]{1,0:T(8,128)(2,1)}, bf16[512,768]{1,0:T(8,128)(2,1)S(1)}, u32[]{:S(2)}) copy-start(bf16[512,768]{1,0:T(8,128)(2,1)S(1)} %collective-permute-done.8) | copy-start | bytes 2359300
  72.2 21.5 %collective-permute-start.10 = (bf16[512,768]{1,0:T(8,128)(2,1)S(1)}, bf16[512,768]{1,0:T(8,128)(2,1)S(1)}, u32[]{:S(2)}, u32[]{:S(2)}) collective-permute-start(bf16[512,768]{1,0:T(8,128)(2,1)S(1)} %collective-permute-done.7), channel_id=1, source_target_pairs={{2,1},{1,0},{6,5},{5,4},{10,9},{9,8},{14,13},{13,12},{18,17},{17,1... | collective-permute-start | bytes 2359304 | tf_op jit(solution)/shard_map/ppermute | solution.py:44
  73.5 20.2 %collective-permute-start.11 = (bf16[512,768]{1,0:T(8,128)(2,1)S(1)}, bf16[512,768]{1,0:T(8,128)(2,1)S(1)}, u32[]{:S(2)}, u32[]{:S(2)}) collective-permute-start(bf16[512,768]{1,0:T(8,128)(2,1)S(1)} %collective-permute-done.8), channel_id=1, source_target_pairs={{1,2},{2,3},{5,6},{6,7},{9,10},{10,11},{13,14},{14,15},{17,18},{18... | collective-permute-start | bytes 2359304 | tf_op jit(solution)/shard_map/ppermute | solution.py:43
  94.9 27.3 %collective-permute-start.13 = (bf16[96,9216]{1,0:T(8,128)(2,1)S(1)}, bf16[96,9216]{1,0:T(8,128)(2,1)S(1)}, u32[]{:S(2)}, u32[]{:S(2)}) collective-permute-start(bf16[96,9216]{1,0:T(8,128)(2,1)S(1)} %collective-permute-done.5.refs_9_.refs_17_.refs_1_), channel_id=1, source_target_pairs={{0,4},{4,0},{8,12},{12,8},{16,20},{20,16},{24,28},{28,24},{1,5},{5... | collective-permute-start | bytes 5308424 | tf_op jit(solution)/shard_map/ppermute | solution.py:860
  94.9 27.3 %collective-permute-start.14 = (bf16[96,9216]{1,0:T(8,128)(2,1)}, bf16[96,9216]{1,0:T(8,128)(2,1)}, u32[]{:S(2)}, u32[]{:S(2)}) collective-permute-start(bf16[96,9216]{1,0:T(8,128)(2,1)} %collective-permute-done.6.refs_10_.refs_18_.refs_2_), channel_id=1, source_target_pairs={{0,4},{4,0},{8,12},{12,8},{16,20},{20,16},{24,28},{28,24},{1,5},{5... | collective-permute-start | bytes 5308424 | tf_op jit(solution)/shard_map/ppermute | solution.py:860
  95.5 21.7 %collective-permute-start.12 = (bf16[96,4608]{1,0:T(8,128)(2,1)S(1)}, bf16[96,4608]{1,0:T(8,128)(2,1)}, u32[]{:S(2)}, u32[]{:S(2)}) collective-permute-start(bf16[96,4608]{1,0:T(8,128)(2,1)S(1)} %slice.221), channel_id=1, source_target_pairs={{0,16},{4,20},{8,24},{12,28},{16,0},{20,4},{24,8},{28,12},{1,17},{... | collective-permute-start | bytes 2654216 | tf_op jit(solution)/shard_map/ppermute | solution.py:860
  98.3 21.4 %collective-permute-start.16 = (bf16[96,4608]{1,0:T(8,128)(2,1)S(1)}, bf16[96,4608]{1,0:T(8,128)(2,1)}, u32[]{:S(2)}, u32[]{:S(2)}) collective-permute-start(bf16[96,4608]{1,0:T(8,128)(2,1)S(1)} %slice.222), channel_id=1, source_target_pairs={{0,8},{4,12},{8,0},{12,4},{16,24},{20,28},{24,16},{28,20},{1,9},{5... | collective-permute-start | bytes 2654216 | tf_op jit(solution)/shard_map/ppermute | solution.py:860
  99.3 22.9 %collective-permute-start.18 = (bf16[512,768]{1,0:T(8,128)(2,1)}, bf16[512,768]{1,0:T(8,128)(2,1)}, u32[]{:S(2)}, u32[]{:S(2)}) collective-permute-start(bf16[512,768]{1,0:T(8,128)(2,1)} %broadcast_select_fusion.1.refs_2_), channel_id=1, source_target_pairs={{1,0},{2,3},{5,4},{6,7},{9,8},{10,11},{13,12},{14,15},{17,16},{18,... | collective-permute-start | bytes 2359304 | tf_op jit(solution)/shard_map/ppermute | solution.py:50
  117.2 7.8 %collective-permute-start.15 = (bf16[96,4608]{1,0:T(8,128)(2,1)}, bf16[96,4608]{1,0:T(8,128)(2,1)}, u32[]{:S(2)}, u32[]{:S(2)}) collective-permute-start(bf16[96,4608]{1,0:T(8,128)(2,1)} %collective-permute-done.12.refs_11_.refs_3_), channel_id=1, source_target_pairs={{0,4},{4,0},{8,12},{12,8},{16,20},{20,16},{24,28},{28,24},{1,5},{5... | collective-permute-start | bytes 2654216 | tf_op jit(solution)/shard_map/ppermute | solution.py:860
  119.8 5.3 %collective-permute-start.17 = (bf16[96,4608]{1,0:T(8,128)(2,1)}, bf16[96,4608]{1,0:T(8,128)(2,1)}, u32[]{:S(2)}, u32[]{:S(2)}) collective-permute-start(bf16[96,4608]{1,0:T(8,128)(2,1)} %collective-permute-done.16.refs_19_.refs_11_), channel_id=1, source_target_pairs={{0,4},{4,0},{8,12},{12,8},{16,20},{20,16},{24,28},{28,24},{1,5},{5... | collective-permute-start | bytes 2654216 | tf_op jit(solution)/shard_map/ppermute | solution.py:860
  198.0 20.9 %collective-permute-start.20 = (bf16[384,3840]{1,0:T(8,128)(2,1)}, bf16[384,3840]{1,0:T(8,128)(2,1)}, u32[]{:S(2)}, u32[]{:S(2)}) collective-permute-start(bf16[384,3840]{1,0:T(8,128)(2,1)} %get-tuple-element.121), channel_id=1, source_target_pairs={{0,4},{4,0},{8,12},{12,8},{16,20},{20,16},{24,28},{28,24},{1,5},{5... | collective-permute-start | bytes 8847368 | tf_op jit(solution)/shard_map/ppermute | solution.py:910
  198.0 20.9 %collective-permute-start.19 = (bf16[384,3072]{1,0:T(8,128)(2,1)}, bf16[384,3072]{1,0:T(8,128)(2,1)}, u32[]{:S(2)}, u32[]{:S(2)}) collective-permute-start(bf16[384,3072]{1,0:T(8,128)(2,1)} %get-tuple-element.120), channel_id=1, source_target_pairs={{0,4},{4,0},{8,12},{12,8},{16,20},{20,16},{24,28},{28,24},{1,5},{5... | collective-permute-start | bytes 7077896 | tf_op jit(solution)/shard_map/ppermute | solution.py:910
  198.5 20.4 %copy-start.6 = (bf16[384,3840]{1,0:T(8,128)(2,1)S(1)}, bf16[384,3840]{1,0:T(8,128)(2,1)}, u32[]{:S(2)}) copy-start(bf16[384,3840]{1,0:T(8,128)(2,1)} %get-tuple-element.131) | copy-start | bytes 8847364
  221.9 58.9 %collective-permute-start.25 = (bf16[2,96,3840]{2,1,0:T(8,128)(2,1)}, bf16[2,96,3840]{2,1,0:T(8,128)(2,1)S(1)}, u32[]{:S(2)}, u32[]{:S(2)}) collective-permute-start(bf16[2,96,3840]{2,1,0:T(8,128)(2,1)} %bitcast.33), channel_id=1, source_target_pairs={{0,16},{4,20},{8,24},{12,28},{16,0},{20,4},{24,8},{28,12},{1,17},{... | collective-permute-start | bytes 4423688 | tf_op jit(solution)/shard_map/ppermute | solution.py:928
  226.0 54.8 %collective-permute-start.24 = (bf16[2,96,3072]{2,1,0:T(8,128)(2,1)S(1)}, bf16[2,96,3072]{2,1,0:T(8,128)(2,1)}, u32[]{:S(2)}, u32[]{:S(2)}) collective-permute-start(bf16[2,96,3072]{2,1,0:T(8,128)(2,1)S(1)} %fusion.6), channel_id=1, source_target_pairs={{0,8},{4,12},{8,0},{12,4},{16,24},{20,28},{24,16},{28,20},{1,9},{5... | collective-permute-start | bytes 3538952 | tf_op jit(solution)/shard_map/ppermute | solution.py:928
  226.0 48.5 %collective-permute-start.21 = (bf16[512,768]{1,0:T(8,128)(2,1)}, bf16[512,768]{1,0:T(8,128)(2,1)}, u32[]{:S(2)}, u32[]{:S(2)}) collective-permute-start(bf16[512,768]{1,0:T(8,128)(2,1)} %get-tuple-element.128), channel_id=1, source_target_pairs={{0,1},{3,2},{4,5},{7,6},{8,9},{11,10},{12,13},{15,14},{16,17},{19,... | collective-permute-start | bytes 2359304 | tf_op jit(solution)/shard_map/ppermute | solution.py:915
  277.0 29.1 %collective-permute-start.22 = (bf16[512,768]{1,0:T(8,128)(2,1)}, bf16[512,768]{1,0:T(8,128)(2,1)}, u32[]{:S(2)}, u32[]{:S(2)}) collective-permute-start(bf16[512,768]{1,0:T(8,128)(2,1)} %add_convert_fusion.3), channel_id=1, source_target_pairs={{0,1},{3,2},{4,5},{7,6},{8,9},{11,10},{12,13},{15,14},{16,17},{19,... | collective-permute-start | bytes 2359304 | tf_op jit(solution)/shard_map/ppermute | solution.py:933
  279.2 26.9 %collective-permute-start.23 = (bf16[512,768]{1,0:T(8,128)(2,1)}, bf16[512,768]{1,0:T(8,128)(2,1)}, u32[]{:S(2)}, u32[]{:S(2)}) collective-permute-start(bf16[512,768]{1,0:T(8,128)(2,1)} %add_convert_fusion.3), channel_id=1, source_target_pairs={{1,2},{2,1},{5,6},{6,5},{9,10},{10,9},{13,14},{14,13},{17,18},{18,... | collective-permute-start | bytes 2359304 | tf_op jit(solution)/shard_map/ppermute | solution.py:934
  284.2 28.7 %collective-permute-start.30 = (bf16[96,3840]{1,0:T(8,128)(2,1)}, bf16[96,3840]{1,0:T(8,128)(2,1)}, u32[]{:S(2)}, u32[]{:S(2)}) collective-permute-start(bf16[96,3840]{1,0:T(8,128)(2,1)} %slice_bitcast_fusion.3), channel_id=1, source_target_pairs={{0,8},{4,12},{8,0},{12,4},{16,24},{20,28},{24,16},{28,20},{1,9},{5... | collective-permute-start | bytes 2211848 | tf_op jit(solution)/shard_map/ppermute | solution.py:114
  287.4 25.5 %collective-permute-start.29 = (bf16[96,3072]{1,0:T(8,128)(2,1)}, bf16[96,3072]{1,0:T(8,128)(2,1)}, u32[]{:S(2)}, u32[]{:S(2)}) collective-permute-start(bf16[96,3072]{1,0:T(8,128)(2,1)} %slice_bitcast_fusion.5), channel_id=1, source_target_pairs={{0,16},{4,20},{8,24},{12,28},{16,0},{20,4},{24,8},{28,12},{1,17},{... | collective-permute-start | bytes 1769480 | tf_op jit(solution)/shard_map/ppermute | solution.py:114
  302.4 13.4 %collective-permute-start.28 = (bf16[4,304,768]{2,1,0:T(8,128)(2,1)}, bf16[4,304,768]{2,1,0:T(8,128)(2,1)S(1)}, u32[]{:S(2)}, u32[]{:S(2)}) collective-permute-start(bf16[4,304,768]{2,1,0:T(8,128)(2,1)} %get-tuple-element.152), channel_id=1, source_target_pairs={{0,4},{4,0},{8,12},{12,8},{16,20},{20,16},{24,28},{28,24},{1,5},{5... | collective-permute-start | bytes 5603336 | tf_op jit(solution)/shard_map/ppermute | solution.py:963
  309.4 19.5 %collective-permute-start.26 = (bf16[512,768]{1,0:T(8,128)(2,1)}, bf16[512,768]{1,0:T(8,128)(2,1)}, u32[]{:S(2)}, u32[]{:S(2)}) collective-permute-start(bf16[512,768]{1,0:T(8,128)(2,1)} %get-tuple-element.188), channel_id=1, source_target_pairs={{0,1},{1,2},{2,3},{4,5},{5,6},{6,7},{8,9},{9,10},{10,11},{12,13},{... | collective-permute-start | bytes 2359304 | tf_op jit(solution)/shard_map/ppermute | solution.py:968
  311.6 30.0 %collective-permute-start.27 = (bf16[512,768]{1,0:T(8,128)(2,1)}, bf16[512,768]{1,0:T(8,128)(2,1)}, u32[]{:S(2)}, u32[]{:S(2)}) collective-permute-start(bf16[512,768]{1,0:T(8,128)(2,1)} %get-tuple-element.189), channel_id=1, source_target_pairs={{1,0},{2,1},{3,2},{5,4},{6,5},{7,6},{9,8},{10,9},{11,10},{13,12},{... | collective-permute-start | bytes 2359304 | tf_op jit(solution)/shard_map/ppermute | solution.py:969
  319.3 43.1 %all-to-all-start = ((bf16[4,304,768]{2,1,0:T(8,128)(2,1)}), bf16[4,304,768]{2,1,0:T(8,128)(2,1)S(1)}, u32[]{:S(2)}, u32[]{:S(2)}) async-start(bf16[4,304,768]{2,1,0:T(8,128)(2,1)} %add_convert_fusion), calls=%async_computation | async-start | bytes 3735552 | tf_op jit(solution)/shard_map/all_to_all | solution.py:991
  323.1 18.5 %copy-start.10 = (f32[512,768]{1,0:T(8,128)S(1)}, f32[512,768]{1,0:T(8,128)}, u32[]{:S(2)}) copy-start(f32[512,768]{1,0:T(8,128)} %get-tuple-element.135) | copy-start | bytes 4718596
  323.2 21.2 %collective-permute-start.31 = (bf16[96,1728]{1,0:T(8,128)(2,1)S(1)}, bf16[96,1728]{1,0:T(8,128)(2,1)S(1)}, u32[]{:S(2)}, u32[]{:S(2)}) collective-permute-start(bf16[96,1728]{1,0:T(8,128)(2,1)S(1)} %get-tuple-element.192), channel_id=1, source_target_pairs={{0,1},{1,2},{2,3},{3,0},{4,5},{5,6},{6,7},{7,4},{8,9},{9,10},{10,1... | collective-permute-start | bytes 995336 | tf_op jit(solution)/shard_map/ppermute | solution.py:72
  325.9 22.6 %collective-permute-start.32 = (bf16[96,1728]{1,0:T(8,128)(2,1)S(1)}, bf16[96,1728]{1,0:T(8,128)(2,1)S(1)}, u32[]{:S(2)}, u32[]{:S(2)}) collective-permute-start(bf16[96,1728]{1,0:T(8,128)(2,1)S(1)} %get-tuple-element.191), channel_id=1, source_target_pairs={{0,3},{1,0},{2,1},{3,2},{4,7},{5,4},{6,5},{7,6},{8,11},{9,8},{10,9... | collective-permute-start | bytes 995336 | tf_op jit(solution)/shard_map/ppermute | solution.py:72
  327.1 34.4 %copy-start.16 = (bf16[96,192]{1,0:T(8,128)(2,1)S(1)}, bf16[96,192]{1,0:T(8,128)(2,1)}, u32[]{:S(2)}) copy-start(bf16[96,192]{1,0:T(8,128)(2,1)} %copy-done.15) | copy-start | bytes 110596
  327.1 34.4 %collective-permute-start.33 = (bf16[96,1728]{1,0:T(8,128)(2,1)S(1)}, bf16[96,1728]{1,0:T(8,128)(2,1)S(1)}, u32[]{:S(2)}, u32[]{:S(2)}) collective-permute-start(bf16[96,1728]{1,0:T(8,128)(2,1)S(1)} %get-tuple-element.190), channel_id=1, source_target_pairs={{0,2},{1,3},{2,0},{3,1},{4,6},{5,7},{6,4},{7,5},{8,10},{9,11},{10,... | collective-permute-start | bytes 995336 | tf_op jit(solution)/shard_map/ppermute | solution.py:72
  365.6 9.2 %collective-permute-start.34 = (bf16[336,192]{1,0:T(8,128)(2,1)S(1)}, bf16[336,192]{1,0:T(8,128)(2,1)S(1)}, u32[]{:S(2)}, u32[]{:S(2)}) collective-permute-start(bf16[336,192]{1,0:T(8,128)(2,1)S(1)} %get-tuple-element.205), channel_id=1, source_target_pairs={{0,1},{1,2},{2,3},{3,0},{4,5},{5,6},{6,7},{7,4},{8,9},{9,10},{10,1... | collective-permute-start | bytes 387080 | tf_op jit(solution)/shard_map/ppermute | solution.py:72
  365.6 9.7 %collective-permute-start.35 = (bf16[336,192]{1,0:T(8,128)(2,1)S(1)}, bf16[336,192]{1,0:T(8,128)(2,1)S(1)}, u32[]{:S(2)}, u32[]{:S(2)}) collective-permute-start(bf16[336,192]{1,0:T(8,128)(2,1)S(1)} %get-tuple-element.204), channel_id=1, source_target_pairs={{0,3},{1,0},{2,1},{3,2},{4,7},{5,4},{6,5},{7,6},{8,11},{9,8},{10,9... | collective-permute-start | bytes 387080 | tf_op jit(solution)/shard_map/ppermute | solution.py:72
  369.4 12.2 %collective-permute-start.36 = (bf16[336,192]{1,0:T(8,128)(2,1)S(1)}, bf16[336,192]{1,0:T(8,128)(2,1)S(1)}, u32[]{:S(2)}, u32[]{:S(2)}) collective-permute-start(bf16[336,192]{1,0:T(8,128)(2,1)S(1)} %get-tuple-element.203), channel_id=1, source_target_pairs={{0,2},{1,3},{2,0},{3,1},{4,6},{5,7},{6,4},{7,5},{8,10},{9,11},{10,... | collective-permute-start | bytes 387080 | tf_op jit(solution)/shard_map/ppermute | solution.py:72
  (19 other events, 66.0 us)

commit v5 on v4

--- a/solution.py
+++ b/solution.py
@@ -661,7 +661,7 @@
         acc_s[...] += nt(g_pre, w_s[0, t])
         return 0
 
-    lax.fori_loop(0, parts, back, 0)
+    lax.fori_loop(0, parts, back, 0, unroll=2)
     g_normed = acc_s[...]
     n1 = n1_s[...]
     g_first = norm_back(g_normed, n1, r1_s[:, 0:1], vec_ref[1:2, :])

time: 386 us -> 389 us (level); the launches traced: 384 us -> 383 us
    ppermute x1, starting transfers between devices: 28.2 us -> 24.2 us  [on_device(): r1 = lax.ppermute(dx_b, 'tensor', [(0, 1), (3, 2)])]
where the time goes in v5:
time: 389 us; the launch traced here: 383 us
  Pallas kernels  128 us (33%)
  waiting for transfers between devices  117 us (30%)
  starting transfers between devices  80.8 us (21%)
  other arithmetic  31.5 us (8%)
  local copies, waits for them, and re-layouts  24.3 us (6%)
    pallas_call x2, Pallas kernels, attend_backward(): pl.pallas_call(partial(backward_kernel, slots=slots, first=first, last=la...  40.4 us
    pallas_call x1, Pallas kernels, attend_forward(): pl.pallas_call(partial(forward_kernel, slots=slots, count=count, offsets=...  28.8 us
    ppermute x6, waiting for transfers between devices, spread(): lax.ppermute(block, 'tensor', [(i, (i + shift) % 4) for i in range(4)])  28.4 us
    pallas_call x1, Pallas kernels, middle(): pl.pallas_call(partial(middle_kernel, count=count, offsets=offsets), out_...  28.4 us
    ppermute x1, starting transfers between devices, on_device(): r1 = lax.ppermute(dx_b, 'tensor', [(0, 1), (3, 2)])  24.2 us
    ppermute x2, waiting for transfers between devices, line_second(): above2 = lax.ppermute(above, 'tensor', [(2, 1), (1, 0)])  22.5 us
    ppermute x2, waiting for transfers between devices, line_first(): above = lax.ppermute(own, 'tensor', [(1, 0), (2, 1), (3, 2)])  21.6 us
    ppermute x9, waiting for transfers between devices, over(): return lax.ppermute(block, 'fsdp', partner(bit))  19.3 us
  transfers between devices with their start and end apart: 38, of which 16 were waited for; matrix products, arithmetic and copies ran while one was open for 10% of the time, Pallas kernels for 14%

profile of v5, /device:TPU:0, one launch (start us, length us, event | category | flops | bytes accessed | tf_op | source)
XLA Modules:
  0.0 383.1 jit_solution(12340114347558401191)
XLA Ops:
  3.6 1.3 collective-permute-start
  4.9 5.6 %collective-permute-start.1 = (bf16[3,96,768]{2,1,0:T(8,128)(2,1)S(1)}, bf16[3,96,768]{2,1,0:T(8,128)(2,1)S(1)}, u32[]{:S(2)}, u32[]{:S(2)}) collective-permute-start(bf16[3,96,768]{2,1,0:T(8,128)(2,1)S(1)} %pad_maximum_fusion.2), channel_id=1, source_target_pairs={{0,1},{1,2},{2,3},{4,5},{5,6},{6,7},{8,9},{9,10},{10,11},{12,13},{... | collective-permute-start | bytes 1327112 | tf_op jit(solution)/shard_map/ppermute | solution.py:37
  10.5 8.2 %collective-permute-done = bf16[3,96,768]{2,1,0:T(8,128)(2,1)S(1)} collective-permute-done((bf16[3,96,768]{2,1,0:T(8,128)(2,1)S(1)}, bf16[3,96,768]{2,1,0:T(8,128)(2,1)S(1)}, u32[]{:S(2)}, u32[]{:S(2)}) %collective-permute-start) | collective-permute-done | bytes 442400 | tf_op jit(solution)/shard_map/ppermute | solution.py:38
  27.9 4.1 %collective-permute-done.2 = bf16[3,96,768]{2,1,0:T(8,128)(2,1)S(1)} collective-permute-done((bf16[3,96,768]{2,1,0:T(8,128)(2,1)S(1)}, bf16[3,96,768]{2,1,0:T(8,128)(2,1)S(1)}, u32[]{:S(2)}, u32[]{:S(2)}) %collective-permute-start.2) | collective-permute-done | bytes 442400 | tf_op jit(solution)/shard_map/ppermute | solution.py:44
  34.1 10.2 %collective-permute-done.4 = bf16[3,96,768]{2,1,0:T(8,128)(2,1)S(1)} collective-permute-done((bf16[3,96,768]{2,1,0:T(8,128)(2,1)S(1)}, bf16[3,96,768]{2,1,0:T(8,128)(2,1)S(1)}, u32[]{:S(2)}, u32[]{:S(2)}) %collective-permute-start.4) | collective-permute-done | bytes 442400 | tf_op jit(solution)/shard_map/ppermute | solution.py:50
  45.4 2.0 concatenate.57.refs_8_.refs_16_.refs_0_
  48.8 4.6 %collective-permute-start.8 = (bf16[512,768]{1,0:T(8,128)(2,1)}, bf16[512,768]{1,0:T(8,128)(2,1)S(1)}, u32[]{:S(2)}, u32[]{:S(2)}) collective-permute-start(bf16[512,768]{1,0:T(8,128)(2,1)} %refs_0_.3), channel_id=1, source_target_pairs={{0,1},{1,2},{2,3},{4,5},{5,6},{6,7},{8,9},{9,10},{10,11},{12,13},{... | collective-permute-start | bytes 2359304 | tf_op jit(solution)/shard_map/ppermute | solution.py:37
  54.7 1.5 collective-permute-start.6
  56.2 13.4 %collective-permute-done.7 = bf16[512,768]{1,0:T(8,128)(2,1)S(1)} collective-permute-done((bf16[512,768]{1,0:T(8,128)(2,1)}, bf16[512,768]{1,0:T(8,128)(2,1)S(1)}, u32[]{:S(2)}, u32[]{:S(2)}) %collective-permute-start.7) | collective-permute-done | bytes 786464 | tf_op jit(solution)/shard_map/ppermute | solution.py:38
  70.9 1.3 copy-done.2
  75.2 18.5 %collective-permute-done.10 = bf16[512,768]{1,0:T(8,128)(2,1)S(1)} collective-permute-done((bf16[512,768]{1,0:T(8,128)(2,1)S(1)}, bf16[512,768]{1,0:T(8,128)(2,1)S(1)}, u32[]{:S(2)}, u32[]{:S(2)}) %collective-permute-start.10) | collective-permute-done | bytes 786464 | tf_op jit(solution)/shard_map/ppermute | solution.py:44
  95.5 1.6 collective-permute-start.12
  99.3 1.5 collective-permute-start.18
  100.8 16.4 %collective-permute-done.12.refs_11_.refs_3_ = bf16[96,4608]{1,0:T(8,128)(2,1)} collective-permute-done((bf16[96,4608]{1,0:T(8,128)(2,1)S(1)}, bf16[96,4608]{1,0:T(8,128)(2,1)}, u32[]{:S(2)}, u32[]{:S(2)}) %collective-permute-start.12) | collective-permute-done | bytes 884768 | tf_op jit(solution)/shard_map/ppermute | solution.py:860
  117.2 2.5 collective-permute-done.16.refs_19_.refs_11_
  120.9 1.3 reshape.86.refs_20_
  122.3 2.7 broadcast_select_fusion.refs_3_.refs_1_
  125.0 28.8 %attend_forward.1 = (bf16[512,768]{1,0:T(8,128)(2,1)}, bf16[2048,768]{1,0:T(8,128)(2,1)}, bf16[2048,768]{1,0:T(8,128)(2,1)}, bf16[512,768]{1,0:T(8,128)(2,1)}, f...) custom-call(s32[2048]{0:T(1024)} %bitcast.117, s32[7]{0:T(128)} %concatenate.52.where, bf16[512,768]{1,0:T(8,128)(2,1)} %refs_0_.3, ...), custom_call_target="tpu_custom_call" | custom-call | flops 1000 | bytes 1000 | tf_op jit(solution)/shard_map/attend_forward/pallas_call | solution.py:286
  153.8 28.4 %middle.1 = (bf16[512,768]{1,0:T(8,128)(2,1)}, f32[512,768]{1,0:T(8,128)}, bf16[512,768]{1,0:T(8,128)(2,1)}, bf16[3,512,768]{2,1,0:T(8,128)(2,1)}, bf16[512,6912]{1,0:T(8,128)(2,1)}, /*index=5*/f32[10,768]{1,0:T(8,128)}) custom-call(s32[6]{0:T(128)} %concatenate.53.known, bf16[96,9216]{1,0:T(8,128)(2,1)} %copy-done, bf16[96,9216]{1,0:T(8,128)(2,1)} %copy-done.1, ...), custom_call_target="tpu_custom_call" | custom-call | flops 1000 | bytes 1000 | tf_op jit(solution)/shard_map/middle/pallas_call | solution.py:692
  182.2 15.3 %ffn_grads.1 = (bf16[384,3072]{1,0:T(8,128)(2,1)}, bf16[384,3840]{1,0:T(8,128)(2,1)}, bf16[384,3072]{1,0:T(8,128)(2,1)}, bf16[384,3840]{1,0:T(8,128)(2,1)}) custom-call(s32[1]{0:T(128)} %bitcast.5.place, bf16[3,512,768]{2,1,0:T(8,128)(2,1)} %get-tuple-element.118.left_ref, bf16[512,6912]{1,0:T(8,128)(2,1)} %get-tuple-element.119.right_ref), custom_call_target="tpu_custom_call" | custom-call | flops 1000 | bytes 1000 | tf_op jit(solution)/shard_map/ffn_grads/pallas_call | solution.py:744
  198.0 20.1 %attend_backward.2 = (bf16[1536,768]{1,0:T(8,128)(2,1)}, bf16[1536,768]{1,0:T(8,128)(2,1)}, f32[768,512]{1,0:T(8,128)}, bf16[512,768]{1,0:T(8,128)(2,1)}, bf16[5...) custom-call(s32[2048]{0:T(1024)} %bitcast.118, s32[7]{0:T(128)} %concatenate.52.where, ...), custom_call_target="tpu_custom_call" | custom-call | flops 1000 | bytes 1000 | tf_op jit(solution)/shard_map/attend_backward/pallas_call | solution.py:477
  218.2 3.0 add_convert_fusion.1
  221.2 5.3 %collective-permute-start.25 = (bf16[2,96,3840]{2,1,0:T(8,128)(2,1)}, bf16[2,96,3840]{2,1,0:T(8,128)(2,1)S(1)}, u32[]{:S(2)}, u32[]{:S(2)}) collective-permute-start(bf16[2,96,3840]{2,1,0:T(8,128)(2,1)} %bitcast.33), channel_id=1, source_target_pairs={{0,16},{4,20},{8,24},{12,28},{16,0},{20,4},{24,8},{28,12},{1,17},{... | collective-permute-start | bytes 4423688 | tf_op jit(solution)/shard_map/ppermute | solution.py:928
  226.4 1.7 fusion.6
  228.8 24.2 %collective-permute-start.21 = (bf16[512,768]{1,0:T(8,128)(2,1)}, bf16[512,768]{1,0:T(8,128)(2,1)}, u32[]{:S(2)}, u32[]{:S(2)}) collective-permute-start(bf16[512,768]{1,0:T(8,128)(2,1)} %get-tuple-element.128), channel_id=1, source_target_pairs={{0,1},{3,2},{4,5},{7,6},{8,9},{11,10},{12,13},{15,14},{16,17},{19,... | collective-permute-start | bytes 2359304 | tf_op jit(solution)/shard_map/ppermute | solution.py:915
  253.0 20.3 %attend_backward.3 = (bf16[512,768]{1,0:T(8,128)(2,1)}, bf16[512,768]{1,0:T(8,128)(2,1)}, bf16[512,768]{1,0:T(8,128)(2,1)}, f32[512,768]{1,0:T(8,128)}) custom-call(s32[2048]{0:T(1024)} %bitcast.119, s32[7]{0:T(128)} %concatenate.52.where, bf16[512,768]{1,0:T(8,128)(2,1)} %get-tuple-element.116.refs_0_, bf16[512,768]{1,0:T(8,128)(2,1)} %get-tuple-element.122.refs_1_, ...), custom_call_target="tpu_custom_call" | custom-call | flops 1000 | bytes 1000 | tf_op jit(solution)/shard_map/attend_backward/pallas_call | solution.py:477
  273.3 2.4 add_convert_fusion.3
  275.7 2.2 collective-permute-start.22
  277.9 1.5 collective-permute-start.23
  279.5 2.5 fusion
  283.1 2.2 fusion.1
  286.2 2.0 collective-permute-start.29
  288.8 12.9 %attn_grads.1 = (bf16[4,304,768]{2,1,0:T(8,128)(2,1)}, f32[4,304,768]{2,1,0:T(8,128)}) custom-call(s32[1]{0:T(128)} %slice.227.core_ref, bf16[512,768]{1,0:T(8,128)(2,1)} %refs_0_.3, bf16[512,768]{1,0:T(8,128)(2,1)} %broadcast_select_fusion.refs_3_.refs_1_, bf16[512,768]{1,0:T(8,128)(2,1)} %broadcast_select_fusion.1.refs_2_, ...), custom_call_target="tpu_custom_call" | custom-call | flops 1000 | bytes 1000 | tf_op jit(solution)/shard_map/attn_grads/pallas_call | solution.py:555
  301.7 3.1 collective-permute-start.28
  304.8 3.3 fusion.2
  308.1 2.2 collective-permute-start.26
  314.5 1.8 copy-done.4
  316.3 1.7 add_convert_fusion
  318.0 4.2 %all-to-all-start = ((bf16[4,304,768]{2,1,0:T(8,128)(2,1)}), bf16[4,304,768]{2,1,0:T(8,128)(2,1)S(1)}, u32[]{:S(2)}, u32[]{:S(2)}) async-start(bf16[4,304,768]{2,1,0:T(8,128)(2,1)} %add_convert_fusion), calls=%async_computation | async-start | bytes 3735552 | tf_op jit(solution)/shard_map/all_to_all | solution.py:991
  322.4 2.7 collective-permute-start.31
  327.6 12.7 %collective-permute-done.27 = bf16[512,768]{1,0:T(8,128)(2,1)} collective-permute-done((bf16[512,768]{1,0:T(8,128)(2,1)}, bf16[512,768]{1,0:T(8,128)(2,1)}, u32[]{:S(2)}, u32[]{:S(2)}) %collective-permute-start.27) | collective-permute-done | bytes 786464 | tf_op jit(solution)/shard_map/ppermute | solution.py:969
  340.3 2.8 convert_add_fusion.1
  343.0 4.1 %collective-permute-done.32 = bf16[96,1728]{1,0:T(8,128)(2,1)S(1)} collective-permute-done((bf16[96,1728]{1,0:T(8,128)(2,1)S(1)}, bf16[96,1728]{1,0:T(8,128)(2,1)S(1)}, u32[]{:S(2)}, u32[]{:S(2)}) %collective-permute-start.32) | collective-permute-done | bytes 331808 | tf_op jit(solution)/shard_map/ppermute | solution.py:72
  347.2 13.0 %collective-permute-done.33 = bf16[96,1728]{1,0:T(8,128)(2,1)S(1)} collective-permute-done((bf16[96,1728]{1,0:T(8,128)(2,1)S(1)}, bf16[96,1728]{1,0:T(8,128)(2,1)S(1)}, u32[]{:S(2)}, u32[]{:S(2)}) %collective-permute-start.33) | collective-permute-done | bytes 331808 | tf_op jit(solution)/shard_map/ppermute | solution.py:72
  364.3 3.8 collective-permute-start.35
  369.0 4.4 %collective-permute-done.34.refs_1_ = bf16[336,192]{1,0:T(8,128)(2,1)S(1)} collective-permute-done((bf16[336,192]{1,0:T(8,128)(2,1)S(1)}, bf16[336,192]{1,0:T(8,128)(2,1)S(1)}, u32[]{:S(2)}, u32[]{:S(2)}) %collective-permute-start.34) | collective-permute-done | bytes 129056 | tf_op jit(solution)/shard_map/ppermute | solution.py:72
  374.0 6.3 %collective-permute-done.36.refs_3_ = bf16[336,192]{1,0:T(8,128)(2,1)S(1)} collective-permute-done((bf16[336,192]{1,0:T(8,128)(2,1)S(1)}, bf16[336,192]{1,0:T(8,128)(2,1)S(1)}, u32[]{:S(2)}, u32[]{:S(2)}) %collective-permute-start.36) | collective-permute-done | bytes 129056 | tf_op jit(solution)/shard_map/ppermute | solution.py:72
  381.0 1.9 finish.1
  (169 shorter events, 43.8 us)
Async XLA Ops:
  0.7 26.2 %copy-start.25 = (f32[768]{0:T(1024)S(1)}, f32[768]{0:T(1024)}, u32[]{:S(2)}) copy-start(f32[768]{0:T(1024)} %param.34) | copy-start | bytes 9220
  0.7 26.2 %copy-start.26 = (f32[768]{0:T(1024)S(1)}, f32[768]{0:T(1024)}, u32[]{:S(2)}) copy-start(f32[768]{0:T(1024)} %param.26) | copy-start | bytes 9220
  0.7 26.3 %copy-start.27 = (f32[768]{0:T(1024)S(1)}, f32[768]{0:T(1024)}, u32[]{:S(2)}) copy-start(f32[768]{0:T(1024)} %param.27) | copy-start | bytes 9220
  0.7 26.3 %copy-start.28 = (f32[768]{0:T(1024)S(1)}, f32[768]{0:T(1024)}, u32[]{:S(2)}) copy-start(f32[768]{0:T(1024)} %param.28) | copy-start | bytes 9220
  3.6 15.1 %collective-permute-start = (bf16[3,96,768]{2,1,0:T(8,128)(2,1)S(1)}, bf16[3,96,768]{2,1,0:T(8,128)(2,1)S(1)}, u32[]{:S(2)}, u32[]{:S(2)}) collective-permute-start(bf16[3,96,768]{2,1,0:T(8,128)(2,1)S(1)} %pad_maximum_fusion.2), channel_id=1, source_target_pairs={{1,0},{2,1},{3,2},{5,4},{6,5},{7,6},{9,8},{10,9},{11,10},{13,12},{... | collective-permute-start | bytes 1327112 | tf_op jit(solution)/shard_map/ppermute | solution.py:38
  4.9 15.1 %collective-permute-start.1 = (bf16[3,96,768]{2,1,0:T(8,128)(2,1)S(1)}, bf16[3,96,768]{2,1,0:T(8,128)(2,1)S(1)}, u32[]{:S(2)}, u32[]{:S(2)}) collective-permute-start(bf16[3,96,768]{2,1,0:T(8,128)(2,1)S(1)} %pad_maximum_fusion.2), channel_id=1, source_target_pairs={{0,1},{1,2},{2,3},{4,5},{5,6},{6,7},{8,9},{9,10},{10,11},{12,13},{... | collective-permute-start | bytes 1327112 | tf_op jit(solution)/shard_map/ppermute | solution.py:37
  18.7 13.2 %collective-permute-start.2 = (bf16[3,96,768]{2,1,0:T(8,128)(2,1)S(1)}, bf16[3,96,768]{2,1,0:T(8,128)(2,1)S(1)}, u32[]{:S(2)}, u32[]{:S(2)}) collective-permute-start(bf16[3,96,768]{2,1,0:T(8,128)(2,1)S(1)} %collective-permute-done), channel_id=1, source_target_pairs={{2,1},{1,0},{6,5},{5,4},{10,9},{9,8},{14,13},{13,12},{18,17},{17,1... | collective-permute-start | bytes 1327112 | tf_op jit(solution)/shard_map/ppermute | solution.py:44
  20.0 11.9 %collective-permute-start.3 = (bf16[3,96,768]{2,1,0:T(8,128)(2,1)S(1)}, bf16[3,96,768]{2,1,0:T(8,128)(2,1)S(1)}, u32[]{:S(2)}, u32[]{:S(2)}) collective-permute-start(bf16[3,96,768]{2,1,0:T(8,128)(2,1)S(1)} %collective-permute-done.1), channel_id=1, source_target_pairs={{1,2},{2,3},{5,6},{6,7},{9,10},{10,11},{13,14},{14,15},{17,18},{18... | collective-permute-start | bytes 1327112 | tf_op jit(solution)/shard_map/ppermute | solution.py:43
  21.4 23.0 %copy-start.9 = (s32[1,2048]{1,0:T(1,128)}, s32[1,2048]{1,0:T(1,128)S(1)}, u32[]{:S(2)}) copy-start(s32[1,2048]{1,0:T(1,128)S(1)} %compare_select_fusion.refs_4_.refs_5_.refs_6_.refs_7_.refs_26_.refs_9_.refs_10_.refs_11_) | copy-start | bytes 24580
  32.0 12.3 %collective-permute-start.4 = (bf16[3,96,768]{2,1,0:T(8,128)(2,1)S(1)}, bf16[3,96,768]{2,1,0:T(8,128)(2,1)S(1)}, u32[]{:S(2)}, u32[]{:S(2)}) collective-permute-start(bf16[3,96,768]{2,1,0:T(8,128)(2,1)S(1)} %broadcast_select_fusion.4), channel_id=1, source_target_pairs={{1,0},{2,3},{5,4},{6,7},{9,8},{10,11},{13,12},{14,15},{17,16},{18,... | collective-permute-start | bytes 1327112 | tf_op jit(solution)/shard_map/ppermute | solution.py:50
  47.4 47.2 %copy-start = (bf16[96,9216]{1,0:T(8,128)(2,1)}, bf16[96,9216]{1,0:T(8,128)(2,1)S(1)}, u32[]{:S(2)}) copy-start(bf16[96,9216]{1,0:T(8,128)(2,1)S(1)} %concatenate.57.refs_8_.refs_16_.refs_0_) | copy-start | bytes 5308420
  47.5 23.4 %collective-permute-start.9 = (bf16[96,9216]{1,0:T(8,128)(2,1)S(1)}, bf16[96,9216]{1,0:T(8,128)(2,1)S(1)}, u32[]{:S(2)}, u32[]{:S(2)}) collective-permute-start(bf16[96,9216]{1,0:T(8,128)(2,1)S(1)} %concatenate.57.refs_8_.refs_16_.refs_0_), channel_id=1, source_target_pairs={{0,4},{4,0},{8,12},{12,8},{16,20},{20,16},{24,28},{28,24},{1,5},{5... | collective-permute-start | bytes 5308424 | tf_op jit(solution)/shard_map/ppermute | solution.py:860
  47.5 22.0 %collective-permute-start.7 = (bf16[512,768]{1,0:T(8,128)(2,1)}, bf16[512,768]{1,0:T(8,128)(2,1)S(1)}, u32[]{:S(2)}, u32[]{:S(2)}) collective-permute-start(bf16[512,768]{1,0:T(8,128)(2,1)} %refs_0_.3), channel_id=1, source_target_pairs={{1,0},{2,1},{3,2},{5,4},{6,5},{7,6},{9,8},{10,9},{11,10},{13,12},{... | collective-permute-start | bytes 2359304 | tf_op jit(solution)/shard_map/ppermute | solution.py:38
  48.8 22.0 %collective-permute-start.8 = (bf16[512,768]{1,0:T(8,128)(2,1)}, bf16[512,768]{1,0:T(8,128)(2,1)S(1)}, u32[]{:S(2)}, u32[]{:S(2)}) collective-permute-start(bf16[512,768]{1,0:T(8,128)(2,1)} %refs_0_.3), channel_id=1, source_target_pairs={{0,1},{1,2},{2,3},{4,5},{5,6},{6,7},{8,9},{9,10},{10,11},{12,13},{... | collective-permute-start | bytes 2359304 | tf_op jit(solution)/shard_map/ppermute | solution.py:37
  53.4 41.2 %collective-permute-start.5 = (bf16[96,9216]{1,0:T(8,128)(2,1)S(1)}, bf16[96,9216]{1,0:T(8,128)(2,1)S(1)}, u32[]{:S(2)}, u32[]{:S(2)}) collective-permute-start(bf16[96,9216]{1,0:T(8,128)(2,1)S(1)} %concatenate.57.refs_8_.refs_16_.refs_0_), channel_id=1, source_target_pairs={{0,8},{4,12},{8,0},{12,4},{16,24},{20,28},{24,16},{28,20},{1,9},{5... | collective-permute-start | bytes 5308424 | tf_op jit(solution)/shard_map/ppermute | solution.py:860
  54.7 40.3 %collective-permute-start.6 = (bf16[96,9216]{1,0:T(8,128)(2,1)S(1)}, bf16[96,9216]{1,0:T(8,128)(2,1)}, u32[]{:S(2)}, u32[]{:S(2)}) collective-permute-start(bf16[96,9216]{1,0:T(8,128)(2,1)S(1)} %concatenate.57.refs_8_.refs_16_.refs_0_), channel_id=1, source_target_pairs={{0,16},{4,20},{8,24},{12,28},{16,0},{20,4},{24,8},{28,12},{1,17},{... | collective-permute-start | bytes 5308424 | tf_op jit(solution)/shard_map/ppermute | solution.py:860
  70.9 28.5 %copy-start.5 = (bf16[512,768]{1,0:T(8,128)(2,1)}, bf16[512,768]{1,0:T(8,128)(2,1)S(1)}, u32[]{:S(2)}) copy-start(bf16[512,768]{1,0:T(8,128)(2,1)S(1)} %collective-permute-done.8) | copy-start | bytes 2359300
  72.2 21.5 %collective-permute-start.10 = (bf16[512,768]{1,0:T(8,128)(2,1)S(1)}, bf16[512,768]{1,0:T(8,128)(2,1)S(1)}, u32[]{:S(2)}, u32[]{:S(2)}) collective-permute-start(bf16[512,768]{1,0:T(8,128)(2,1)S(1)} %collective-permute-done.7), channel_id=1, source_target_pairs={{2,1},{1,0},{6,5},{5,4},{10,9},{9,8},{14,13},{13,12},{18,17},{17,1... | collective-permute-start | bytes 2359304 | tf_op jit(solution)/shard_map/ppermute | solution.py:44
  73.5 20.2 %collective-permute-start.11 = (bf16[512,768]{1,0:T(8,128)(2,1)S(1)}, bf16[512,768]{1,0:T(8,128)(2,1)S(1)}, u32[]{:S(2)}, u32[]{:S(2)}) collective-permute-start(bf16[512,768]{1,0:T(8,128)(2,1)S(1)} %collective-permute-done.8), channel_id=1, source_target_pairs={{1,2},{2,3},{5,6},{6,7},{9,10},{10,11},{13,14},{14,15},{17,18},{18... | collective-permute-start | bytes 2359304 | tf_op jit(solution)/shard_map/ppermute | solution.py:43
  94.9 27.3 %collective-permute-start.13 = (bf16[96,9216]{1,0:T(8,128)(2,1)S(1)}, bf16[96,9216]{1,0:T(8,128)(2,1)S(1)}, u32[]{:S(2)}, u32[]{:S(2)}) collective-permute-start(bf16[96,9216]{1,0:T(8,128)(2,1)S(1)} %collective-permute-done.5.refs_9_.refs_17_.refs_1_), channel_id=1, source_target_pairs={{0,4},{4,0},{8,12},{12,8},{16,20},{20,16},{24,28},{28,24},{1,5},{5... | collective-permute-start | bytes 5308424 | tf_op jit(solution)/shard_map/ppermute | solution.py:860
  94.9 27.3 %collective-permute-start.14 = (bf16[96,9216]{1,0:T(8,128)(2,1)}, bf16[96,9216]{1,0:T(8,128)(2,1)}, u32[]{:S(2)}, u32[]{:S(2)}) collective-permute-start(bf16[96,9216]{1,0:T(8,128)(2,1)} %collective-permute-done.6.refs_10_.refs_18_.refs_2_), channel_id=1, source_target_pairs={{0,4},{4,0},{8,12},{12,8},{16,20},{20,16},{24,28},{28,24},{1,5},{5... | collective-permute-start | bytes 5308424 | tf_op jit(solution)/shard_map/ppermute | solution.py:860
  95.5 21.7 %collective-permute-start.12 = (bf16[96,4608]{1,0:T(8,128)(2,1)S(1)}, bf16[96,4608]{1,0:T(8,128)(2,1)}, u32[]{:S(2)}, u32[]{:S(2)}) collective-permute-start(bf16[96,4608]{1,0:T(8,128)(2,1)S(1)} %slice.221), channel_id=1, source_target_pairs={{0,16},{4,20},{8,24},{12,28},{16,0},{20,4},{24,8},{28,12},{1,17},{... | collective-permute-start | bytes 2654216 | tf_op jit(solution)/shard_map/ppermute | solution.py:860
  98.3 21.4 %collective-permute-start.16 = (bf16[96,4608]{1,0:T(8,128)(2,1)S(1)}, bf16[96,4608]{1,0:T(8,128)(2,1)}, u32[]{:S(2)}, u32[]{:S(2)}) collective-permute-start(bf16[96,4608]{1,0:T(8,128)(2,1)S(1)} %slice.222), channel_id=1, source_target_pairs={{0,8},{4,12},{8,0},{12,4},{16,24},{20,28},{24,16},{28,20},{1,9},{5... | collective-permute-start | bytes 2654216 | tf_op jit(solution)/shard_map/ppermute | solution.py:860
  99.3 22.9 %collective-permute-start.18 = (bf16[512,768]{1,0:T(8,128)(2,1)}, bf16[512,768]{1,0:T(8,128)(2,1)}, u32[]{:S(2)}, u32[]{:S(2)}) collective-permute-start(bf16[512,768]{1,0:T(8,128)(2,1)} %broadcast_select_fusion.1.refs_2_), channel_id=1, source_target_pairs={{1,0},{2,3},{5,4},{6,7},{9,8},{10,11},{13,12},{14,15},{17,16},{18,... | collective-permute-start | bytes 2359304 | tf_op jit(solution)/shard_map/ppermute | solution.py:50
  117.2 7.8 %collective-permute-start.15 = (bf16[96,4608]{1,0:T(8,128)(2,1)}, bf16[96,4608]{1,0:T(8,128)(2,1)}, u32[]{:S(2)}, u32[]{:S(2)}) collective-permute-start(bf16[96,4608]{1,0:T(8,128)(2,1)} %collective-permute-done.12.refs_11_.refs_3_), channel_id=1, source_target_pairs={{0,4},{4,0},{8,12},{12,8},{16,20},{20,16},{24,28},{28,24},{1,5},{5... | collective-permute-start | bytes 2654216 | tf_op jit(solution)/shard_map/ppermute | solution.py:860
  119.8 5.3 %collective-permute-start.17 = (bf16[96,4608]{1,0:T(8,128)(2,1)}, bf16[96,4608]{1,0:T(8,128)(2,1)}, u32[]{:S(2)}, u32[]{:S(2)}) collective-permute-start(bf16[96,4608]{1,0:T(8,128)(2,1)} %collective-permute-done.16.refs_19_.refs_11_), channel_id=1, source_target_pairs={{0,4},{4,0},{8,12},{12,8},{16,20},{20,16},{24,28},{28,24},{1,5},{5... | collective-permute-start | bytes 2654216 | tf_op jit(solution)/shard_map/ppermute | solution.py:860
  197.5 20.7 %collective-permute-start.20 = (bf16[384,3840]{1,0:T(8,128)(2,1)}, bf16[384,3840]{1,0:T(8,128)(2,1)}, u32[]{:S(2)}, u32[]{:S(2)}) collective-permute-start(bf16[384,3840]{1,0:T(8,128)(2,1)} %get-tuple-element.121), channel_id=1, source_target_pairs={{0,4},{4,0},{8,12},{12,8},{16,20},{20,16},{24,28},{28,24},{1,5},{5... | collective-permute-start | bytes 8847368 | tf_op jit(solution)/shard_map/ppermute | solution.py:910
  197.5 20.6 %collective-permute-start.19 = (bf16[384,3072]{1,0:T(8,128)(2,1)}, bf16[384,3072]{1,0:T(8,128)(2,1)}, u32[]{:S(2)}, u32[]{:S(2)}) collective-permute-start(bf16[384,3072]{1,0:T(8,128)(2,1)} %get-tuple-element.120), channel_id=1, source_target_pairs={{0,4},{4,0},{8,12},{12,8},{16,20},{20,16},{24,28},{28,24},{1,5},{5... | collective-permute-start | bytes 7077896 | tf_op jit(solution)/shard_map/ppermute | solution.py:910
  198.0 20.2 %copy-start.6 = (bf16[384,3840]{1,0:T(8,128)(2,1)S(1)}, bf16[384,3840]{1,0:T(8,128)(2,1)}, u32[]{:S(2)}) copy-start(bf16[384,3840]{1,0:T(8,128)(2,1)} %get-tuple-element.131) | copy-start | bytes 8847364
  221.2 58.3 %collective-permute-start.25 = (bf16[2,96,3840]{2,1,0:T(8,128)(2,1)}, bf16[2,96,3840]{2,1,0:T(8,128)(2,1)S(1)}, u32[]{:S(2)}, u32[]{:S(2)}) collective-permute-start(bf16[2,96,3840]{2,1,0:T(8,128)(2,1)} %bitcast.33), channel_id=1, source_target_pairs={{0,16},{4,20},{8,24},{12,28},{16,0},{20,4},{24,8},{28,12},{1,17},{... | collective-permute-start | bytes 4423688 | tf_op jit(solution)/shard_map/ppermute | solution.py:928
  228.1 51.4 %collective-permute-start.24 = (bf16[2,96,3072]{2,1,0:T(8,128)(2,1)S(1)}, bf16[2,96,3072]{2,1,0:T(8,128)(2,1)}, u32[]{:S(2)}, u32[]{:S(2)}) collective-permute-start(bf16[2,96,3072]{2,1,0:T(8,128)(2,1)S(1)} %fusion.6), channel_id=1, source_target_pairs={{0,8},{4,12},{8,0},{12,4},{16,24},{20,28},{24,16},{28,20},{1,9},{5... | collective-permute-start | bytes 3538952 | tf_op jit(solution)/shard_map/ppermute | solution.py:928
  228.8 44.5 %collective-permute-start.21 = (bf16[512,768]{1,0:T(8,128)(2,1)}, bf16[512,768]{1,0:T(8,128)(2,1)}, u32[]{:S(2)}, u32[]{:S(2)}) collective-permute-start(bf16[512,768]{1,0:T(8,128)(2,1)} %get-tuple-element.128), channel_id=1, source_target_pairs={{0,1},{3,2},{4,5},{7,6},{8,9},{11,10},{12,13},{15,14},{16,17},{19,... | collective-permute-start | bytes 2359304 | tf_op jit(solution)/shard_map/ppermute | solution.py:915
  275.7 29.1 %collective-permute-start.22 = (bf16[512,768]{1,0:T(8,128)(2,1)}, bf16[512,768]{1,0:T(8,128)(2,1)}, u32[]{:S(2)}, u32[]{:S(2)}) collective-permute-start(bf16[512,768]{1,0:T(8,128)(2,1)} %add_convert_fusion.3), channel_id=1, source_target_pairs={{0,1},{3,2},{4,5},{7,6},{8,9},{11,10},{12,13},{15,14},{16,17},{19,... | collective-permute-start | bytes 2359304 | tf_op jit(solution)/shard_map/ppermute | solution.py:933
  277.9 26.9 %collective-permute-start.23 = (bf16[512,768]{1,0:T(8,128)(2,1)}, bf16[512,768]{1,0:T(8,128)(2,1)}, u32[]{:S(2)}, u32[]{:S(2)}) collective-permute-start(bf16[512,768]{1,0:T(8,128)(2,1)} %add_convert_fusion.3), channel_id=1, source_target_pairs={{1,2},{2,1},{5,6},{6,5},{9,10},{10,9},{13,14},{14,13},{17,18},{18,... | collective-permute-start | bytes 2359304 | tf_op jit(solution)/shard_map/ppermute | solution.py:934
  282.9 28.7 %collective-permute-start.30 = (bf16[96,3840]{1,0:T(8,128)(2,1)}, bf16[96,3840]{1,0:T(8,128)(2,1)}, u32[]{:S(2)}, u32[]{:S(2)}) collective-permute-start(bf16[96,3840]{1,0:T(8,128)(2,1)} %slice_bitcast_fusion.3), channel_id=1, source_target_pairs={{0,8},{4,12},{8,0},{12,4},{16,24},{20,28},{24,16},{28,20},{1,9},{5... | collective-permute-start | bytes 2211848 | tf_op jit(solution)/shard_map/ppermute | solution.py:114
  286.2 25.4 %collective-permute-start.29 = (bf16[96,3072]{1,0:T(8,128)(2,1)}, bf16[96,3072]{1,0:T(8,128)(2,1)}, u32[]{:S(2)}, u32[]{:S(2)}) collective-permute-start(bf16[96,3072]{1,0:T(8,128)(2,1)} %slice_bitcast_fusion.5), channel_id=1, source_target_pairs={{0,16},{4,20},{8,24},{12,28},{16,0},{20,4},{24,8},{28,12},{1,17},{... | collective-permute-start | bytes 1769480 | tf_op jit(solution)/shard_map/ppermute | solution.py:114
  301.7 12.8 %collective-permute-start.28 = (bf16[4,304,768]{2,1,0:T(8,128)(2,1)}, bf16[4,304,768]{2,1,0:T(8,128)(2,1)S(1)}, u32[]{:S(2)}, u32[]{:S(2)}) collective-permute-start(bf16[4,304,768]{2,1,0:T(8,128)(2,1)} %get-tuple-element.152), channel_id=1, source_target_pairs={{0,4},{4,0},{8,12},{12,8},{16,20},{20,16},{24,28},{28,24},{1,5},{5... | collective-permute-start | bytes 5603336 | tf_op jit(solution)/shard_map/ppermute | solution.py:963
  308.1 19.5 %collective-permute-start.26 = (bf16[512,768]{1,0:T(8,128)(2,1)}, bf16[512,768]{1,0:T(8,128)(2,1)}, u32[]{:S(2)}, u32[]{:S(2)}) collective-permute-start(bf16[512,768]{1,0:T(8,128)(2,1)} %get-tuple-element.188), channel_id=1, source_target_pairs={{0,1},{1,2},{2,3},{4,5},{5,6},{6,7},{8,9},{9,10},{10,11},{12,13},{... | collective-permute-start | bytes 2359304 | tf_op jit(solution)/shard_map/ppermute | solution.py:968
  310.3 30.0 %collective-permute-start.27 = (bf16[512,768]{1,0:T(8,128)(2,1)}, bf16[512,768]{1,0:T(8,128)(2,1)}, u32[]{:S(2)}, u32[]{:S(2)}) collective-permute-start(bf16[512,768]{1,0:T(8,128)(2,1)} %get-tuple-element.189), channel_id=1, source_target_pairs={{1,0},{2,1},{3,2},{5,4},{6,5},{7,6},{9,8},{10,9},{11,10},{13,12},{... | collective-permute-start | bytes 2359304 | tf_op jit(solution)/shard_map/ppermute | solution.py:969
  318.0 43.1 %all-to-all-start = ((bf16[4,304,768]{2,1,0:T(8,128)(2,1)}), bf16[4,304,768]{2,1,0:T(8,128)(2,1)S(1)}, u32[]{:S(2)}, u32[]{:S(2)}) async-start(bf16[4,304,768]{2,1,0:T(8,128)(2,1)} %add_convert_fusion), calls=%async_computation | async-start | bytes 3735552 | tf_op jit(solution)/shard_map/all_to_all | solution.py:991
  322.3 17.9 %copy-start.10 = (f32[512,768]{1,0:T(8,128)S(1)}, f32[512,768]{1,0:T(8,128)}, u32[]{:S(2)}) copy-start(f32[512,768]{1,0:T(8,128)} %get-tuple-element.135) | copy-start | bytes 4718596
  322.4 20.6 %collective-permute-start.31 = (bf16[96,1728]{1,0:T(8,128)(2,1)S(1)}, bf16[96,1728]{1,0:T(8,128)(2,1)S(1)}, u32[]{:S(2)}, u32[]{:S(2)}) collective-permute-start(bf16[96,1728]{1,0:T(8,128)(2,1)S(1)} %get-tuple-element.192), channel_id=1, source_target_pairs={{0,1},{1,2},{2,3},{3,0},{4,5},{5,6},{6,7},{7,4},{8,9},{9,10},{10,1... | collective-permute-start | bytes 995336 | tf_op jit(solution)/shard_map/ppermute | solution.py:72
  325.1 22.0 %collective-permute-start.32 = (bf16[96,1728]{1,0:T(8,128)(2,1)S(1)}, bf16[96,1728]{1,0:T(8,128)(2,1)S(1)}, u32[]{:S(2)}, u32[]{:S(2)}) collective-permute-start(bf16[96,1728]{1,0:T(8,128)(2,1)S(1)} %get-tuple-element.191), channel_id=1, source_target_pairs={{0,3},{1,0},{2,1},{3,2},{4,7},{5,4},{6,5},{7,6},{8,11},{9,8},{10,9... | collective-permute-start | bytes 995336 | tf_op jit(solution)/shard_map/ppermute | solution.py:72
  326.3 33.8 %copy-start.16 = (bf16[96,192]{1,0:T(8,128)(2,1)S(1)}, bf16[96,192]{1,0:T(8,128)(2,1)}, u32[]{:S(2)}) copy-start(bf16[96,192]{1,0:T(8,128)(2,1)} %copy-done.15) | copy-start | bytes 110596
  326.3 33.8 %collective-permute-start.33 = (bf16[96,1728]{1,0:T(8,128)(2,1)S(1)}, bf16[96,1728]{1,0:T(8,128)(2,1)S(1)}, u32[]{:S(2)}, u32[]{:S(2)}) collective-permute-start(bf16[96,1728]{1,0:T(8,128)(2,1)S(1)} %get-tuple-element.190), channel_id=1, source_target_pairs={{0,2},{1,3},{2,0},{3,1},{4,6},{5,7},{6,4},{7,5},{8,10},{9,11},{10,... | collective-permute-start | bytes 995336 | tf_op jit(solution)/shard_map/ppermute | solution.py:72
  364.2 9.2 %collective-permute-start.34 = (bf16[336,192]{1,0:T(8,128)(2,1)S(1)}, bf16[336,192]{1,0:T(8,128)(2,1)S(1)}, u32[]{:S(2)}, u32[]{:S(2)}) collective-permute-start(bf16[336,192]{1,0:T(8,128)(2,1)S(1)} %get-tuple-element.205), channel_id=1, source_target_pairs={{0,1},{1,2},{2,3},{3,0},{4,5},{5,6},{6,7},{7,4},{8,9},{9,10},{10,1... | collective-permute-start | bytes 387080 | tf_op jit(solution)/shard_map/ppermute | solution.py:72
  364.3 9.7 %collective-permute-start.35 = (bf16[336,192]{1,0:T(8,128)(2,1)S(1)}, bf16[336,192]{1,0:T(8,128)(2,1)S(1)}, u32[]{:S(2)}, u32[]{:S(2)}) collective-permute-start(bf16[336,192]{1,0:T(8,128)(2,1)S(1)} %get-tuple-element.204), channel_id=1, source_target_pairs={{0,3},{1,0},{2,1},{3,2},{4,7},{5,4},{6,5},{7,6},{8,11},{9,8},{10,9... | collective-permute-start | bytes 387080 | tf_op jit(solution)/shard_map/ppermute | solution.py:72
  368.1 12.2 %collective-permute-start.36 = (bf16[336,192]{1,0:T(8,128)(2,1)S(1)}, bf16[336,192]{1,0:T(8,128)(2,1)S(1)}, u32[]{:S(2)}, u32[]{:S(2)}) collective-permute-start(bf16[336,192]{1,0:T(8,128)(2,1)S(1)} %get-tuple-element.203), channel_id=1, source_target_pairs={{0,2},{1,3},{2,0},{3,1},{4,6},{5,7},{6,4},{7,5},{8,10},{9,11},{10,... | collective-permute-start | bytes 387080 | tf_op jit(solution)/shard_map/ppermute | solution.py:72
  (19 other events, 68.9 us)
